TPU v7x, 32 devices: a whole 2x2x4 slice. The times are simulated.
32 devices in a mesh: groups: 2 (over y), seq: 4 (over z), head: 2 (over x), sub: 2 (over core).
Axes of the slice: x: 2, y: 2, z: 4, core: 2. Of those that a mesh axis runs over, the one named last changes fastest.
Arguments:
- x_raw: bfloat16 [4096, 16384], P(('groups', 'seq'), ('head', 'sub')), parts along dimension 0, may hold values from -6 to 6
- bc_raw: bfloat16 [4096, 2, 1024], P(('groups', 'seq'), None, ('head', 'sub')), parts along dimension 0, may hold values from -6 to 6
- dt_raw: float32 [128, 4096], P(('head', 'sub'), ('groups', 'seq')), parts along dimension 1, may hold values from -3 to 3
- dt_bias: float32 [128], P(('head', 'sub')), may hold values from -3.8 to -3.2
- a_log: float32 [128], P(('head', 'sub')), may hold values from -12 to 1
- d_skip: float32 [128], P(('head', 'sub')), may hold values from 0 to 2.5
- conv_x: float32 [4, 16384], P(None, ('head', 'sub')), may hold values from -3 to 3
- conv_x_bias: float32 [16384], P(('head', 'sub')), may hold values from -0.8 to -0.3
- conv_bc: float32 [4, 2, 1024], P(None, None, ('head', 'sub')), may hold values from -1.5 to 1.5
- conv_bc_bias: float32 [2, 1024], P(None, ('head', 'sub')), may hold values from -0.35 to 0.05
- doc_starts: int32 [8], P('groups'), parts along dimension 0, may hold values from 0 to 1792, as said below
Outputs:
- scan_output: bfloat16 [4096, 16384], P(('groups', 'seq'), ('head', 'sub')), parts along dimension 0
There are 2 independent parts, one for each index of `groups`. A program takes and returns all parts, laid end to end along the dimension named above; an argument that names none is the same for every part. Nothing has to cross between parts.
Inputs may be any that keep to these rules, and one draw needn't show every extreme that they name: doc_starts[0] is 0 and the entries rise strictly; the last entry is 1792; document j runs from doc_starts[j] up to the next entry, the last one up to 2048.
All inputs are finite; a program needn't handle non-finite values.
Results may differ from a plain program's by a relative error of at most 0.0048.
Values may be sent and summed in bfloat16 or wider, within the bound.
No kernel may reach another device: no remote copies, remote signals or barrier semaphores. Data moves between devices by JAX's collectives and lax.ppermute only.
A program may use at most 128 MiB of HBM per device.

v0:
```python
import math

import jax
import jax.numpy as jnp
from jax import lax
from jax.sharding import PartitionSpec as P

P_SIZE = 128
N = 128
BLK = 512


def from_behind(array, axis, by):
    count = lax.axis_size(axis)
    pairs = [(i, i + by) for i in range(count) if 0 <= i + by < count]
    return lax.ppermute(array, axis, pairs)


def carried_in_2(part, axis, combine, identity):
    place = lax.axis_index(axis)
    gathered = jax.tree.map(lambda a: lax.all_gather(a, axis), part)
    state = jax.tree.map(lambda a, e: jnp.zeros_like(a) + jnp.asarray(e, a.dtype), part, identity)

    def one(turn, state):
        return combine(
            state, jax.tree.map(lambda a: lax.dynamic_index_in_dim(a, turn, 0, False), gathered)
        )

    return lax.fori_loop(0, place, one, state)


def segment_ids(positions, doc_starts):
    counted = jnp.sum((doc_starts[None, :] <= positions[:, None]).astype(jnp.int32), axis=1)
    return counted - 1


def convolve(extended, weight, bias_row, same_doc):
    row_count = same_doc.shape[1]
    mask_shape = (row_count,) + (1,) * (extended.ndim - 1)
    summed = jnp.where(
        same_doc[0].reshape(mask_shape), weight[0] * extended[0:row_count].astype(jnp.float32), 0.0
    )
    for tap_index in range(1, weight.shape[0]):
        tap_term = weight[tap_index] * extended[tap_index : tap_index + row_count].astype(
            jnp.float32
        )
        summed = summed + jnp.where(same_doc[tap_index].reshape(mask_shape), tap_term, 0.0)
    return jax.nn.silu(summed + bias_row)


def block_terms(mixed_x, mixed_bc, rate_block, step_block, doc_block, doc_before):
    row_count = mixed_x.shape[0]
    group_count = rate_block.shape[0]
    per_group = rate_block.shape[1]
    x_four = mixed_x.reshape(row_count, group_count, per_group, P_SIZE)
    b_groups = mixed_bc[:, 0, :].reshape(row_count, group_count, N)
    c_groups = mixed_bc[:, 1, :].reshape(row_count, group_count, N)
    cum_rates = jnp.cumsum(rate_block, axis=2)
    row_order = jnp.arange(row_count)
    causal_mask = (row_order[:, None] >= row_order[None, :]) & (
        doc_block[:, None] == doc_block[None, :]
    )
    scores = jnp.einsum("tgn,sgn->gts", c_groups, b_groups, preferred_element_type=jnp.float32)
    last_cum = cum_rates[:, :, row_count - 1 :]
    tail_factor = (
        jnp.exp(jnp.where(doc_block == doc_block[row_count - 1], last_cum - cum_rates, -jnp.inf))
        * step_block
    )
    b_moved = jnp.transpose(b_groups, (1, 0, 2)).astype(jnp.float32)
    slice_width = math.gcd(4, per_group)

    def one_slice(slice_start):
        cum_part = lax.dynamic_slice_in_dim(cum_rates, slice_start, slice_width, 1)
        step_part = lax.dynamic_slice_in_dim(step_block, slice_start, slice_width, 1)
        tail_part = lax.dynamic_slice_in_dim(tail_factor, slice_start, slice_width, 1)
        x_part = lax.dynamic_slice_in_dim(x_four, slice_start, slice_width, 2)
        log_gaps = jnp.where(
            causal_mask, cum_part[:, :, :, None] - cum_part[:, :, None, :], -jnp.inf
        )
        weights = (scores[:, None] * jnp.exp(log_gaps) * step_part[:, :, None, :]).astype(
            jnp.bfloat16
        )
        inner_part = jnp.einsum(
            "gits,sgip->tgip", weights, x_part, preferred_element_type=jnp.float32
        )
        tail_weights = (b_moved[:, None] * tail_part[..., None]).astype(jnp.bfloat16)
        state_part = jnp.einsum(
            "gisn,sgip->gipn", tail_weights, x_part, preferred_element_type=jnp.float32
        )
        return (inner_part, state_part)

    starts = jnp.arange(per_group // slice_width, dtype=jnp.int32) * slice_width
    inner_parts, state_parts = lax.map(one_slice, starts)
    inner_terms = jnp.transpose(inner_parts, (1, 2, 0, 3, 4)).reshape(
        row_count, group_count, per_group, P_SIZE
    )
    block_state = jnp.transpose(state_parts, (1, 0, 2, 3, 4)).reshape(
        group_count, per_group, P_SIZE, N
    )
    block_decay = jnp.where(doc_block[row_count - 1] == doc_before, jnp.exp(last_cum[:, :, 0]), 0.0)
    entry_factor = jnp.where(doc_block == doc_before, jnp.exp(cum_rates), 0.0)
    return (inner_terms, block_state, block_decay, entry_factor)


def block_output(inner_terms, entry_factor, mixed_bc, carried, mixed_x, skip_four):
    row_count = mixed_x.shape[0]
    group_count = carried.shape[0]
    c_float = mixed_bc[:, 1, :].reshape(row_count, group_count, N).astype(jnp.float32)
    from_before = jnp.einsum("tgn,gipn->tgip", c_float, carried, precision=lax.Precision.HIGHEST)
    x_four = mixed_x.reshape(row_count, group_count, -1, P_SIZE)
    summed = (
        inner_terms
        + from_before * jnp.transpose(entry_factor, (2, 0, 1))[..., None]
        + skip_four[None, :, :, None] * x_four.astype(jnp.float32)
    )
    return summed.astype(jnp.bfloat16).reshape(row_count, -1)


def per_device(
    x_raw,
    bc_raw,
    dt_raw,
    dt_bias,
    a_log,
    d_skip,
    conv_x,
    conv_x_bias,
    conv_bc,
    conv_bc_bias,
    doc_starts,
):
    local_rows = x_raw.shape[0]
    x_width = x_raw.shape[1]
    tap_count = conv_x.shape[0]
    group_count = bc_raw.shape[2] // N
    head_count = dt_raw.shape[0]
    per_group = head_count // group_count
    block_count = local_rows // BLK
    keep_from = local_rows - tap_count + 1
    tail_rows = jnp.concatenate(
        [x_raw[keep_from:], bc_raw[keep_from:].reshape(tap_count - 1, -1)], axis=1
    )
    rim_rows = from_behind(tail_rows, "seq", 1)
    rim_x = rim_rows[:, :x_width]
    rim_bc = rim_rows[:, x_width:].reshape(tap_count - 1, 2, -1)
    first_row = lax.axis_index("seq") * local_rows
    positions = first_row + jnp.arange(1 - tap_count, local_rows, dtype=jnp.int32)
    doc_ext = segment_ids(positions, doc_starts)
    doc_rows = doc_ext[tap_count - 1 :]
    same_doc = jnp.stack(
        [doc_ext[tap_index : tap_index + local_rows] == doc_rows for tap_index in range(tap_count)]
    )
    mixed_x = convolve(
        jnp.concatenate([rim_x, x_raw], axis=0), conv_x, conv_x_bias, same_doc
    ).astype(jnp.bfloat16)
    mixed_bc = convolve(
        jnp.concatenate([rim_bc, bc_raw], axis=0), conv_bc, conv_bc_bias, same_doc
    ).astype(jnp.bfloat16)
    step_sizes = jax.nn.softplus(dt_raw + dt_bias[:, None])
    log_rates = -jnp.exp(a_log)[:, None] * step_sizes
    skip_four = d_skip.reshape(group_count, per_group)

    def by_block(values):
        return jnp.transpose(values.reshape(group_count, per_group, block_count, BLK), (2, 0, 1, 3))

    doc_blocks = doc_rows.reshape(block_count, BLK)
    doc_before = doc_ext[tap_count - 2 : tap_count - 2 + local_rows].reshape(block_count, BLK)[:, 0]
    x_blocks = mixed_x.reshape(block_count, BLK, -1)
    bc_blocks = mixed_bc.reshape(block_count, BLK, 2, -1)
    inner_terms, block_states, block_decays, entry_factors = lax.map(
        lambda packed: block_terms(*packed),
        (x_blocks, bc_blocks, by_block(log_rates), by_block(step_sizes), doc_blocks, doc_before),
    )

    def compose(pair, block_pair):
        return (
            (pair[0] * block_pair[0], pair[1] * block_pair[0][:, :, None, None] + block_pair[1]),
            None,
        )

    unit_decay = jnp.ones((group_count, per_group), jnp.float32)
    zero_state = jnp.zeros((group_count, per_group, P_SIZE, N), jnp.float32)
    (device_decay, device_state), unused = lax.scan(
        compose, (unit_decay, zero_state), (block_decays, block_states)
    )

    def join_states(earlier, later):
        return (earlier[0] * later[0], earlier[1] * later[0][:, :, None, None] + later[1])

    carried_in = carried_in_2(
        (device_decay, device_state), "seq", join_states, (unit_decay, zero_state)
    )[1]

    def emit_block(carried, packed):
        inner_part, decay_part, state_part, entry_part, bc_part, x_part = packed
        output_rows = block_output(inner_part, entry_part, bc_part, carried, x_part, skip_four)
        return (decay_part[:, :, None, None] * carried + state_part, output_rows)

    final_state, outputs = lax.scan(
        emit_block,
        carried_in,
        (inner_terms, block_decays, block_states, entry_factors, bc_blocks, x_blocks),
    )
    return outputs.reshape(local_rows, -1)


def solution(mesh):
    return jax.shard_map(
        per_device,
        mesh=mesh,
        in_specs=(
            P(("groups", "seq"), ("head", "sub")),
            P(("groups", "seq"), None, ("head", "sub")),
            P(("head", "sub"), ("groups", "seq")),
            P(("head", "sub")),
            P(("head", "sub")),
            P(("head", "sub")),
            P(None, ("head", "sub")),
            P(("head", "sub")),
            P(None, None, ("head", "sub")),
            P(None, ("head", "sub")),
            P("groups"),
        ),
        out_specs=P(("groups", "seq"), ("head", "sub")),
        check_vma=False,
    )
```

profile of v0, /device:TPU:0, one launch (start us, length us, event | category | flops | bytes accessed | tf_op | source)
XLA Modules:
  0.0 276.1 jit_solution(14254757183825410028)
XLA Ops:
  8.1 4.9 %collective-permute-start = (bf16[3,4608]{1,0:T(4,128)(2,1)S(1)}, bf16[3,4608]{1,0:T(4,128)(2,1)S(1)}, u32[]{:S(2)}, u32[]{:S(2)}) collective-permute-start(bf16[3,4608]{1,0:T(4,128)(2,1)S(1)} %pad_maximum_fusion.2), channel_id=1, source_target_pairs={{0,4},{4,8},{8,12},{1,5},{5,9},{9,13},{2,6},{6,10},{10,14},{3,7},{... | collective-permute-start | bytes 82952 | tf_op jit(solution)/shard_map/ppermute | solution.py:16
  15.1 1.4 broadcast_compare_fusion
  18.6 1.7 fusion.26
  20.9 1.0 broadcast_multiply_fusion
  21.9 2.3 reduce-window.6
  27.1 1.3 copy.63
  28.6 2.1 multiply_convert_fusion.7
  32.3 15.2 %multiply_convert_fusion.6 = bf16[512,4096]{1,0:T(8,128)(2,1)} fusion(bf16[512,4096]{1,0:T(8,128)(2,1)} %param.15, bf16[3,4096]{1,0:T(4,128)(2,1)S(1)} %slice.126, f32[4096]{0:T(1024)} %param.22, f32[4096]{0:T(1024)} %bitcast.98, f32[4096]{0:T(1024)} %bitcast.99, f32[4096]{0:T(1024)} %bitcast.97, f32[4096]{0:T(1024)} %bitcast.96, ...), kind=kLoop, calls=%fused_computation.31 | loop fusion | flops 60817408 | bytes 8496640 | tf_op jit(solution)/shard_map/convert_element_type | solution.py:155
  47.4 6.5 %copy.61 = bf16[512,4096]{0,1:T(8,128)(2,1)} copy(bf16[512,4096]{1,0:T(8,128)(2,1)} %multiply_convert_fusion.6) | data formatting | bytes 8388608 | tf_op jit(solution)/shard_map/convert_element_type | solution.py:155
  53.9 45.9 %while.25 = (s32[]{:T(128)}, f32[4,512,2,4,128]{1,4,3,2,0:T(8,128)}, f32[4,2,4,128,128]{4,3,2,0,1:T(8,128)}, s32[4]{0:T(128)S(1)}, bf16[512,2,16,128]{0,3,2,1:T(...) while((s32[]{:T(128)}, ...), condition=%wide.region_4.5_spmd.clone, body=%wide.region_3.4_spmd.clone.sunk | while | flops 683409408 | bytes 8031427 | solution.py:93
  57.6 5.1 %bitcast_dynamic-update-slice_fusion.2 = f32[4,512,2,4,128]{1,4,3,2,0:T(8,128)} fusion(f32[4,512,2,4,128]{1,4,3,2,0:T(8,128)} %get-tuple-element.443, s32[]{:T(128)} %get-tuple-element.442, f32[2,4,512]{2,1,0:T(4,128)S(1)} %get-tuple-element.426, f32[2,4,512]{2,1,0:T(4,128)S(1)} %constant_dynamic-slice_fusion.6, ...), kind=kOutput, calls=%fused_computation.11.clone.1 | convolution fusion | flops 547356672 | bytes 5554692 | tf_op jit(solution)/shard_map/while/body/eval_jaxpr/while/body/eval_jaxpr/gits,sgip->tgip/dot_general | solution.py:83
  62.6 2.8 %fusion.40 = f32[4,2,4,128,128]{4,3,2,0,1:T(8,128)} fusion(f32[4,2,4,128,128]{4,3,2,0,1:T(8,128)} %get-tuple-element.444, s32[]{:T(128)} %get-tuple-element.442, f32[2,4,512]{2,1,0:T(4,128)S(1)} %get-tuple-element.427, f32[2,512,128]{2,1,0:T(8,128)S(1)} %get-tuple-element.464, bf16[512,2,16,128]{0,3,2,1:T(8,128)(2,1)} %get-tuple-element.460, ...), kind=kOutput, calls=%fused_computation.14.clone.1 | convolution fusion | flops 135266304 | bytes 2114052 | tf_op jit(solution)/shard_map/while/body/eval_jaxpr/while/body/eval_jaxpr/gisn,sgip->gipn/dot_general | solution.py:87
  69.1 5.0 %bitcast_dynamic-update-slice_fusion.2 = f32[4,512,2,4,128]{1,4,3,2,0:T(8,128)} fusion(f32[4,512,2,4,128]{1,4,3,2,0:T(8,128)} %get-tuple-element.443, s32[]{:T(128)} %get-tuple-element.442, f32[2,4,512]{2,1,0:T(4,128)S(1)} %get-tuple-element.426, f32[2,4,512]{2,1,0:T(4,128)S(1)} %constant_dynamic-slice_fusion.6, ...), kind=kOutput, calls=%fused_computation.11.clone.1 | convolution fusion | flops 547356672 | bytes 5554692 | tf_op jit(solution)/shard_map/while/body/eval_jaxpr/while/body/eval_jaxpr/gits,sgip->tgip/dot_general | solution.py:83
  74.1 2.8 %fusion.40 = f32[4,2,4,128,128]{4,3,2,0,1:T(8,128)} fusion(f32[4,2,4,128,128]{4,3,2,0,1:T(8,128)} %get-tuple-element.444, s32[]{:T(128)} %get-tuple-element.442, f32[2,4,512]{2,1,0:T(4,128)S(1)} %get-tuple-element.427, f32[2,512,128]{2,1,0:T(8,128)S(1)} %get-tuple-element.464, bf16[512,2,16,128]{0,3,2,1:T(8,128)(2,1)} %get-tuple-element.460, ...), kind=kOutput, calls=%fused_computation.14.clone.1 | convolution fusion | flops 135266304 | bytes 2114052 | tf_op jit(solution)/shard_map/while/body/eval_jaxpr/while/body/eval_jaxpr/gisn,sgip->gipn/dot_general | solution.py:87
  80.5 5.1 %bitcast_dynamic-update-slice_fusion.2 = f32[4,512,2,4,128]{1,4,3,2,0:T(8,128)} fusion(f32[4,512,2,4,128]{1,4,3,2,0:T(8,128)} %get-tuple-element.443, s32[]{:T(128)} %get-tuple-element.442, f32[2,4,512]{2,1,0:T(4,128)S(1)} %get-tuple-element.426, f32[2,4,512]{2,1,0:T(4,128)S(1)} %constant_dynamic-slice_fusion.6, ...), kind=kOutput, calls=%fused_computation.11.clone.1 | convolution fusion | flops 547356672 | bytes 5554692 | tf_op jit(solution)/shard_map/while/body/eval_jaxpr/while/body/eval_jaxpr/gits,sgip->tgip/dot_general | solution.py:83
  85.6 2.8 %fusion.40 = f32[4,2,4,128,128]{4,3,2,0,1:T(8,128)} fusion(f32[4,2,4,128,128]{4,3,2,0,1:T(8,128)} %get-tuple-element.444, s32[]{:T(128)} %get-tuple-element.442, f32[2,4,512]{2,1,0:T(4,128)S(1)} %get-tuple-element.427, f32[2,512,128]{2,1,0:T(8,128)S(1)} %get-tuple-element.464, bf16[512,2,16,128]{0,3,2,1:T(8,128)(2,1)} %get-tuple-element.460, ...), kind=kOutput, calls=%fused_computation.14.clone.1 | convolution fusion | flops 135266304 | bytes 2114052 | tf_op jit(solution)/shard_map/while/body/eval_jaxpr/while/body/eval_jaxpr/gisn,sgip->gipn/dot_general | solution.py:87
  92.0 5.0 %bitcast_dynamic-update-slice_fusion.2 = f32[4,512,2,4,128]{1,4,3,2,0:T(8,128)} fusion(f32[4,512,2,4,128]{1,4,3,2,0:T(8,128)} %get-tuple-element.443, s32[]{:T(128)} %get-tuple-element.442, f32[2,4,512]{2,1,0:T(4,128)S(1)} %get-tuple-element.426, f32[2,4,512]{2,1,0:T(4,128)S(1)} %constant_dynamic-slice_fusion.6, ...), kind=kOutput, calls=%fused_computation.11.clone.1 | convolution fusion | flops 547356672 | bytes 5554692 | tf_op jit(solution)/shard_map/while/body/eval_jaxpr/while/body/eval_jaxpr/gits,sgip->tgip/dot_general | solution.py:83
  97.0 2.8 %fusion.40 = f32[4,2,4,128,128]{4,3,2,0,1:T(8,128)} fusion(f32[4,2,4,128,128]{4,3,2,0,1:T(8,128)} %get-tuple-element.444, s32[]{:T(128)} %get-tuple-element.442, f32[2,4,512]{2,1,0:T(4,128)S(1)} %get-tuple-element.427, f32[2,512,128]{2,1,0:T(8,128)S(1)} %get-tuple-element.464, bf16[512,2,16,128]{0,3,2,1:T(8,128)(2,1)} %get-tuple-element.460, ...), kind=kOutput, calls=%fused_computation.14.clone.1 | convolution fusion | flops 135266304 | bytes 2114052 | tf_op jit(solution)/shard_map/while/body/eval_jaxpr/while/body/eval_jaxpr/gisn,sgip->gipn/dot_general | solution.py:87
  99.8 3.1 %broadcast_add_fusion = f32[1,2,16,128,128]{4,3,2,1,0:T(8,128)} fusion(f32[1,2,16,128,128]{4,3,2,1,0:T(8,128)} %bitcast.23, f32[2,16]{1,0:T(2,128)S(1)} %copy-done.3), kind=kLoop, calls=%fused_computation.37 | loop fusion | flops 524288 | bytes 4194432 | tf_op jit(solution)/shard_map/while/body/eval_jaxpr/add | solution.py:177
  103.1 9.1 %all-gather = f32[8,16,1]{1,2,0:T(1,128)S(1)} all-gather(f32[2,16,1]{1,2,0:T(1,128)S(1)} %copy.71), channel_id=2, replica_groups=mesh['groups'=2,'seq'=4,'head'=2,'sub'=2] {'seq'}, dimensions={0}, use_global_device_ids=true | all-gather | bytes 640 | tf_op jit(solution)/shard_map/all_gather | solution.py:21
  112.3 8.9 %copy.70 = f32[512,2,4,4,128]{0,4,3,2,1:T(8,128)} copy(f32[512,2,4,4,128]{0,4,3,1,2:T(8,128)} %bitcast.88) | data formatting | bytes 16777216 | tf_op jit(solution)/shard_map/while/body/eval_jaxpr/transpose | solution.py:94
  121.2 131.8 %all-gather.3.cloned.1.call-done = f32[4,2,16,128,128]{4,3,2,1,0:T(8,128)} async-done(((f32[1,2,16,128,128]{4,3,2,1,0:T(8,128)}), f32[4,2,16,128,128]{4,3,2,1,0:T(8,128)}) %all-gather.3.cloned.1.call-update) | async-done | bytes 8388624 | tf_op jit(solution)/shard_map/all_gather | solution.py:21
  254.1 8.9 %fusion.20 = bf16[512,2,16,128]{0,3,2,1:T(8,128)(2,1)} fusion(f32[512,2,16,128]{0,3,2,1:T(8,128)} %bitcast.85, bf16[512,2,16,128]{0,3,2,1:T(8,128)(2,1)} %get-tuple-element.495, f32[2,16]{1,0:T(2,128)S(1)} %mul.235, f32[512,2,16]{0,2,1:T(8,128)S(1)} %copy-done, f32[2,16,128,128]{3,2,1,0:T(8,128)S(1)} %get-tuple-element.187, ...), kind=kOutput, calls=%fused_computation.30 | convolution fusion | flops 3233808384 | bytes 19202176 | tf_op jit(solution)/shard_map/while/body/eval_jaxpr/tgn,gipn->tgip/dot_general | solution.py:109
  262.9 6.3 %copy.74 = bf16[512,4096]{1,0:T(8,128)(2,1)} copy(bf16[512,4096]{0,1:T(8,128)(2,1)} %bitcast.87) | data formatting | bytes 8388608 | tf_op jit(solution)/shard_map/reshape | solution.py:204
  (66 shorter events, 17.4 us)
Async XLA Ops:
  6.5 246.5 %all-gather.3.cloned.1.call-start = ((), (), s32[]{:S(2)}) async-start(), calls=%async_computation | async-start | bytes 10485760 | tf_op jit(solution)/shard_map/all_gather | solution.py:21
  8.1 20.3 %collective-permute-start = (bf16[3,4608]{1,0:T(4,128)(2,1)S(1)}, bf16[3,4608]{1,0:T(4,128)(2,1)S(1)}, u32[]{:S(2)}, u32[]{:S(2)}) collective-permute-start(bf16[3,4608]{1,0:T(4,128)(2,1)S(1)} %pad_maximum_fusion.2), channel_id=1, source_target_pairs={{0,4},{4,8},{8,12},{1,5},{5,9},{9,13},{2,6},{6,10},{10,14},{3,7},{... | collective-permute-start | bytes 82952 | tf_op jit(solution)/shard_map/ppermute | solution.py:16
  28.4 2.4 copy-start.2
  32.3 21.6 %copy-start.5 = (s32[4]{0:T(128)S(1)}, s32[4]{0:T(128)}, u32[]{:S(2)}) copy-start(s32[4]{0:T(128)} %iota_multiply_fusion) | copy-start | bytes 52
  53.9 45.9 %copy-start.3 = (f32[2,16]{1,0:T(2,128)S(1)}, f32[2,16]{1,0:T(2,128)}, u32[]{:S(2)}) copy-start(f32[2,16]{1,0:T(2,128)} %select_multiply_fusion) | copy-start | bytes 388
  53.9 49.1 %copy-start.1 = (f32[2,16,1]{2,1,0:T(8,128)S(1)}, f32[2,16,1]{2,1,0:T(8,128)}, u32[]{:S(2)}) copy-start(f32[2,16,1]{2,1,0:T(8,128)} %get-tuple-element.306) | copy-start | bytes 388
  53.9 49.1 %copy-start.4 = (f32[32]{0:T(128)S(1)}, f32[32]{0:T(128)}, u32[]{:S(2)}) copy-start(f32[32]{0:T(128)} %param.20) | copy-start | bytes 388
  253.2 0.8 copy-start
Sparse Core Ops, SparseCore 0:
  103.1 149.8 all-gather.2
where the time goes:
time: 279 us; the launch traced here: 276 us
  waiting for transfers between devices  132 us (47%)
  matrix products  40.8 us (15%)
  local copies, waits for them, and re-layouts  36.5 us (13%)
  other arithmetic  30 us (11%)
  between operations  15 us (5%)
  blocking collectives  9.14 us (3%)
  loops' own time  7.88 us (3%)
  starting transfers between devices  4.93 us (2%)
    all_gather x1, waiting for transfers between devices, carried_in_2(): gathered = jax.tree.map(lambda a: lax.all_gather(a, axis), part)  132 us
    dot_general x4, matrix products, one_slice(): jnp.einsum('gits,sgip->tgip', weights, x_part, preferred_element_type=jnp...  20.1 us
    convert_element_type x1, other arithmetic, per_device(): mixed_x = convolve(jnp.concatenate([rim_x, x_raw], axis=0), conv_x, conv_...  15.2 us
    dot_general x4, matrix products, one_slice(): jnp.einsum('gisn,sgip->gipn', tail_weights, x_part, preferred_element_typ...  11.4 us
    all_gather x1, blocking collectives, carried_in_2(): gathered = jax.tree.map(lambda a: lax.all_gather(a, axis), part)  9.14 us
    transpose x1, local copies, waits for them, and re-layouts, block_terms(): jnp.transpose(inner_parts, (1, 2, 0, 3, 4))  8.9 us
    dot_general x1, matrix products, block_output(): jnp.einsum('tgn,gipn->tgip', c_float, carried, precision=lax.Precision.HI...  8.86 us
    another operation x1, loops' own time, block_terms(): inner_parts, state_parts = lax.map(one_slice, starts)  7.87 us
  transfers between devices with their start and end apart: 2, of which 1 were waited for; matrix products, arithmetic and copies ran while one was open for 8% of the time, Pallas kernels for 0%

commit v1 on v0

v1 whole, which is shorter than its diff:
```python
import functools
import math

import jax
import jax.numpy as jnp
from jax import lax
from jax.experimental import pallas as pl
from jax.experimental.pallas import tpu as pltpu
from jax.sharding import PartitionSpec as P

D = 128
Q = 128
BLK = 512
NQ = BLK // Q
HC = 4
CW = HC * D
RIM = 8
LOG2E = math.log2(math.e)
F32 = jnp.float32
BF16 = jnp.bfloat16


def doc_of(pos, starts_ref):
    count = jnp.zeros_like(pos)
    for j in range(starts_ref.shape[0]):
        count = count + (pos >= starts_ref[j]).astype(jnp.int32)
    return count - 1


def silu_half(u):
    return u + u * jnp.tanh(u)


def params_kernel(row_ref, starts_ref, dt_ref, bias_ref, alog_ref, cols_ref, rows_ref, dec_ref, mask_ref):
    first = row_ref[0]
    heads = dt_ref.shape[0]
    v = dt_ref[...] + bias_ref[...]
    step = jnp.maximum(v, 0.0) + jnp.log(1.0 + jnp.exp(-jnp.abs(v)))
    rate = -jnp.exp(alog_ref[...]) * step
    tri = (
        lax.broadcasted_iota(jnp.int32, (Q, Q), 0) <= lax.broadcasted_iota(jnp.int32, (Q, Q), 1)
    ).astype(F32)
    doc_before = doc_of(first - 1, starts_ref)
    base = jnp.zeros((heads, 1), F32)
    for q in range(NQ):
        span = slice(q * Q, (q + 1) * Q)
        cum = jnp.dot(rate[:, span], tri, precision=lax.Precision.HIGHEST, preferred_element_type=F32)
        last = cum[:, Q - 1 : Q]
        step_q = step[:, span]
        pos = first + q * Q + lax.broadcasted_iota(jnp.int32, (1, Q), 1)
        doc = doc_of(pos, starts_ref)
        doc_prev = doc_of(first + q * Q - 1, starts_ref)
        doc_end = doc_of(first + (q + 1) * Q - 1, starts_ref)
        tail = jnp.where(doc == doc_end, jnp.exp(last - cum) * step_q, 0.0)
        entry = jnp.where(doc == doc_prev, jnp.exp(cum), 0.0)
        far = jnp.where(doc == doc_before, jnp.exp(cum + base), 0.0)
        packed = [tail, cum * LOG2E, entry, far]
        if 4 * heads < D:
            packed.append(jnp.zeros((D - 4 * heads, Q), F32))
        cols_ref[span, :] = jnp.transpose(jnp.concatenate(packed, axis=0), (1, 0))
        rows_ref[:, span] = (cum - jnp.log(step_q)) * LOG2E
        keep = jnp.where(doc_end == doc_prev, 1.0, 0.0)
        dec_ref[:, q : q + 1] = jnp.exp(last) * keep
        base = base + last
    doc_last = doc_of(first + BLK - 1, starts_ref)
    dec_ref[:, NQ : NQ + 1] = jnp.exp(base) * jnp.where(doc_last == doc_before, 1.0, 0.0)
    dec_ref[:, NQ + 1 :] = jnp.zeros((heads, dec_ref.shape[1] - NQ - 1), F32)
    for k in range(3):
        pos = first + lax.broadcasted_iota(jnp.int32, (BLK, D), 0)
        same = doc_of(pos, starts_ref) == doc_of(pos - (3 - k), starts_ref)
        mask_ref[k] = same.astype(F32)


def fill(buf_ref, rim_ref, x_ref):
    buf_ref[0:RIM, :] = rim_ref[...].astype(F32)
    for r in range(0, BLK, Q):
        buf_ref[RIM + r : RIM + r + Q, :] = x_ref[r : r + Q, :].astype(F32)


def conv_tile(buf_ref, w_ref, b_ref, mask_ref, r, lanes):
    total = 0.5 * w_ref[3:4, lanes] * buf_ref[pl.ds(RIM + r, Q), lanes] + 0.5 * b_ref[0:1, lanes]
    for k in range(3):
        term = 0.5 * w_ref[k : k + 1, lanes] * buf_ref[pl.ds(RIM - 3 + k + r, Q), lanes]
        total = total + mask_ref[k, r : r + Q, :] * term
    return silu_half(total).astype(BF16)


def state_kernel(
    row_ref, starts_ref, dec_ref, x_ref, rim_ref, wx_ref, bx_ref, mask_ref, cols_ref,
    bc_ref, rimbc_ref, wbc_ref, bbc_ref,
    mx_ref, enter_ref, end_ref, c_ref, score_ref,
    buf_ref, scaled_ref, bt_ref, *, groups, per_group,
):
    c = pl.program_id(0)
    heads = groups * per_group * HC

    @pl.when(c == 0)
    def first():
        first_row = row_ref[0]
        for part in range(2):
            for g in range(groups):
                lo = (part * groups + g) * D
                lanes = slice(lo, lo + D)
                buf_ref[0:RIM, 0:D] = rimbc_ref[:, lanes].astype(F32)
                buf_ref[RIM : RIM + BLK, 0:D] = bc_ref[:, lanes].astype(F32)
                for r in range(0, BLK, Q):
                    total = 0.5 * wbc_ref[3:4, lanes] * buf_ref[pl.ds(RIM + r, Q), 0:D]
                    total = total + 0.5 * bbc_ref[0:1, lanes]
                    for k in range(3):
                        term = 0.5 * wbc_ref[k : k + 1, lanes] * buf_ref[pl.ds(RIM - 3 + k + r, Q), 0:D]
                        total = total + mask_ref[k, r : r + Q, :] * term
                    mixed = silu_half(total)
                    if part == 0:
                        bt_ref[g, :, r : r + Q] = jnp.transpose(mixed, (1, 0)).astype(BF16)
                    else:
                        c_ref[r : r + Q, g * D : (g + 1) * D] = mixed.astype(BF16)
        for q in range(NQ):
            at = first_row + q * Q
            row = at + lax.broadcasted_iota(jnp.int32, (Q, Q), 0)
            col = at + lax.broadcasted_iota(jnp.int32, (Q, Q), 1)
            keep = (row >= col) & (doc_of(row, starts_ref) == doc_of(col, starts_ref))
            for g in range(groups):
                score = jnp.dot(
                    c_ref[q * Q : (q + 1) * Q, g * D : (g + 1) * D],
                    bt_ref[g, :, q * Q : (q + 1) * Q],
                    preferred_element_type=F32,
                )
                score_ref[q * Q : (q + 1) * Q, g * D : (g + 1) * D] = jnp.where(keep, score, 0.0)

    fill(buf_ref, rim_ref, x_ref)
    shift = lax.rem(D - HC * c, D)
    for q in range(NQ):
        r = q * Q
        cols = pltpu.roll(cols_ref[r : r + Q, :], shift, 1)
        for i in range(HC):
            lanes = slice(i * D, (i + 1) * D)
            mixed = conv_tile(buf_ref, wx_ref, bx_ref, mask_ref, r, lanes)
            mx_ref[r : r + Q, lanes] = mixed
            scaled_ref[r : r + Q, lanes] = (mixed.astype(F32) * cols[:, i : i + 1]).astype(BF16)
    g = lax.div(c, per_group)
    for q in range(NQ):
        part = jnp.dot(
            bt_ref[g, :, q * Q : (q + 1) * Q],
            scaled_ref[q * Q : (q + 1) * Q, :],
            preferred_element_type=F32,
        )
        for i in range(HC):
            lanes = slice(i * D, (i + 1) * D)
            if q == 0:
                end_ref[:, lanes] = part[:, lanes]
            else:
                before = end_ref[:, lanes]
                enter_ref[q - 1, :, lanes] = before.astype(BF16)
                end_ref[:, lanes] = dec_ref[c * HC + i, q] * before + part[:, lanes]


def intra_kernel(skip_ref, mx_ref, enter_ref, c_ref, score_ref, cols_ref, rows_ref, y_ref, *, heads):
    c = pl.program_id(0)
    shift = lax.rem(D - HC * c, D)
    for q in range(NQ):
        r = q * Q
        cols = pltpu.roll(cols_ref[r : r + Q, :], shift, 1)
        score = score_ref[r : r + Q, :]
        both = rows_ref[pl.ds(pl.multiple_of(2 * HC * lax.div(c, 2), 2 * HC), 2 * HC), r : r + Q]
        terms = jnp.where(lax.rem(c, 2) == 0, both[:HC], both[HC:])
        if q:
            far = jnp.dot(c_ref[r : r + Q, :], enter_ref[q - 1], preferred_element_type=F32)
        for i in range(HC):
            lanes = slice(i * D, (i + 1) * D)
            head = c * HC + i
            gap = cols[:, heads + i : heads + i + 1] - terms[i : i + 1]
            weight = (score * jnp.exp2(jnp.minimum(gap, 100.0))).astype(BF16)
            x = mx_ref[r : r + Q, lanes]
            y = jnp.dot(weight, x, preferred_element_type=F32) + skip_ref[head] * x.astype(F32)
            if q:
                y = y + cols[:, 2 * heads + i : 2 * heads + i + 1] * far[:, lanes]
            y_ref[r : r + Q, lanes] = y.astype(BF16)


def start_kernel(table_ref, end_ref, send_ref):
    send_ref[...] = end_ref[...].astype(BF16)


def pass_kernel(table_ref, dec_ref, recv_ref, end_ref, held_ref, send_ref, keep_ref, *, turn, stream, per_stream):
    chunk = stream * per_stream + table_ref[2 * turn]
    for i in range(HC):
        lanes = slice(i * D, (i + 1) * D)
        got = recv_ref[:, lanes]
        keep_ref[:, lanes] = got
        send_ref[:, lanes] = (
            dec_ref[chunk * HC + i, NQ] * got.astype(F32) + end_ref[:, lanes]
        ).astype(BF16)


def keep_kernel(table_ref, recv_ref, held_ref, keep_ref):
    keep_ref[...] = recv_ref[...]


def final_kernel(y_ref, c_ref, cols_ref, held0_ref, held1_ref, out_ref, *, heads, per_stream):
    c = pl.program_id(0)
    held = jnp.where(c < per_stream, held0_ref[...], held1_ref[...])
    shift = lax.rem(D - HC * c, D)
    for q in range(NQ):
        r = q * Q
        cols = pltpu.roll(cols_ref[r : r + Q, :], shift, 1)
        far = jnp.dot(c_ref[r : r + Q, :], held, preferred_element_type=F32)
        for i in range(HC):
            lanes = slice(i * D, (i + 1) * D)
            y = y_ref[r : r + Q, lanes].astype(F32)
            out_ref[r : r + Q, lanes] = (
                y + cols[:, 3 * heads + i : 3 * heads + i + 1] * far[:, lanes]
            ).astype(BF16)


SMEM = pl.BlockSpec(memory_space=pltpu.SMEM)
ANY = pl.BlockSpec(memory_space=pl.ANY)


def whole(shape):
    return pl.BlockSpec(shape, lambda c: (0,) * len(shape))


def shape_of(shape, dtype):
    return jax.ShapeDtypeStruct(shape, dtype)


def per_device(
    x_raw, bc_raw, dt_raw, dt_bias, a_log, d_skip, conv_x, conv_x_bias, conv_bc, conv_bc_bias, doc_starts
):
    rows, width = x_raw.shape
    groups = bc_raw.shape[2] // D
    heads = dt_raw.shape[0]
    chunks = heads // HC
    per_group = chunks // groups
    seq = lax.axis_size("seq")
    place = lax.axis_index("seq")
    first_row = (place * rows).astype(jnp.int32).reshape(1)
    ring = [(i, (i + 1) % seq) for i in range(seq)]

    bc = bc_raw.reshape(rows, -1)
    tail = jnp.concatenate([x_raw[rows - RIM :], bc_raw[rows - RIM :].reshape(RIM, -1)], axis=1)
    rim = lax.ppermute(tail, "seq", ring)

    cols, row_terms, dec, mask = pl.pallas_call(
        params_kernel,
        in_specs=[SMEM, SMEM] + [pl.BlockSpec(memory_space=pltpu.VMEM)] * 3,
        out_specs=[pl.BlockSpec(memory_space=pltpu.VMEM)] * 4,
        out_shape=[
            shape_of((BLK, D), F32),
            shape_of((heads, BLK), F32),
            shape_of((heads, 8), F32),
            shape_of((3, BLK, D), F32),
        ],
        name="params",
    )(first_row, doc_starts, dt_raw, dt_bias[:, None], a_log[:, None])

    mixed_x, enter, end, mixed_c, score = pl.pallas_call(
        functools.partial(state_kernel, groups=groups, per_group=per_group),
        grid=(chunks,),
        in_specs=[
            SMEM, SMEM, SMEM,
            pl.BlockSpec((BLK, CW), lambda c: (0, c)),
            pl.BlockSpec((RIM, CW), lambda c: (0, c)),
            pl.BlockSpec((4, CW), lambda c: (0, c)),
            pl.BlockSpec((1, CW), lambda c: (0, c)),
            whole((3, BLK, D)),
            whole((BLK, D)),
            whole((BLK, 2 * groups * D)),
            whole((RIM, 2 * groups * D)),
            whole((4, 2 * groups * D)),
            whole((1, 2 * groups * D)),
        ],
        out_specs=[
            pl.BlockSpec((BLK, CW), lambda c: (0, c)),
            pl.BlockSpec((NQ - 1, D, CW), lambda c: (0, 0, c)),
            pl.BlockSpec((D, CW), lambda c: (0, c)),
            whole((BLK, groups * D)),
            whole((BLK, groups * D)),
        ],
        out_shape=[
            shape_of((BLK, width), BF16),
            shape_of((NQ - 1, D, width), BF16),
            shape_of((D, width), F32),
            shape_of((BLK, groups * D), BF16),
            shape_of((BLK, groups * D), F32),
        ],
        scratch_shapes=[
            pltpu.VMEM((RIM + BLK, CW), F32),
            pltpu.VMEM((BLK, CW), BF16),
            pltpu.VMEM((groups, D, BLK), BF16),
        ],
        name="states",
    )(
        first_row, doc_starts, dec, x_raw, rim[:, :width], conv_x, conv_x_bias[None], mask, cols,
        bc, rim[:, width:], conv_bc.reshape(4, -1), conv_bc_bias.reshape(1, -1),
    )

    streams = 2
    per_stream = chunks // streams
    slots = per_stream + seq - 2
    turn_no = jnp.arange(slots + 1, dtype=jnp.int32) - place
    valid = (turn_no >= 0) & (turn_no < per_stream) & (place > 0)
    table = jnp.stack(
        [jnp.clip(turn_no, 0, per_stream - 1), jnp.where(valid, turn_no, per_stream)], axis=1
    ).astype(jnp.int32).reshape(-1)

    chunk_shape = shape_of((D, CW), BF16)
    held_shape = shape_of((D, (per_stream + 1) * CW), BF16)
    held = [jnp.zeros(held_shape.shape, BF16) for _ in range(streams)]
    flying = [None] * streams
    for s in range(streams):
        send = pl.pallas_call(
            start_kernel,
            grid_spec=pltpu.PrefetchScalarGridSpec(
                num_scalar_prefetch=1,
                grid=(1,),
                in_specs=[pl.BlockSpec((D, CW), lambda i, tab, s=s: (0, s * per_stream + tab[0]))],
                out_specs=pl.BlockSpec((D, CW), lambda i, tab: (0, 0)),
            ),
            out_shape=chunk_shape,
            name="start",
        )(table, end)
        flying[s] = lax.ppermute(send, "seq", ring)

    y = pl.pallas_call(
        functools.partial(intra_kernel, heads=heads),
        grid=(chunks,),
        in_specs=[
            SMEM,
            pl.BlockSpec((BLK, CW), lambda c: (0, c)),
            pl.BlockSpec((NQ - 1, D, CW), lambda c: (0, 0, c)),
            pl.BlockSpec((BLK, D), lambda c: (0, c // per_group)),
            pl.BlockSpec((BLK, D), lambda c: (0, c // per_group)),
            whole((BLK, D)),
            whole((heads, BLK)),
        ],
        out_specs=pl.BlockSpec((BLK, CW), lambda c: (0, c)),
        out_shape=shape_of((BLK, width), BF16),
        cost_estimate=pl.CostEstimate(flops=4 * BLK * Q * width, bytes_accessed=8 * BLK * width, transcendentals=0),
        name="intra",
    )(d_skip, mixed_x, enter, mixed_c, score, cols, row_terms)

    for turn in range(1, slots + 1):
        for s in range(streams):
            if turn == slots:
                held[s] = pl.pallas_call(
                    keep_kernel,
                    grid_spec=pltpu.PrefetchScalarGridSpec(
                        num_scalar_prefetch=1,
                        grid=(1,),
                        in_specs=[pl.BlockSpec((D, CW), lambda i, tab: (0, 0)), ANY],
                        out_specs=pl.BlockSpec((D, CW), lambda i, tab, t=turn: (0, tab[2 * t + 1])),
                    ),
                    out_shape=held_shape,
                    input_output_aliases={2: 0},
                    name="keep",
                )(table, flying[s], held[s])
                continue
            send, held[s] = pl.pallas_call(
                functools.partial(pass_kernel, turn=turn, stream=s, per_stream=per_stream),
                grid_spec=pltpu.PrefetchScalarGridSpec(
                    num_scalar_prefetch=1,
                    grid=(1,),
                    in_specs=[
                        SMEM,
                        pl.BlockSpec((D, CW), lambda i, tab: (0, 0)),
                        pl.BlockSpec((D, CW), lambda i, tab, t=turn, s=s: (0, s * per_stream + tab[2 * t])),
                        ANY,
                    ],
                    out_specs=[
                        pl.BlockSpec((D, CW), lambda i, tab: (0, 0)),
                        pl.BlockSpec((D, CW), lambda i, tab, t=turn: (0, tab[2 * t + 1])),
                    ],
                ),
                out_shape=[chunk_shape, held_shape],
                input_output_aliases={4: 1},
                name="pass",
            )(table, dec, flying[s], end, held[s])
            flying[s] = lax.ppermute(send, "seq", ring)

    return pl.pallas_call(
        functools.partial(final_kernel, heads=heads, per_stream=per_stream),
        grid=(chunks,),
        in_specs=[
            pl.BlockSpec((BLK, CW), lambda c: (0, c)),
            pl.BlockSpec((BLK, D), lambda c: (0, c // per_group)),
            whole((BLK, D)),
            pl.BlockSpec((D, CW), lambda c: (0, jnp.minimum(c, per_stream - 1))),
            pl.BlockSpec((D, CW), lambda c: (0, jnp.maximum(c - per_stream, 0))),
        ],
        out_specs=pl.BlockSpec((BLK, CW), lambda c: (0, c)),
        out_shape=shape_of((BLK, width), BF16),
        name="final",
    )(y, mixed_c, cols, held[0], held[1])


def solution(mesh):
    return jax.shard_map(
        per_device,
        mesh=mesh,
        in_specs=(
            P(("groups", "seq"), ("head", "sub")),
            P(("groups", "seq"), None, ("head", "sub")),
            P(("head", "sub"), ("groups", "seq")),
            P(("head", "sub")),
            P(("head", "sub")),
            P(("head", "sub")),
            P(None, ("head", "sub")),
            P(("head", "sub")),
            P(None, None, ("head", "sub")),
            P(None, ("head", "sub")),
            P("groups"),
        ),
        out_specs=P(("groups", "seq"), ("head", "sub")),
        check_vma=False,
    )
```

time: 279 us -> 120 us (0.43)
  waiting for transfers between devices: 132 us -> 16.7 us
  Pallas kernels: 0 us -> 73.5 us
  matrix products: 40.8 us -> 0 us
  other arithmetic: 30 us -> 0.03 us
  local copies, waits for them, and re-layouts: 36.5 us -> 18.9 us
  between operations: 15 us -> 0.08 us
  blocking collectives: 9.14 us -> 0 us
  loops' own time: 7.88 us -> 0 us
  starting transfers between devices: 4.93 us -> 9.4 us
    all_gather x1 -> x0, waiting for transfers between devices: 132 us -> none  [carried_in_2(): gathered = jax.tree.map(lambda a: lax.all_gather(a, axis), part)]
    pallas_call x0 -> x18, Pallas kernels: none -> 73.5 us  [the longest x10 24.4 us: per_device(): pl.pallas_call(functools.partial(pass_kernel, turn=turn, stream=s, per_st...]
    dot_general x10 -> x0, matrix products: 40.8 us -> none  [the longest x4 20.1 us: one_slice(): jnp.einsum('gits,sgip->tgip', weights, x_part, preferred_element_type=jnp...]
    convert_element_type x3 -> x0, other arithmetic: 17.3 us -> none  [the longest x1 15.2 us: per_device(): mixed_x = convolve(jnp.concatenate([rim_x, x_raw], axis=0), conv_x, conv_...]
    ppermute x1 -> x13, waiting for transfers between devices: 0.01 us -> 16.7 us  [the longest x12 16.7 us: per_device(): flying[s] = lax.ppermute(send, 'seq', ring)]
    all_gather x1 -> x0, blocking collectives: 9.14 us -> none  [carried_in_2(): gathered = jax.tree.map(lambda a: lax.all_gather(a, axis), part)]
    transpose x1 -> x0, local copies, waits for them, and re-layouts: 8.9 us -> none  [block_terms(): jnp.transpose(inner_parts, (1, 2, 0, 3, 4))]
    unnamed x16 -> x29, local copies, waits for them, and re-layouts: 3.04 us -> 11.6 us
  transfers between devices with their start and end apart: 2 -> 13, of which waited for: 1 -> 9; matrix products, arithmetic and copies ran while one was open for 8% -> 8% of each run, Pallas kernels for 0% -> 37%
where the time goes in v1:
time: 120 us; the launch traced here: 119 us
  Pallas kernels  73.5 us (61%)
  local copies, waits for them, and re-layouts  18.9 us (16%)
  waiting for transfers between devices  16.7 us (14%)
  starting transfers between devices  9.4 us (8%)
    pallas_call x10, Pallas kernels, per_device(): pl.pallas_call(functools.partial(pass_kernel, turn=turn, stream=s, per_st...  24.4 us
    ppermute x12, waiting for transfers between devices, per_device(): flying[s] = lax.ppermute(send, 'seq', ring)  16.7 us
    pallas_call x1, Pallas kernels, per_device(): pl.pallas_call(functools.partial(state_kernel, groups=groups, per_group=p...  14.8 us
    pallas_call x1, Pallas kernels, per_device(): pl.pallas_call(functools.partial(intra_kernel, heads=heads), grid=(chunks...  11.9 us
    unnamed x29, local copies, waits for them, and re-layouts  11.6 us
    pallas_call x1, Pallas kernels, per_device(): pl.pallas_call(functools.partial(final_kernel, heads=heads, per_stream=pe...  10.2 us
    ppermute x12, starting transfers between devices, per_device(): flying[s] = lax.ppermute(send, 'seq', ring)  6.33 us
    pallas_call x2, Pallas kernels, per_device(): pl.pallas_call(start_kernel, grid_spec=pltpu.PrefetchScalarGridSpec(num_s...  4.56 us
  transfers between devices with their start and end apart: 13, of which 9 were waited for; matrix products, arithmetic and copies ran while one was open for 8% of the time, Pallas kernels for 37%

profile of v1, /device:TPU:0, one launch (start us, length us, event | category | flops | bytes accessed | tf_op | source)
XLA Modules:
  0.0 118.6 jit_solution(17659245707992577720)
XLA Ops:
  1.6 3.1 %collective-permute-start = (bf16[8,4608]{1,0:T(8,128)(2,1)S(1)}, bf16[8,4608]{1,0:T(8,128)(2,1)S(1)}, u32[]{:S(2)}, u32[]{:S(2)}) collective-permute-start(bf16[8,4608]{1,0:T(8,128)(2,1)S(1)} %pad_maximum_fusion), channel_id=1, source_target_pairs={{0,4},{4,8},{8,12},{12,0},{1,5},{5,9},{9,13},{13,1},{2,6},{6,10},{... | collective-permute-start | bytes 221192 | tf_op jit(solution)/shard_map/ppermute | solution.py:242
  7.3 1.9 %copy.32 = bf16[64,8,2,256]{3,1,2,0:T(8,128)(2,1)} copy(bf16[64,8,2,256]{3,2,1,0:T(2,128)(2,1)} %bitcast.15) | data formatting | bytes 1048576
  12.4 3.1 %params.1 = (f32[512,128]{1,0:T(8,128)}, f32[32,512]{1,0:T(8,128)}, f32[32,8]{1,0:T(8,128)}, f32[3,512,128]{2,1,0:T(8,128)}) custom-call(s32[1]{0:T(128)} %bitcast.row_ref, s32[4]{0:T(128)} %starts_ref.3, f32[32,512]{1,0:T(8,128)} %dt_ref.1, f32[32,1]{1,0:T(8,128)} %copy.28.bias_ref, f32[32,1]{1,0:T(8,128)} %copy.29.alog_ref), custom_call_target="tpu_custom_call" | custom-call | tf_op jit(solution)/shard_map/params/pallas_call | solution.py:244
  16.8 14.8 %states.1 = (bf16[512,4096]{1,0:T(8,128)(2,1)}, bf16[3,128,4096]{2,1,0:T(8,128)(2,1)}, f32[128,4096]{1,0:T(8,128)}, bf16[512,256]{1,0:T(8,128)(2,1)}, f32[512,256]{1,0:T(8,128)}) custom-call(s32[1]{0:T(128)} %bitcast.row_ref, s32[4]{0:T(128)} %starts_ref.3, f32[32,8]{1,0:T(8,128)} %get-tuple-element.34.dec_ref, bf16[512,4096]{1,0:T(8,128)(2,1)} %x_ref.1, ...), custom_call_target="tpu_custom_call" | custom-call | tf_op jit(solution)/shard_map/states/pallas_call | solution.py:257
  31.5 2.3 %start.3 = bf16[128,512]{1,0:T(8,128)(2,1)} custom-call(s32[14]{0:T(128)} %reshape.49.table_ref, f32[128,4096]{1,0:T(8,128)} %get-tuple-element.42.end_ref), custom_call_target="tpu_custom_call" | custom-call | tf_op jit(solution)/shard_map/start/pallas_call | solution.py:312
  35.4 2.3 %start.2 = bf16[128,512]{1,0:T(8,128)(2,1)} custom-call(s32[14]{0:T(128)} %reshape.49.table_ref, f32[128,4096]{1,0:T(8,128)} %get-tuple-element.42.end_ref), custom_call_target="tpu_custom_call" | custom-call | tf_op jit(solution)/shard_map/start/pallas_call | solution.py:312
  41.7 2.4 %pass.15 = (bf16[128,512]{1,0:T(8,128)(2,1)}, bf16[128,2560]{1,0:T(8,128)(2,1)}) custom-call(s32[14]{0:T(128)} %reshape.49.table_ref, f32[32,8]{1,0:T(8,128)} %get-tuple-element.34.dec_ref, bf16[128,512]{1,0:T(8,128)(2,1)} %copy-done.9, f32[128,4096]{1,0:T(8,128)} %get-tuple-element.42.end_ref, ...), custom_call_target="tpu_custom_call", output_to_operand_aliasing={{1}: (4, {})} | custom-call | tf_op jit(solution)/shard_map/pass/pallas_call | solution.py:359
  45.6 2.4 %pass.10 = (bf16[128,512]{1,0:T(8,128)(2,1)}, bf16[128,2560]{1,0:T(8,128)(2,1)}) custom-call(s32[14]{0:T(128)} %reshape.49.table_ref, f32[32,8]{1,0:T(8,128)} %get-tuple-element.34.dec_ref, bf16[128,512]{1,0:T(8,128)(2,1)} %copy-done.2, f32[128,4096]{1,0:T(8,128)} %get-tuple-element.42.end_ref, ...), custom_call_target="tpu_custom_call", output_to_operand_aliasing={{1}: (4, {})} | custom-call | tf_op jit(solution)/shard_map/pass/pallas_call | solution.py:359
  49.5 2.1 %collective-permute-done.8.recv_ref = bf16[128,512]{1,0:T(8,128)(2,1)S(1)} collective-permute-done((bf16[128,512]{1,0:T(8,128)(2,1)}, bf16[128,512]{1,0:T(8,128)(2,1)S(1)}, u32[]{:S(2)}, u32[]{:S(2)}) %collective-permute-start.8) | collective-permute-done | bytes 131104 | tf_op jit(solution)/shard_map/ppermute | solution.py:379
  52.2 2.5 %pass.16 = (bf16[128,512]{1,0:T(8,128)(2,1)}, bf16[128,2560]{1,0:T(8,128)(2,1)}) custom-call(s32[14]{0:T(128)} %reshape.49.table_ref, f32[32,8]{1,0:T(8,128)} %get-tuple-element.34.dec_ref, bf16[128,512]{1,0:T(8,128)(2,1)} %copy-done.1, f32[128,4096]{1,0:T(8,128)} %get-tuple-element.42.end_ref, ...), custom_call_target="tpu_custom_call", output_to_operand_aliasing={{1}: (4, {})} | custom-call | tf_op jit(solution)/shard_map/pass/pallas_call | solution.py:359
  55.7 2.4 %pass.11 = (bf16[128,512]{1,0:T(8,128)(2,1)}, bf16[128,2560]{1,0:T(8,128)(2,1)}) custom-call(s32[14]{0:T(128)} %reshape.49.table_ref, f32[32,8]{1,0:T(8,128)} %get-tuple-element.34.dec_ref, bf16[128,512]{1,0:T(8,128)(2,1)} %copy-done.3, f32[128,4096]{1,0:T(8,128)} %get-tuple-element.42.end_ref, ...), custom_call_target="tpu_custom_call", output_to_operand_aliasing={{1}: (4, {})} | custom-call | tf_op jit(solution)/shard_map/pass/pallas_call | solution.py:359
  58.8 4.1 %collective-permute-done.9.recv_ref = bf16[128,512]{1,0:T(8,128)(2,1)S(1)} collective-permute-done((bf16[128,512]{1,0:T(8,128)(2,1)}, bf16[128,512]{1,0:T(8,128)(2,1)S(1)}, u32[]{:S(2)}, u32[]{:S(2)}) %collective-permute-start.9) | collective-permute-done | bytes 131104 | tf_op jit(solution)/shard_map/ppermute | solution.py:379
  63.5 2.5 %pass.17 = (bf16[128,512]{1,0:T(8,128)(2,1)}, bf16[128,2560]{1,0:T(8,128)(2,1)}) custom-call(s32[14]{0:T(128)} %reshape.49.table_ref, f32[32,8]{1,0:T(8,128)} %get-tuple-element.34.dec_ref, bf16[128,512]{1,0:T(8,128)(2,1)} %copy-done.4, f32[128,4096]{1,0:T(8,128)} %get-tuple-element.42.end_ref, ...), custom_call_target="tpu_custom_call", output_to_operand_aliasing={{1}: (4, {})} | custom-call | tf_op jit(solution)/shard_map/pass/pallas_call | solution.py:359
  66.6 2.4 %pass.12 = (bf16[128,512]{1,0:T(8,128)(2,1)}, bf16[128,2560]{1,0:T(8,128)(2,1)}) custom-call(s32[14]{0:T(128)} %reshape.49.table_ref, f32[32,8]{1,0:T(8,128)} %get-tuple-element.34.dec_ref, bf16[128,512]{1,0:T(8,128)(2,1)} %copy-done.5, f32[128,4096]{1,0:T(8,128)} %get-tuple-element.42.end_ref, ...), custom_call_target="tpu_custom_call", output_to_operand_aliasing={{1}: (4, {})} | custom-call | tf_op jit(solution)/shard_map/pass/pallas_call | solution.py:359
  69.1 4.2 %collective-permute-done.10.recv_ref = bf16[128,512]{1,0:T(8,128)(2,1)S(1)} collective-permute-done((bf16[128,512]{1,0:T(8,128)(2,1)}, bf16[128,512]{1,0:T(8,128)(2,1)S(1)}, u32[]{:S(2)}, u32[]{:S(2)}) %collective-permute-start.10) | collective-permute-done | bytes 131104 | tf_op jit(solution)/shard_map/ppermute | solution.py:379
  74.0 2.5 %pass.18 = (bf16[128,512]{1,0:T(8,128)(2,1)}, bf16[128,2560]{1,0:T(8,128)(2,1)}) custom-call(s32[14]{0:T(128)} %reshape.49.table_ref, f32[32,8]{1,0:T(8,128)} %get-tuple-element.34.dec_ref, bf16[128,512]{1,0:T(8,128)(2,1)} %copy-done.6, f32[128,4096]{1,0:T(8,128)} %get-tuple-element.42.end_ref, ...), custom_call_target="tpu_custom_call", output_to_operand_aliasing={{1}: (4, {})} | custom-call | tf_op jit(solution)/shard_map/pass/pallas_call | solution.py:359
  77.5 2.4 %pass.13 = (bf16[128,512]{1,0:T(8,128)(2,1)}, bf16[128,2560]{1,0:T(8,128)(2,1)}) custom-call(s32[14]{0:T(128)} %reshape.49.table_ref, f32[32,8]{1,0:T(8,128)} %get-tuple-element.34.dec_ref, bf16[128,512]{1,0:T(8,128)(2,1)} %copy-done.7, f32[128,4096]{1,0:T(8,128)} %get-tuple-element.42.end_ref, ...), custom_call_target="tpu_custom_call", output_to_operand_aliasing={{1}: (4, {})} | custom-call | tf_op jit(solution)/shard_map/pass/pallas_call | solution.py:359
  80.3 3.2 %collective-permute-done.11.recv_ref = bf16[128,512]{1,0:T(8,128)(2,1)S(1)} collective-permute-done((bf16[128,512]{1,0:T(8,128)(2,1)}, bf16[128,512]{1,0:T(8,128)(2,1)S(1)}, u32[]{:S(2)}, u32[]{:S(2)}) %collective-permute-start.11) | collective-permute-done | bytes 131104 | tf_op jit(solution)/shard_map/ppermute | solution.py:379
  84.1 2.4 %pass.19 = (bf16[128,512]{1,0:T(8,128)(2,1)}, bf16[128,2560]{1,0:T(8,128)(2,1)}) custom-call(s32[14]{0:T(128)} %reshape.49.table_ref, f32[32,8]{1,0:T(8,128)} %get-tuple-element.34.dec_ref, bf16[128,512]{1,0:T(8,128)(2,1)} %copy-done.8, f32[128,4096]{1,0:T(8,128)} %get-tuple-element.42.end_ref, ...), custom_call_target="tpu_custom_call", output_to_operand_aliasing={{1}: (4, {})} | custom-call | tf_op jit(solution)/shard_map/pass/pallas_call | solution.py:359
  87.6 2.4 %pass.14 = (bf16[128,512]{1,0:T(8,128)(2,1)}, bf16[128,2560]{1,0:T(8,128)(2,1)}) custom-call(s32[14]{0:T(128)} %reshape.49.table_ref, f32[32,8]{1,0:T(8,128)} %get-tuple-element.34.dec_ref, bf16[128,512]{1,0:T(8,128)(2,1)} %copy-done, f32[128,4096]{1,0:T(8,128)} %get-tuple-element.42.end_ref, ...), custom_call_target="tpu_custom_call", output_to_operand_aliasing={{1}: (4, {})} | custom-call | tf_op jit(solution)/shard_map/pass/pallas_call | solution.py:359
  90.7 11.9 %intra.1.y_ref = bf16[512,4096]{1,0:T(8,128)(2,1)} custom-call(f32[32]{0:T(128)} %skip_ref.1, bf16[512,4096]{1,0:T(8,128)(2,1)} %get-tuple-element.37.mx_ref, bf16[3,128,4096]{2,1,0:T(8,128)(2,1)} %get-tuple-element.38.enter_ref, bf16[512,256]{1,0:T(8,128)(2,1)} %get-tuple-element.39.c_ref, f32[512,256]{1,0:T(8,128)} %get-tuple-element.40.score_ref, ...), custom_call_target="tpu_custom_call" | custom-call | flops 1073741824 | bytes 16777216 | tf_op jit(solution)/shard_map/intra/pallas_call | solution.py:325
  103.2 2.3 %keep.3.held1_ref = bf16[128,2560]{1,0:T(8,128)(2,1)} custom-call(s32[14]{0:T(128)} %reshape.49.table_ref, bf16[128,512]{1,0:T(8,128)(2,1)} %copy-done.10, bf16[128,2560]{1,0:T(8,128)(2,1)} %get-tuple-element.62.held_ref), custom_call_target="tpu_custom_call", output_to_operand_aliasing={{}: (2, {})} | custom-call | tf_op jit(solution)/shard_map/keep/pallas_call | solution.py:346
  106.2 2.2 %keep.2.held0_ref = bf16[128,2560]{1,0:T(8,128)(2,1)} custom-call(s32[14]{0:T(128)} %reshape.49.table_ref, bf16[128,512]{1,0:T(8,128)(2,1)} %copy-done.11, bf16[128,2560]{1,0:T(8,128)(2,1)} %get-tuple-element.52.held_ref), custom_call_target="tpu_custom_call", output_to_operand_aliasing={{}: (2, {})} | custom-call | tf_op jit(solution)/shard_map/keep/pallas_call | solution.py:346
  108.4 10.2 %final.1 = bf16[512,4096]{1,0:T(8,128)(2,1)} custom-call(bf16[512,4096]{1,0:T(8,128)(2,1)} %intra.1.y_ref, bf16[512,256]{1,0:T(8,128)(2,1)} %get-tuple-element.39.c_ref, f32[512,128]{1,0:T(8,128)} %get-tuple-element.36.cols_ref, bf16[128,2560]{1,0:T(8,128)(2,1)} %keep.2.held0_ref, bf16[128,2560]{1,0:T(8,128)(2,1)} %keep.3.held1_ref), custom_call_target="tpu_custom_call" | custom-call | tf_op jit(solution)/shard_map/final/pallas_call | solution.py:381
  (61 shorter events, 26.5 us)
Async XLA Ops:
  1.6 14.0 %collective-permute-start = (bf16[8,4608]{1,0:T(8,128)(2,1)S(1)}, bf16[8,4608]{1,0:T(8,128)(2,1)S(1)}, u32[]{:S(2)}, u32[]{:S(2)}) collective-permute-start(bf16[8,4608]{1,0:T(8,128)(2,1)S(1)} %pad_maximum_fusion), channel_id=1, source_target_pairs={{0,4},{4,8},{8,12},{12,0},{1,5},{5,9},{9,13},{13,1},{2,6},{6,10},{... | collective-permute-start | bytes 221192 | tf_op jit(solution)/shard_map/ppermute | solution.py:242
  33.8 7.0 %collective-permute-start.7 = (bf16[128,512]{1,0:T(8,128)(2,1)}, bf16[128,512]{1,0:T(8,128)(2,1)S(1)}, u32[]{:S(2)}, u32[]{:S(2)}) collective-permute-start(bf16[128,512]{1,0:T(8,128)(2,1)} %start.3), channel_id=1, source_target_pairs={{0,4},{4,8},{8,12},{12,0},{1,5},{5,9},{9,13},{13,1},{2,6},{6,10},{... | collective-permute-start | bytes 393224 | tf_op jit(solution)/shard_map/ppermute | solution.py:323
  37.7 7.0 %collective-permute-start.1 = (bf16[128,512]{1,0:T(8,128)(2,1)}, bf16[128,512]{1,0:T(8,128)(2,1)S(1)}, u32[]{:S(2)}, u32[]{:S(2)}) collective-permute-start(bf16[128,512]{1,0:T(8,128)(2,1)} %start.2), channel_id=1, source_target_pairs={{0,4},{4,8},{8,12},{12,0},{1,5},{5,9},{9,13},{13,1},{2,6},{6,10},{... | collective-permute-start | bytes 393224 | tf_op jit(solution)/shard_map/ppermute | solution.py:323
  40.8 0.9 copy-start.9
  44.2 7.4 %collective-permute-start.8 = (bf16[128,512]{1,0:T(8,128)(2,1)}, bf16[128,512]{1,0:T(8,128)(2,1)S(1)}, u32[]{:S(2)}, u32[]{:S(2)}) collective-permute-start(bf16[128,512]{1,0:T(8,128)(2,1)} %get-tuple-element.53), channel_id=1, source_target_pairs={{0,4},{4,8},{8,12},{12,0},{1,5},{5,9},{9,13},{13,1},{2,6},{6,10},{... | collective-permute-start | bytes 393224 | tf_op jit(solution)/shard_map/ppermute | solution.py:379
  44.6 0.9 copy-start.2
  48.0 7.0 %collective-permute-start.2 = (bf16[128,512]{1,0:T(8,128)(2,1)}, bf16[128,512]{1,0:T(8,128)(2,1)S(1)}, u32[]{:S(2)}, u32[]{:S(2)}) collective-permute-start(bf16[128,512]{1,0:T(8,128)(2,1)} %get-tuple-element.43), channel_id=1, source_target_pairs={{0,4},{4,8},{8,12},{12,0},{1,5},{5,9},{9,13},{13,1},{2,6},{6,10},{... | collective-permute-start | bytes 393224 | tf_op jit(solution)/shard_map/ppermute | solution.py:379
  51.5 0.6 copy-start.1
  54.6 8.2 %collective-permute-start.9 = (bf16[128,512]{1,0:T(8,128)(2,1)}, bf16[128,512]{1,0:T(8,128)(2,1)S(1)}, u32[]{:S(2)}, u32[]{:S(2)}) collective-permute-start(bf16[128,512]{1,0:T(8,128)(2,1)} %get-tuple-element.55), channel_id=1, source_target_pairs={{0,4},{4,8},{8,12},{12,0},{1,5},{5,9},{9,13},{13,1},{2,6},{6,10},{... | collective-permute-start | bytes 393224 | tf_op jit(solution)/shard_map/ppermute | solution.py:379
  55.0 0.6 copy-start.3
  58.1 7.9 %collective-permute-start.3 = (bf16[128,512]{1,0:T(8,128)(2,1)}, bf16[128,512]{1,0:T(8,128)(2,1)S(1)}, u32[]{:S(2)}, u32[]{:S(2)}) collective-permute-start(bf16[128,512]{1,0:T(8,128)(2,1)} %get-tuple-element.45), channel_id=1, source_target_pairs={{0,4},{4,8},{8,12},{12,0},{1,5},{5,9},{9,13},{13,1},{2,6},{6,10},{... | collective-permute-start | bytes 393224 | tf_op jit(solution)/shard_map/ppermute | solution.py:379
  62.9 0.7 copy-start.4
  66.0 7.4 %collective-permute-start.10 = (bf16[128,512]{1,0:T(8,128)(2,1)}, bf16[128,512]{1,0:T(8,128)(2,1)S(1)}, u32[]{:S(2)}, u32[]{:S(2)}) collective-permute-start(bf16[128,512]{1,0:T(8,128)(2,1)} %get-tuple-element.57), channel_id=1, source_target_pairs={{0,4},{4,8},{8,12},{12,0},{1,5},{5,9},{9,13},{13,1},{2,6},{6,10},{... | collective-permute-start | bytes 393224 | tf_op jit(solution)/shard_map/ppermute | solution.py:379
  66.0 0.7 copy-start.5
  69.1 7.7 %collective-permute-start.4 = (bf16[128,512]{1,0:T(8,128)(2,1)}, bf16[128,512]{1,0:T(8,128)(2,1)S(1)}, u32[]{:S(2)}, u32[]{:S(2)}) collective-permute-start(bf16[128,512]{1,0:T(8,128)(2,1)} %get-tuple-element.47), channel_id=1, source_target_pairs={{0,4},{4,8},{8,12},{12,0},{1,5},{5,9},{9,13},{13,1},{2,6},{6,10},{... | collective-permute-start | bytes 393224 | tf_op jit(solution)/shard_map/ppermute | solution.py:379
  73.3 0.7 copy-start.6
  76.5 7.0 %collective-permute-start.11 = (bf16[128,512]{1,0:T(8,128)(2,1)}, bf16[128,512]{1,0:T(8,128)(2,1)S(1)}, u32[]{:S(2)}, u32[]{:S(2)}) collective-permute-start(bf16[128,512]{1,0:T(8,128)(2,1)} %get-tuple-element.59), channel_id=1, source_target_pairs={{0,4},{4,8},{8,12},{12,0},{1,5},{5,9},{9,13},{13,1},{2,6},{6,10},{... | collective-permute-start | bytes 393224 | tf_op jit(solution)/shard_map/ppermute | solution.py:379
  76.8 0.7 copy-start.7
  79.9 7.0 %collective-permute-start.5 = (bf16[128,512]{1,0:T(8,128)(2,1)}, bf16[128,512]{1,0:T(8,128)(2,1)S(1)}, u32[]{:S(2)}, u32[]{:S(2)}) collective-permute-start(bf16[128,512]{1,0:T(8,128)(2,1)} %get-tuple-element.49), channel_id=1, source_target_pairs={{0,4},{4,8},{8,12},{12,0},{1,5},{5,9},{9,13},{13,1},{2,6},{6,10},{... | collective-permute-start | bytes 393224 | tf_op jit(solution)/shard_map/ppermute | solution.py:379
  86.5 16.1 %collective-permute-start.12 = (bf16[128,512]{1,0:T(8,128)(2,1)}, bf16[128,512]{1,0:T(8,128)(2,1)S(1)}, u32[]{:S(2)}, u32[]{:S(2)}) collective-permute-start(bf16[128,512]{1,0:T(8,128)(2,1)} %get-tuple-element.61), channel_id=1, source_target_pairs={{0,4},{4,8},{8,12},{12,0},{1,5},{5,9},{9,13},{13,1},{2,6},{6,10},{... | collective-permute-start | bytes 393224 | tf_op jit(solution)/shard_map/ppermute | solution.py:379
  86.9 0.6 copy-start
  90.0 15.5 %collective-permute-start.6 = (bf16[128,512]{1,0:T(8,128)(2,1)}, bf16[128,512]{1,0:T(8,128)(2,1)S(1)}, u32[]{:S(2)}, u32[]{:S(2)}) collective-permute-start(bf16[128,512]{1,0:T(8,128)(2,1)} %get-tuple-element.51), channel_id=1, source_target_pairs={{0,4},{4,8},{8,12},{12,0},{1,5},{5,9},{9,13},{13,1},{2,6},{6,10},{... | collective-permute-start | bytes 393224 | tf_op jit(solution)/shard_map/ppermute | solution.py:379
  102.6 0.7 copy-start.10
  105.5 0.7 copy-start.11
  (1 other events, 0.6 us)

commit v2 on v0

v2 whole, which is shorter than its diff:
```python
import functools
import math

import jax
import jax.numpy as jnp
from jax import lax
from jax.experimental import pallas as pl
from jax.experimental.pallas import tpu as pltpu
from jax.sharding import PartitionSpec as P

D = 128
Q = 128
BLK = 512
NQ = BLK // Q
HC = 4
CW = HC * D
RIM = 8
LOG2E = math.log2(math.e)
F32 = jnp.float32
BF16 = jnp.bfloat16


def doc_of(pos, starts_ref):
    count = jnp.zeros_like(pos)
    for j in range(starts_ref.shape[0]):
        count = count + (pos >= starts_ref[j]).astype(jnp.int32)
    return count - 1


def silu_half(u):
    return u + u * jnp.tanh(u)


def doc_at(pos, starts_ref):
    count = jnp.int32(-1)
    for j in range(starts_ref.shape[0]):
        count = count + (pos >= starts_ref[j]).astype(jnp.int32)
    return count


def column_of(ref):
    heads = ref.shape[0]
    index = lax.broadcasted_iota(jnp.int32, (heads, 1), 0)
    column = jnp.zeros((heads, 1), F32)
    for h in range(heads):
        column = jnp.where(index == h, ref[h], column)
    return column


def split(value, parts):
    pieces = []
    for _ in range(parts - 1):
        piece = value.astype(BF16).astype(F32)
        pieces.append(piece)
        value = value - piece
    return pieces + [value]


def doc_at(pos, starts_ref):
    count = jnp.int32(-1)
    for j in range(starts_ref.shape[0]):
        count = count + (pos >= starts_ref[j]).astype(jnp.int32)
    return count


def column_of(ref):
    heads = ref.shape[0]
    index = lax.broadcasted_iota(jnp.int32, (heads, 1), 0)
    column = jnp.zeros((heads, 1), F32)
    for h in range(heads):
        column = jnp.where(index == h, ref[h], column)
    return column


def split(value, parts):
    pieces = []
    for _ in range(parts - 1):
        piece = value.astype(BF16).astype(F32)
        pieces.append(piece)
        value = value - piece
    return pieces + [value]


def doc_at(pos, starts_ref):
    count = jnp.int32(-1)
    for j in range(starts_ref.shape[0]):
        count = count + (pos >= starts_ref[j]).astype(jnp.int32)
    return count


def column_of(ref):
    heads = ref.shape[0]
    index = lax.broadcasted_iota(jnp.int32, (heads, 1), 0)
    column = jnp.zeros((heads, 1), F32)
    for h in range(heads):
        column = jnp.where(index == h, ref[h], column)
    return column


def split(value, parts):
    pieces = []
    for _ in range(parts - 1):
        piece = value.astype(BF16).astype(F32)
        pieces.append(piece)
        value = value - piece
    return pieces + [value]


def params_kernel(
    place_ref, starts_ref, bias_ref, alog_ref, skip_ref, dt_ref, scale_ref, cum_ref, rows_ref, dec_ref, shift_ref
):
    first = place_ref[0] * BLK
    heads = dt_ref.shape[0]
    v = dt_ref[...] + column_of(bias_ref)
    step = jnp.maximum(v, 0.0) + jnp.log(1.0 + jnp.exp(-jnp.abs(v)))
    rate = -jnp.exp(column_of(alog_ref)) * step
    tri = (
        lax.broadcasted_iota(jnp.int32, (Q, Q), 0) <= lax.broadcasted_iota(jnp.int32, (Q, Q), 1)
    ).astype(F32)
    doc_before = doc_at(first - 1, starts_ref)
    base = jnp.zeros((heads, 1), F32)
    dec_ref[...] = jnp.zeros_like(dec_ref)
    dec_ref[:, 2 * NQ : 2 * NQ + 1] = column_of(skip_ref)
    for q in range(NQ):
        span = slice(q * Q, (q + 1) * Q)
        cum = jnp.dot(rate[:, span], tri, precision=lax.Precision.HIGHEST, preferred_element_type=F32)
        last = cum[:, Q - 1 : Q]
        step_q = step[:, span]
        pos = first + q * Q + lax.broadcasted_iota(jnp.int32, (1, Q), 1)
        doc = doc_of(pos, starts_ref)
        doc_prev = doc_at(first + q * Q - 1, starts_ref)
        doc_end = doc_at(first + (q + 1) * Q - 1, starts_ref)
        tail = jnp.where(doc == doc_end, jnp.exp(last - cum) * step_q, 0.0)
        entry = jnp.where(doc == doc_prev, jnp.exp(cum), 0.0)
        packed = split(tail, 2) + split(entry, 2)
        if 4 * heads < D:
            packed.append(jnp.zeros((D - 4 * heads, Q), F32))
        scale_ref[span, :] = jnp.transpose(jnp.concatenate(packed, axis=0), (1, 0)).astype(BF16)
        packed = split(cum * LOG2E, 3) + [jnp.zeros((D - 3 * heads, Q), F32)]
        cum_ref[span, :] = jnp.transpose(jnp.concatenate(packed, axis=0), (1, 0)).astype(BF16)
        rows_ref[:, span] = (cum - jnp.log(step_q)) * LOG2E
        dec_ref[:, q : q + 1] = jnp.exp(last) * jnp.where(doc_end == doc_prev, 1.0, 0.0)
        if q:
            dec_ref[:, NQ + q : NQ + q + 1] = jnp.exp(base) * jnp.where(doc_prev == doc_before, 1.0, 0.0)
        base = base + last
    doc_last = doc_at(first + BLK - 1, starts_ref)
    dec_ref[:, NQ : NQ + 1] = jnp.exp(base) * jnp.where(doc_last == doc_before, 1.0, 0.0)
    for q in range(NQ):
        row = lax.broadcasted_iota(jnp.int32, (Q, 2 * Q), 0)
        col = lax.broadcasted_iota(jnp.int32, (Q, 2 * Q), 1) - Q
        at = first + q * Q
        same = doc_of(at + row, starts_ref) == doc_of(at + col, starts_ref)
        for k in range(3):
            hit = same & (col == row - (3 - k))
            shift_ref[q, k * Q : (k + 1) * Q, :] = jnp.where(hit, 1.0, 0.0).astype(BF16)


def chooser(heads, chunk, lo, hi, width):
    k = lax.broadcasted_iota(jnp.int32, (D, width), 0)
    head = HC * chunk + lax.broadcasted_iota(jnp.int32, (D, width), 1) // D
    hit = ((k & (heads - 1)) == head) & (k >= lo * heads) & (k < hi * heads)
    return jnp.where(hit, 1.0, 0.0).astype(BF16)


def convolved(q, window, now, shift_ref, taps, bias):
    moved = jnp.dot(shift_ref[q], window, preferred_element_type=F32)
    total = (0.5 * taps[3]) * now.astype(F32) + 0.5 * bias
    for k in range(3):
        total = total + (0.5 * taps[k]) * moved[k * Q : (k + 1) * Q]
    return silu_half(total)


def window_of(q, edge_ref, x_ref):
    return edge_ref[...] if q == 0 else x_ref[(q - 1) * Q : (q + 1) * Q, :]


def edge(edge_ref, rim_ref, x_ref):
    width = x_ref.shape[1]
    rim = jnp.concatenate([jnp.zeros((Q - RIM, width), F32), rim_ref[...].astype(F32)], axis=0)
    edge_ref[0:Q, 0:width] = rim.astype(BF16)
    edge_ref[Q : 2 * Q, 0:width] = x_ref[0:Q, :]


def state_body(
    chunk, per_group, dec_ref, x_ref, rim_ref, wx_ref, bx_ref, shift_ref, scale_ref, bt_ref,
    mx_ref, enter_ref, end_ref, edge_ref, send_ref=None,
):
    heads = dec_ref.shape[0]
    edge(edge_ref, rim_ref, x_ref)
    pick = chooser(heads, chunk, 0, 2, CW)
    g = lax.div(chunk, per_group)
    taps = [wx_ref[k : k + 1, :] for k in range(4)]
    state = None
    for q in range(NQ):
        span = slice(q * Q, (q + 1) * Q)
        mixed = convolved(q, window_of(q, edge_ref, x_ref), x_ref[span, :], shift_ref, taps, bx_ref[...])
        mx_ref[span, :] = mixed.astype(BF16)
        scale = jnp.dot(scale_ref[span, :], pick, preferred_element_type=F32)
        part = jnp.dot(bt_ref[g, :, span], (mixed * scale).astype(BF16), preferred_element_type=F32)
        for i in range(HC):
            lanes = slice(i * D, (i + 1) * D)
            if q == 0:
                end_ref[0, :, lanes] = part[:, lanes]
            else:
                before = end_ref[0, :, lanes]
                enter_ref[q - 1, :, lanes] = before.astype(BF16)
                end_ref[0, :, lanes] = dec_ref[chunk * HC + i, q] * before + part[:, lanes]
    if send_ref is not None:
        send_ref[...] = end_ref[0].astype(BF16)


def first_kernel(
    place_ref, starts_ref, dec_ref, x_ref, rim_ref, wx_ref, bx_ref, shift_ref, scale_ref,
    bc_ref, rimbc_ref, wbc_ref, bbc_ref,
    mx_ref, enter_ref, end_ref, send_ref, bt_ref, c_ref, score_ref,
    edge_ref, *, per_group,
):
    groups = bt_ref.shape[0]
    wide = 2 * groups * D
    edge(edge_ref, rimbc_ref, bc_ref)

    def joined(rows):
        return jnp.concatenate(rows, axis=1)

    taps = [joined([wbc_ref[k, p : p + 1, :] for p in range(2)]) for k in range(4)]
    bias = joined([bbc_ref[p : p + 1, :] for p in range(2)])
    for q in range(NQ):
        span = slice(q * Q, (q + 1) * Q)
        window = edge_ref[:, 0:wide] if q == 0 else bc_ref[(q - 1) * Q : (q + 1) * Q, :]
        mixed = convolved(q, window, bc_ref[span, :], shift_ref, taps, bias)
        c_ref[span, :] = mixed[:, groups * D :].astype(BF16)
        at = place_ref[0] * BLK + q * Q
        row = at + lax.broadcasted_iota(jnp.int32, (Q, Q), 0)
        col = at + lax.broadcasted_iota(jnp.int32, (Q, Q), 1)
        keep = (row >= col) & (doc_of(row, starts_ref) == doc_of(col, starts_ref))
        for g in range(groups):
            lanes = slice(g * D, (g + 1) * D)
            bt = jnp.transpose(mixed[:, lanes], (1, 0)).astype(BF16)
            bt_ref[g, :, span] = bt
            score = jnp.dot(c_ref[span, lanes], bt, preferred_element_type=F32)
            score_ref[span, lanes] = jnp.where(keep, score, 0.0)
    state_body(
        0, per_group, dec_ref, x_ref, rim_ref, wx_ref, bx_ref, shift_ref, scale_ref, bt_ref,
        mx_ref, enter_ref, end_ref, edge_ref, send_ref,
    )


def more_kernel(
    dec_ref, x_ref, rim_ref, wx_ref, bx_ref, shift_ref, scale_ref, bt_ref, old1, old2, old3,
    mx_ref, enter_ref, end_ref, *rest, per_group, chunk_of, sends,
):
    send_ref, edge_ref = rest if sends else (None, rest[0])
    state_body(
        chunk_of(pl.program_id(0)), per_group, dec_ref, x_ref, rim_ref, wx_ref, bx_ref, shift_ref, scale_ref,
        bt_ref, mx_ref, enter_ref, end_ref, edge_ref, send_ref,
    )


def join_kernel(place_ref, dec_ref, recv_ref, end_ref, token_ref, send_ref, *, turn, stream, per_stream):
    chunk = stream * per_stream + jnp.clip(turn - place_ref[0], 0, per_stream - 1)
    for i in range(HC):
        lanes = slice(i * D, (i + 1) * D)
        fade = dec_ref[chunk * HC + i, NQ]
        send_ref[:, lanes] = (fade * recv_ref[:, lanes].astype(F32) + end_ref[0, :, lanes]).astype(BF16)


def out_kernel(
    place_ref, dec_ref, mx_ref, enter_ref, c_ref, score_ref, scale_ref, cum_ref, rows_ref, recv_ref,
    *rest, turn, stream, per_stream,
):
    out_ref, token_ref = rest[-2:]
    token_ref[...] = jnp.zeros_like(token_ref)
    heads = rows_ref.shape[0]
    rank = turn - place_ref[0]
    chunk = stream * per_stream + jnp.clip(rank, 0, per_stream - 1)

    @pl.when((rank >= 0) & (rank < per_stream))
    def compute():
        pick_cum = chooser(heads, chunk, 0, 3, CW)
        pick_entry = chooser(heads, chunk, 2, 4, CW)
        for q in range(NQ):
            span = slice(q * Q, (q + 1) * Q)
            both = rows_ref[pl.ds(pl.multiple_of(2 * HC * lax.div(chunk, 2), 2 * HC), 2 * HC), span]
            terms = jnp.where(lax.rem(chunk, 2) == 0, both[:HC], both[HC:])
            cums = jnp.dot(cum_ref[span, :], pick_cum, preferred_element_type=F32)
            entry = jnp.dot(scale_ref[span, :], pick_entry, preferred_element_type=F32)
            if q:
                parts = []
                for i in range(HC):
                    lanes = slice(i * D, (i + 1) * D)
                    reach = dec_ref[chunk * HC + i, NQ + q]
                    parts.append(
                        (enter_ref[q - 1, :, lanes].astype(F32) + reach * recv_ref[:, lanes].astype(F32)).astype(BF16)
                    )
                state = jnp.concatenate(parts, axis=1)
            else:
                state = recv_ref[...]
            far = jnp.dot(c_ref[span, :], state, preferred_element_type=F32)
            score = score_ref[span, :]
            for i in range(HC):
                lanes = slice(i * D, (i + 1) * D)
                gap = cums[:, lanes] - terms[i : i + 1]
                weight = (score * jnp.exp2(jnp.minimum(gap, 100.0))).astype(BF16)
                x = mx_ref[span, lanes]
                y = jnp.dot(weight, x, preferred_element_type=F32)
                y = y + entry[:, lanes] * far[:, lanes] + dec_ref[chunk * HC + i, 2 * NQ] * x.astype(F32)
                out_ref[span, lanes] = y.astype(BF16)

    if turn >= per_stream:
        @pl.when(rank >= per_stream)
        def again():
            out_ref[...] = rest[0][...]


SMEM = pl.BlockSpec(memory_space=pltpu.SMEM)
ROOM = pltpu.CompilerParams(vmem_limit_bytes=16 * 2**20)
ANY = pl.BlockSpec(memory_space=pl.ANY)


def whole(shape):
    return pl.BlockSpec(shape, lambda *_: (0,) * len(shape))


def shape_of(shape, dtype):
    return jax.ShapeDtypeStruct(shape, dtype)


def per_device(
    x_raw, bc_raw, dt_raw, dt_bias, a_log, d_skip, conv_x, conv_x_bias, conv_bc, conv_bc_bias, doc_starts
):
    rows, width = x_raw.shape
    held = [x_raw, dt_raw, dt_bias, a_log, d_skip, conv_x, conv_bc, conv_bc_bias, doc_starts]
    held = [pltpu.with_memory_space_constraint(a, pltpu.HBM) for a in held]
    x_pin, dt_raw, dt_bias, a_log, d_skip, conv_x, conv_bc, conv_bc_bias, doc_starts = held
    groups = bc_raw.shape[2] // D
    heads = dt_raw.shape[0]
    chunks = heads // HC
    per_group = chunks // groups
    wide = 2 * groups * D
    seq = lax.axis_size("seq")
    place = lax.axis_index("seq").astype(jnp.int32)
    place_row = place.reshape(1)
    ring = [(i, (i + 1) % seq) for i in range(seq)]
    streams = 2
    per_stream = chunks // streams
    slots = per_stream + seq - 2

    tail = jnp.concatenate([x_raw[rows - RIM :], bc_raw[rows - RIM :].reshape(RIM, -1)], axis=1)
    rim = lax.ppermute(tail, "seq", ring)
    bc = bc_raw.reshape(rows, -1)
    bias_x = pltpu.with_memory_space_constraint(conv_x_bias[None], pltpu.HBM)

    scale, cums, row_terms, dec, shift = pl.pallas_call(
        params_kernel,
        in_specs=[SMEM] * 5 + [pl.BlockSpec(memory_space=pltpu.VMEM)],
        out_specs=[pl.BlockSpec(memory_space=pltpu.VMEM)] * 5,
        out_shape=[
            shape_of((BLK, D), BF16),
            shape_of((BLK, D), BF16),
            shape_of((heads, BLK), F32),
            shape_of((heads, 16), F32),
            shape_of((NQ, 3 * Q, 2 * Q), BF16),
        ],
        compiler_params=ROOM,
        name="params",
    )(place_row, doc_starts, dt_bias, a_log, d_skip, dt_raw)

    def chunk_specs(chunk_of):
        ins = [
            pl.BlockSpec((BLK, CW), lambda i: (0, chunk_of(i))),
            pl.BlockSpec((RIM, CW), lambda i: (0, chunk_of(i))),
            pl.BlockSpec((4, CW), lambda i: (0, chunk_of(i))),
            pl.BlockSpec((1, CW), lambda i: (0, chunk_of(i))),
            whole((NQ, 3 * Q, 2 * Q)),
            whole((BLK, D)),
        ]
        outs = [
            pl.BlockSpec((BLK, CW), lambda i: (0, chunk_of(i))),
            pl.BlockSpec((NQ - 1, D, CW), lambda i: (0, 0, chunk_of(i))),
            pl.BlockSpec((1, D, CW), lambda i: (chunk_of(i), 0, 0)),
        ]
        return ins, outs

    big = [
        shape_of((BLK, width), BF16),
        shape_of((NQ - 1, D, width), BF16),
        shape_of((chunks, D, CW), F32),
    ]
    chunk_shape = shape_of((D, CW), BF16)
    edge_scratch = [pltpu.VMEM((2 * Q, CW), BF16)]
    ins, outs = chunk_specs(lambda i: 0)
    mixed_x, enter, end, send_a, bt, mixed_c, score = pl.pallas_call(
        functools.partial(first_kernel, per_group=per_group),
        grid=(1,),
        in_specs=[
            SMEM, SMEM, SMEM, *ins,
            whole((BLK, wide)),
            pl.BlockSpec((RIM, wide), lambda i: (0, width // wide)),
            whole((4, 2, groups * D)),
            whole((2, groups * D)),
        ],
        out_specs=[
            *outs,
            whole((D, CW)),
            whole((groups, D, BLK)),
            whole((BLK, groups * D)),
            whole((BLK, groups * D)),
        ],
        out_shape=[
            *big,
            chunk_shape,
            shape_of((groups, D, BLK), BF16),
            shape_of((BLK, groups * D), BF16),
            shape_of((BLK, groups * D), F32),
        ],
        scratch_shapes=edge_scratch,
        compiler_params=ROOM,
        name="first",
    )(
        place_row, doc_starts, dec, x_pin, rim, conv_x, bias_x, shift, scale,
        bc, rim, conv_bc, conv_bc_bias,
    )

    def more(count, chunk_of, sends, mixed_x, enter, end):
        ins, outs = chunk_specs(chunk_of)
        return pl.pallas_call(
            functools.partial(more_kernel, per_group=per_group, chunk_of=chunk_of, sends=sends),
            grid=(count,),
            in_specs=[SMEM, *ins, whole((groups, D, BLK)), ANY, ANY, ANY],
            out_specs=outs + [whole((D, CW))] * sends,
            out_shape=big + [chunk_shape] * sends,
            input_output_aliases={8: 0, 9: 1, 10: 2},
            scratch_shapes=edge_scratch,
            cost_estimate=pl.CostEstimate(
                flops=4 * count * BLK * D * CW, bytes_accessed=4 * count * BLK * CW, transcendentals=0
            ),
            compiler_params=ROOM,
        name="more",
        )(dec, x_pin, rim, conv_x, bias_x, shift, scale, bt, mixed_x, enter, end)

    flying = [lax.ppermute(send_a, "seq", ring), None]
    mixed_x, enter, end, send_b = more(1, lambda i: per_stream, 1, mixed_x, enter, end)
    flying[1] = lax.ppermute(send_b, "seq", ring)
    rest = (per_stream - 1) * streams
    mixed_x, enter, end = more(
        rest, lambda i: 1 + i // 2 + (i % 2) * per_stream, 0, mixed_x, enter, end
    )

    def join(turn, s, recv, token):
        def chunk(at):
            return s * per_stream + jnp.clip(turn - at[0], 0, per_stream - 1)

        return pl.pallas_call(
            functools.partial(join_kernel, turn=turn, stream=s, per_stream=per_stream),
            grid_spec=pltpu.PrefetchScalarGridSpec(
                num_scalar_prefetch=1,
                grid=(1,),
                in_specs=[
                    SMEM,
                    whole((D, CW)),
                    pl.BlockSpec((1, D, CW), lambda i, at: (chunk(at), 0, 0)),
                    whole((8, D)),
                ],
                out_specs=whole((D, CW)),
            ),
            out_shape=chunk_shape,
            compiler_params=ROOM,
            name="join",
        )(place_row, dec, recv, end, token)

    def output(turn, s, recv, out):
        def chunk(place_ref):
            return s * per_stream + jnp.clip(turn - place_ref[0], 0, per_stream - 1)

        block = pl.BlockSpec((BLK, CW), lambda i, at: (0, chunk(at)))
        old = [] if out is None else [out]
        return pl.pallas_call(
            functools.partial(out_kernel, turn=turn, stream=s, per_stream=per_stream),
            grid_spec=pltpu.PrefetchScalarGridSpec(
                num_scalar_prefetch=1,
                grid=(1,),
                in_specs=[
                    SMEM,
                    block,
                    pl.BlockSpec((NQ - 1, D, CW), lambda i, at: (0, 0, chunk(at))),
                    pl.BlockSpec((BLK, D), lambda i, at: (0, chunk(at) // per_group)),
                    pl.BlockSpec((BLK, D), lambda i, at: (0, chunk(at) // per_group)),
                    whole((BLK, D)),
                    whole((BLK, D)),
                    whole((heads, BLK)),
                    whole((D, CW)),
                ]
                + [block if turn >= per_stream else ANY] * len(old),
                out_specs=[block, whole((8, D))],
            ),
            out_shape=[shape_of((BLK, width), BF16), shape_of((8, D), F32)],
            input_output_aliases={10: 0} if old else {},
            cost_estimate=pl.CostEstimate(
                flops=8 * BLK * Q * CW, bytes_accessed=6 * BLK * CW, transcendentals=0
            ),
            compiler_params=ROOM,
        name="out",
        )(place_row, dec, mixed_x, enter, mixed_c, score, scale, cums, row_terms, recv, *old)

    out, token = None, None
    carried = [send_a, send_b]
    for turn in range(slots + 1):
        for s in range(streams):
            if turn:
                recv = flying[s]
                if turn < slots:
                    flying[s] = lax.ppermute(join(turn, s, recv, token), "seq", ring)
                carried[s] = recv
            out, token = output(turn, s, carried[s], out)
    return out


def solution(mesh):
    return jax.shard_map(
        per_device,
        mesh=mesh,
        in_specs=(
            P(("groups", "seq"), ("head", "sub")),
            P(("groups", "seq"), None, ("head", "sub")),
            P(("head", "sub"), ("groups", "seq")),
            P(("head", "sub")),
            P(("head", "sub")),
            P(("head", "sub")),
            P(None, ("head", "sub")),
            P(("head", "sub")),
            P(None, None, ("head", "sub")),
            P(None, ("head", "sub")),
            P("groups"),
        ),
        out_specs=P(("groups", "seq"), ("head", "sub")),
        check_vma=False,
    )
```

time: 279 us -> 83.7 us (0.30)
  waiting for transfers between devices: 132 us -> 3.82 us
  Pallas kernels: 0 us -> 59.5 us
  matrix products: 40.8 us -> 0 us
  local copies, waits for them, and re-layouts: 36.5 us -> 2.68 us
  other arithmetic: 30 us -> 0.01 us
  between operations: 15 us -> 0.15 us
  starting transfers between devices: 4.93 us -> 16.9 us
  blocking collectives: 9.14 us -> 0 us
  loops' own time: 7.88 us -> 0 us
    all_gather x1 -> x0, waiting for transfers between devices: 132 us -> none  [carried_in_2(): gathered = jax.tree.map(lambda a: lax.all_gather(a, axis), part)]
    pallas_call x0 -> x28, Pallas kernels: none -> 59.5 us  [the longest x14 32.6 us: output(): pl.pallas_call(functools.partial(out_kernel, turn=turn, stream=s, per_str...]
    dot_general x10 -> x0, matrix products: 40.8 us -> none  [the longest x4 20.1 us: one_slice(): jnp.einsum('gits,sgip->tgip', weights, x_part, preferred_element_type=jnp...]
    convert_element_type x3 -> x0, other arithmetic: 17.3 us -> none  [the longest x1 15.2 us: per_device(): mixed_x = convolve(jnp.concatenate([rim_x, x_raw], axis=0), conv_x, conv_...]
    ppermute x1 -> x13, starting transfers between devices: 4.93 us -> 16.9 us  [the longest x10 12.1 us: per_device(): flying[s] = lax.ppermute(join(turn, s, recv, token), 'seq', ring)]
    all_gather x1 -> x0, blocking collectives: 9.14 us -> none  [carried_in_2(): gathered = jax.tree.map(lambda a: lax.all_gather(a, axis), part)]
    transpose x1 -> x0, local copies, waits for them, and re-layouts: 8.9 us -> none  [block_terms(): jnp.transpose(inner_parts, (1, 2, 0, 3, 4))]
    another operation x2 -> x0, loops' own time: 7.88 us -> none  [the longest x1 7.87 us: block_terms(): inner_parts, state_parts = lax.map(one_slice, starts)]
  transfers between devices with their start and end apart: 2 -> 13, of which waited for: 1 -> 4; matrix products, arithmetic and copies ran while one was open for 8% -> 1% of each run, Pallas kernels for 0% -> 64%
where the time goes in v2:
time: 83.7 us; the launch traced here: 83 us
  Pallas kernels  59.5 us (71%)
  starting transfers between devices  16.9 us (20%)
  waiting for transfers between devices  3.82 us (5%)
  local copies, waits for them, and re-layouts  2.68 us (3%)
    pallas_call x14, Pallas kernels, output(): pl.pallas_call(functools.partial(out_kernel, turn=turn, stream=s, per_str...  32.6 us
    pallas_call x2, Pallas kernels, more(): pl.pallas_call(functools.partial(more_kernel, per_group=per_group, chunk_...  12.9 us
    ppermute x10, starting transfers between devices, per_device(): flying[s] = lax.ppermute(join(turn, s, recv, token), 'seq', ring)  12.1 us
    pallas_call x10, Pallas kernels, join(): pl.pallas_call(functools.partial(join_kernel, turn=turn, stream=s, per_st...  8.45 us
    pallas_call x1, Pallas kernels, per_device(): pl.pallas_call(functools.partial(first_kernel, per_group=per_group), grid...  4.02 us
    ppermute x1, starting transfers between devices, per_device(): rim = lax.ppermute(tail, 'seq', ring)  3.08 us
    ppermute x10, waiting for transfers between devices, per_device(): flying[s] = lax.ppermute(join(turn, s, recv, token), 'seq', ring)  2.16 us
    unnamed x3, local copies, waits for them, and re-layouts  1.83 us
  transfers between devices with their start and end apart: 13, of which 4 were waited for; matrix products, arithmetic and copies ran while one was open for 1% of the time, Pallas kernels for 64%

profile of v2, /device:TPU:0, one launch (start us, length us, event | category | flops | bytes accessed | tf_op | source)
XLA Modules:
  0.0 83.0 jit_solution(5262134817246871368)
XLA Ops:
  1.6 3.1 %collective-permute-start = (bf16[8,4608]{1,0:T(8,128)(2,1)S(1)}, bf16[8,4608]{1,0:T(8,128)(2,1)S(1)}, u32[]{:S(2)}, u32[]{:S(2)}) collective-permute-start(bf16[8,4608]{1,0:T(8,128)(2,1)S(1)} %pad_maximum_fusion), channel_id=1, source_target_pairs={{0,4},{4,8},{8,12},{12,0},{1,5},{5,9},{9,13},{13,1},{2,6},{6,10},{... | collective-permute-start | bytes 221192 | tf_op jit(solution)/shard_map/ppermute | solution.py:349
  5.8 1.6 %params.1 = (bf16[512,128]{1,0:T(8,128)(2,1)S(1)}, bf16[512,128]{1,0:T(8,128)(2,1)S(1)}, f32[32,512]{1,0:T(8,128)S(1)}, f32[32,16]{1,0:T(8,128)S(1)}, bf16[4,384,256]{2,1,0:T(8,128)(2,1)S(1)}) custom-call(s32[1]{0:T(128)} %bitcast.place_ref, s32[4]{0:T(128)} %starts_ref.3, f32[32]{0:T(128)} %bias_ref.1, f32[32]{0:T(128)} %alog_ref.1, f32[32]{0:T(128)} %skip_ref.1, ...), custom_call_target="tpu_custom_call" | custom-call | tf_op jit(solution)/shard_map/params/pallas_call | solution.py:353
  7.3 1.7 %collective-permute-done.rim_ref.rimbc_ref = bf16[8,4608]{1,0:T(8,128)(2,1)S(1)} collective-permute-done((bf16[8,4608]{1,0:T(8,128)(2,1)S(1)}, bf16[8,4608]{1,0:T(8,128)(2,1)S(1)}, u32[]{:S(2)}, u32[]{:S(2)}) %collective-permute-start) | collective-permute-done | bytes 73760 | tf_op jit(solution)/shard_map/ppermute | solution.py:349
  9.0 4.0 %first.1 = (bf16[512,4096]{1,0:T(8,128)(2,1)S(1)}, bf16[3,128,4096]{2,1,0:T(8,128)(2,1)S(1)}, f32[8,128,512]{2,1,0:T(8,128)S(1)}, bf16[128,512]{1,0:T(8,128)(2,1...) custom-call(s32[1]{0:T(128)} %bitcast.place_ref, s32[4]{0:T(128)} %starts_ref.3, ...), custom_call_target="tpu_custom_call" | custom-call | tf_op jit(solution)/shard_map/first/pallas_call | solution.py:392
  13.1 2.5 %more.2 = (bf16[512,4096]{1,0:T(8,128)(2,1)S(1)}, bf16[3,128,4096]{2,1,0:T(8,128)(2,1)S(1)}, f32[8,128,512]{2,1,0:T(8,128)S(1)}, bf16[128,512]{1,0:T(8,128)(2,1)S(1)}) custom-call(f32[32,16]{1,0:T(8,128)S(1)} %get-tuple-element.48.dec_ref, bf16[512,4096]{1,0:T(8,128)(2,1)} %x_ref.5, ...), custom_call_target="tpu_custom_call", output_to_operand_aliasing={{0}: (8, {}), {1}: (9, {}), {2}: (10, {})} | custom-call | flops 134217728 | bytes 1048576 | tf_op jit(solution)/shard_map/more/pallas_call | solution.py:426
  15.6 1.6 %collective-permute-start.1 = (bf16[128,512]{1,0:T(8,128)(2,1)S(1)}, bf16[128,512]{1,0:T(8,128)(2,1)S(1)}, u32[]{:S(2)}, u32[]{:S(2)}) collective-permute-start(bf16[128,512]{1,0:T(8,128)(2,1)S(1)} %get-tuple-element.64.recv_ref), channel_id=1, source_target_pairs={{0,4},{4,8},{8,12},{12,0},{1,5},{5,9},{9,13},{13,1},{2,6},{6,10},{... | collective-permute-start | bytes 393224 | tf_op jit(solution)/shard_map/ppermute | solution.py:443
  17.3 10.3 %more.3 = (bf16[512,4096]{1,0:T(8,128)(2,1)S(1)}, bf16[3,128,4096]{2,1,0:T(8,128)(2,1)S(1)}, f32[8,128,512]{2,1,0:T(8,128)S(1)}) custom-call(f32[32,16]{1,0:T(8,128)S(1)} %get-tuple-element.48.dec_ref, bf16[512,4096]{1,0:T(8,128)(2,1)} %x_ref.5, ...), custom_call_target="tpu_custom_call", output_to_operand_aliasing={{0}: (8, {}), {1}: (9, {}), {2}: (10, {})} | custom-call | flops 805306368 | bytes 6291456 | tf_op jit(solution)/shard_map/more/pallas_call | solution.py:426
  27.6 2.6 %out.14 = (bf16[512,4096]{1,0:T(8,128)(2,1)}, f32[8,128]{1,0:T(8,128)}) custom-call(s32[1]{0:T(128)} %bitcast.place_ref, f32[32,16]{1,0:T(8,128)S(1)} %get-tuple-element.48.dec_ref, bf16[512,4096]{1,0:T(8,128)(2,1)S(1)} %get-tuple-element.58.mx_ref, bf16[3,128,4096]{2,1,0:T(8,128)(2,1)S(1)} %get-tuple-element.59.enter_ref, ...), custom_call_target="tpu_custom_call" | custom-call | flops 268435456 | bytes 1572864 | tf_op jit(solution)/shard_map/out/pallas_call | solution.py:477
  30.2 2.6 %out.15 = (bf16[512,4096]{1,0:T(8,128)(2,1)}, f32[8,128]{1,0:T(8,128)S(1)}) custom-call(s32[1]{0:T(128)} %bitcast.place_ref, f32[32,16]{1,0:T(8,128)S(1)} %get-tuple-element.48.dec_ref, bf16[512,4096]{1,0:T(8,128)(2,1)S(1)} %get-tuple-element.58.mx_ref, bf16[3,128,4096]{2,1,0:T(8,128)(2,1)S(1)} %get-tuple-element.59.enter_ref, ...), custom_call_target="tpu_custom_call", output_to_operand_aliasing={{0}: (10, {})} | custom-call | flops 268435456 | bytes 1572864 | tf_op jit(solution)/shard_map/out/pallas_call | solution.py:477
  33.7 2.6 %out.16 = (bf16[512,4096]{1,0:T(8,128)(2,1)}, f32[8,128]{1,0:T(8,128)S(1)}) custom-call(s32[1]{0:T(128)} %bitcast.place_ref, f32[32,16]{1,0:T(8,128)S(1)} %get-tuple-element.48.dec_ref, bf16[512,4096]{1,0:T(8,128)(2,1)S(1)} %get-tuple-element.58.mx_ref, bf16[3,128,4096]{2,1,0:T(8,128)(2,1)S(1)} %get-tuple-element.59.enter_ref, ...), custom_call_target="tpu_custom_call", output_to_operand_aliasing={{0}: (10, {})} | custom-call | flops 268435456 | bytes 1572864 | tf_op jit(solution)/shard_map/out/pallas_call | solution.py:477
  38.6 2.6 %out.17 = (bf16[512,4096]{1,0:T(8,128)(2,1)}, f32[8,128]{1,0:T(8,128)S(1)}) custom-call(s32[1]{0:T(128)} %bitcast.place_ref, f32[32,16]{1,0:T(8,128)S(1)} %get-tuple-element.48.dec_ref, bf16[512,4096]{1,0:T(8,128)(2,1)S(1)} %get-tuple-element.58.mx_ref, bf16[3,128,4096]{2,1,0:T(8,128)(2,1)S(1)} %get-tuple-element.59.enter_ref, ...), custom_call_target="tpu_custom_call", output_to_operand_aliasing={{0}: (10, {})} | custom-call | flops 268435456 | bytes 1572864 | tf_op jit(solution)/shard_map/out/pallas_call | solution.py:477
  42.1 2.6 %out.18 = (bf16[512,4096]{1,0:T(8,128)(2,1)}, f32[8,128]{1,0:T(8,128)S(1)}) custom-call(s32[1]{0:T(128)} %bitcast.place_ref, f32[32,16]{1,0:T(8,128)S(1)} %get-tuple-element.48.dec_ref, bf16[512,4096]{1,0:T(8,128)(2,1)S(1)} %get-tuple-element.58.mx_ref, bf16[3,128,4096]{2,1,0:T(8,128)(2,1)S(1)} %get-tuple-element.59.enter_ref, ...), custom_call_target="tpu_custom_call", output_to_operand_aliasing={{0}: (10, {})} | custom-call | flops 268435456 | bytes 1572864 | tf_op jit(solution)/shard_map/out/pallas_call | solution.py:477
  45.5 1.6 %collective-permute-start.5 = (bf16[128,512]{1,0:T(8,128)(2,1)S(1)}, bf16[128,512]{1,0:T(8,128)(2,1)S(1)}, u32[]{:S(2)}, u32[]{:S(2)}) collective-permute-start(bf16[128,512]{1,0:T(8,128)(2,1)S(1)} %join.12), channel_id=1, source_target_pairs={{0,4},{4,8},{8,12},{12,0},{1,5},{5,9},{9,13},{13,1},{2,6},{6,10},{... | collective-permute-start | bytes 393224 | tf_op jit(solution)/shard_map/ppermute | solution.py:512
  47.1 2.6 %out.19 = (bf16[512,4096]{1,0:T(8,128)(2,1)}, f32[8,128]{1,0:T(8,128)S(1)}) custom-call(s32[1]{0:T(128)} %bitcast.place_ref, f32[32,16]{1,0:T(8,128)S(1)} %get-tuple-element.48.dec_ref, bf16[512,4096]{1,0:T(8,128)(2,1)S(1)} %get-tuple-element.58.mx_ref, bf16[3,128,4096]{2,1,0:T(8,128)(2,1)S(1)} %get-tuple-element.59.enter_ref, ...), custom_call_target="tpu_custom_call", output_to_operand_aliasing={{0}: (10, {})} | custom-call | flops 268435456 | bytes 1572864 | tf_op jit(solution)/shard_map/out/pallas_call | solution.py:477
  51.8 2.6 %out.20 = (bf16[512,4096]{1,0:T(8,128)(2,1)}, f32[8,128]{1,0:T(8,128)S(1)}) custom-call(s32[1]{0:T(128)} %bitcast.place_ref, f32[32,16]{1,0:T(8,128)S(1)} %get-tuple-element.48.dec_ref, bf16[512,4096]{1,0:T(8,128)(2,1)S(1)} %get-tuple-element.58.mx_ref, bf16[3,128,4096]{2,1,0:T(8,128)(2,1)S(1)} %get-tuple-element.59.enter_ref, ...), custom_call_target="tpu_custom_call", output_to_operand_aliasing={{0}: (10, {})} | custom-call | flops 268435456 | bytes 1572864 | tf_op jit(solution)/shard_map/out/pallas_call | solution.py:477
  56.7 2.6 %out.21 = (bf16[512,4096]{1,0:T(8,128)(2,1)}, f32[8,128]{1,0:T(8,128)S(1)}) custom-call(s32[1]{0:T(128)} %bitcast.place_ref, f32[32,16]{1,0:T(8,128)S(1)} %get-tuple-element.48.dec_ref, bf16[512,4096]{1,0:T(8,128)(2,1)S(1)} %get-tuple-element.58.mx_ref, bf16[3,128,4096]{2,1,0:T(8,128)(2,1)S(1)} %get-tuple-element.59.enter_ref, ...), custom_call_target="tpu_custom_call", output_to_operand_aliasing={{0}: (10, {})} | custom-call | flops 268435456 | bytes 1572864 | tf_op jit(solution)/shard_map/out/pallas_call | solution.py:477
  60.2 2.0 %out.22 = (bf16[512,4096]{1,0:T(8,128)(2,1)}, f32[8,128]{1,0:T(8,128)S(1)}) custom-call(s32[1]{0:T(128)} %bitcast.place_ref, f32[32,16]{1,0:T(8,128)S(1)} %get-tuple-element.48.dec_ref, bf16[512,4096]{1,0:T(8,128)(2,1)S(1)} %get-tuple-element.58.mx_ref, bf16[3,128,4096]{2,1,0:T(8,128)(2,1)S(1)} %get-tuple-element.59.enter_ref, ...), custom_call_target="tpu_custom_call", output_to_operand_aliasing={{0}: (10, {})} | custom-call | flops 268435456 | bytes 1572864 | tf_op jit(solution)/shard_map/out/pallas_call | solution.py:477
  63.6 3.2 %collective-permute-start.9 = (bf16[128,512]{1,0:T(8,128)(2,1)S(1)}, bf16[128,512]{1,0:T(8,128)(2,1)S(1)}, u32[]{:S(2)}, u32[]{:S(2)}) collective-permute-start(bf16[128,512]{1,0:T(8,128)(2,1)S(1)} %join.16), channel_id=1, source_target_pairs={{0,4},{4,8},{8,12},{12,0},{1,5},{5,9},{9,13},{13,1},{2,6},{6,10},{... | collective-permute-start | bytes 393224 | tf_op jit(solution)/shard_map/ppermute | solution.py:512
  66.8 2.0 %out.23 = (bf16[512,4096]{1,0:T(8,128)(2,1)}, f32[8,128]{1,0:T(8,128)S(1)}) custom-call(s32[1]{0:T(128)} %bitcast.place_ref, f32[32,16]{1,0:T(8,128)S(1)} %get-tuple-element.48.dec_ref, bf16[512,4096]{1,0:T(8,128)(2,1)S(1)} %get-tuple-element.58.mx_ref, bf16[3,128,4096]{2,1,0:T(8,128)(2,1)S(1)} %get-tuple-element.59.enter_ref, ...), custom_call_target="tpu_custom_call", output_to_operand_aliasing={{0}: (10, {})} | custom-call | flops 268435456 | bytes 1572864 | tf_op jit(solution)/shard_map/out/pallas_call | solution.py:477
  69.7 1.7 %collective-permute-start.12 = (bf16[128,512]{1,0:T(8,128)(2,1)S(1)}, bf16[128,512]{1,0:T(8,128)(2,1)S(1)}, u32[]{:S(2)}, u32[]{:S(2)}) collective-permute-start(bf16[128,512]{1,0:T(8,128)(2,1)S(1)} %join.19), channel_id=1, source_target_pairs={{0,4},{4,8},{8,12},{12,0},{1,5},{5,9},{9,13},{13,1},{2,6},{6,10},{... | collective-permute-start | bytes 393224 | tf_op jit(solution)/shard_map/ppermute | solution.py:512
  71.3 2.0 %out.24 = (bf16[512,4096]{1,0:T(8,128)(2,1)}, f32[8,128]{1,0:T(8,128)S(1)}) custom-call(s32[1]{0:T(128)} %bitcast.place_ref, f32[32,16]{1,0:T(8,128)S(1)} %get-tuple-element.48.dec_ref, bf16[512,4096]{1,0:T(8,128)(2,1)S(1)} %get-tuple-element.58.mx_ref, bf16[3,128,4096]{2,1,0:T(8,128)(2,1)S(1)} %get-tuple-element.59.enter_ref, ...), custom_call_target="tpu_custom_call", output_to_operand_aliasing={{0}: (10, {})} | custom-call | flops 268435456 | bytes 1572864 | tf_op jit(solution)/shard_map/out/pallas_call | solution.py:477
  75.7 2.0 %out.25 = (bf16[512,4096]{1,0:T(8,128)(2,1)}, f32[8,128]{1,0:T(8,128)}) custom-call(s32[1]{0:T(128)} %bitcast.place_ref, f32[32,16]{1,0:T(8,128)S(1)} %get-tuple-element.48.dec_ref, bf16[512,4096]{1,0:T(8,128)(2,1)S(1)} %get-tuple-element.58.mx_ref, bf16[3,128,4096]{2,1,0:T(8,128)(2,1)S(1)} %get-tuple-element.59.enter_ref, ...), custom_call_target="tpu_custom_call", output_to_operand_aliasing={{0}: (10, {})} | custom-call | flops 268435456 | bytes 1572864 | tf_op jit(solution)/shard_map/out/pallas_call | solution.py:477
  77.7 2.0 %out.26 = (bf16[512,4096]{1,0:T(8,128)(2,1)}, f32[8,128]{1,0:T(8,128)}) custom-call(s32[1]{0:T(128)} %bitcast.place_ref, f32[32,16]{1,0:T(8,128)S(1)} %get-tuple-element.48.dec_ref, bf16[512,4096]{1,0:T(8,128)(2,1)S(1)} %get-tuple-element.58.mx_ref, bf16[3,128,4096]{2,1,0:T(8,128)(2,1)S(1)} %get-tuple-element.59.enter_ref, ...), custom_call_target="tpu_custom_call", output_to_operand_aliasing={{0}: (10, {})} | custom-call | flops 268435456 | bytes 1572864 | tf_op jit(solution)/shard_map/out/pallas_call | solution.py:477
  81.0 2.0 %out.27 = (bf16[512,4096]{1,0:T(8,128)(2,1)}, f32[8,128]{1,0:T(8,128)}) custom-call(s32[1]{0:T(128)} %bitcast.place_ref, f32[32,16]{1,0:T(8,128)S(1)} %get-tuple-element.48.dec_ref, bf16[512,4096]{1,0:T(8,128)(2,1)S(1)} %get-tuple-element.58.mx_ref, bf16[3,128,4096]{2,1,0:T(8,128)(2,1)S(1)} %get-tuple-element.59.enter_ref, ...), custom_call_target="tpu_custom_call", output_to_operand_aliasing={{0}: (10, {})} | custom-call | flops 268435456 | bytes 1572864 | tf_op jit(solution)/shard_map/out/pallas_call | solution.py:477
  (35 shorter events, 19.0 us)
Async XLA Ops:
  1.6 7.4 %collective-permute-start = (bf16[8,4608]{1,0:T(8,128)(2,1)S(1)}, bf16[8,4608]{1,0:T(8,128)(2,1)S(1)}, u32[]{:S(2)}, u32[]{:S(2)}) collective-permute-start(bf16[8,4608]{1,0:T(8,128)(2,1)S(1)} %pad_maximum_fusion), channel_id=1, source_target_pairs={{0,4},{4,8},{8,12},{12,0},{1,5},{5,9},{9,13},{13,1},{2,6},{6,10},{... | collective-permute-start | bytes 221192 | tf_op jit(solution)/shard_map/ppermute | solution.py:349
  13.0 19.7 %collective-permute-start.2 = (bf16[128,512]{1,0:T(8,128)(2,1)S(1)}, bf16[128,512]{1,0:T(8,128)(2,1)S(1)}, u32[]{:S(2)}, u32[]{:S(2)}) collective-permute-start(bf16[128,512]{1,0:T(8,128)(2,1)S(1)} %get-tuple-element.66.recv_ref), channel_id=1, source_target_pairs={{0,4},{4,8},{8,12},{12,0},{1,5},{5,9},{9,13},{13,1},{2,6},{6,10},{... | collective-permute-start | bytes 393224 | tf_op jit(solution)/shard_map/ppermute | solution.py:441
  15.6 20.6 %collective-permute-start.1 = (bf16[128,512]{1,0:T(8,128)(2,1)S(1)}, bf16[128,512]{1,0:T(8,128)(2,1)S(1)}, u32[]{:S(2)}, u32[]{:S(2)}) collective-permute-start(bf16[128,512]{1,0:T(8,128)(2,1)S(1)} %get-tuple-element.64.recv_ref), channel_id=1, source_target_pairs={{0,4},{4,8},{8,12},{12,0},{1,5},{5,9},{9,13},{13,1},{2,6},{6,10},{... | collective-permute-start | bytes 393224 | tf_op jit(solution)/shard_map/ppermute | solution.py:443
  33.6 7.6 %collective-permute-start.4 = (bf16[128,512]{1,0:T(8,128)(2,1)S(1)}, bf16[128,512]{1,0:T(8,128)(2,1)S(1)}, u32[]{:S(2)}, u32[]{:S(2)}) collective-permute-start(bf16[128,512]{1,0:T(8,128)(2,1)S(1)} %join.11), channel_id=1, source_target_pairs={{0,4},{4,8},{8,12},{12,0},{1,5},{5,9},{9,13},{13,1},{2,6},{6,10},{... | collective-permute-start | bytes 393224 | tf_op jit(solution)/shard_map/ppermute | solution.py:512
  37.1 7.6 %collective-permute-start.3 = (bf16[128,512]{1,0:T(8,128)(2,1)S(1)}, bf16[128,512]{1,0:T(8,128)(2,1)S(1)}, u32[]{:S(2)}, u32[]{:S(2)}) collective-permute-start(bf16[128,512]{1,0:T(8,128)(2,1)S(1)} %join.10), channel_id=1, source_target_pairs={{0,4},{4,8},{8,12},{12,0},{1,5},{5,9},{9,13},{13,1},{2,6},{6,10},{... | collective-permute-start | bytes 393224 | tf_op jit(solution)/shard_map/ppermute | solution.py:512
  42.0 7.9 %collective-permute-start.6 = (bf16[128,512]{1,0:T(8,128)(2,1)S(1)}, bf16[128,512]{1,0:T(8,128)(2,1)S(1)}, u32[]{:S(2)}, u32[]{:S(2)}) collective-permute-start(bf16[128,512]{1,0:T(8,128)(2,1)S(1)} %join.13), channel_id=1, source_target_pairs={{0,4},{4,8},{8,12},{12,0},{1,5},{5,9},{9,13},{13,1},{2,6},{6,10},{... | collective-permute-start | bytes 393224 | tf_op jit(solution)/shard_map/ppermute | solution.py:512
  45.5 8.8 %collective-permute-start.5 = (bf16[128,512]{1,0:T(8,128)(2,1)S(1)}, bf16[128,512]{1,0:T(8,128)(2,1)S(1)}, u32[]{:S(2)}, u32[]{:S(2)}) collective-permute-start(bf16[128,512]{1,0:T(8,128)(2,1)S(1)} %join.12), channel_id=1, source_target_pairs={{0,4},{4,8},{8,12},{12,0},{1,5},{5,9},{9,13},{13,1},{2,6},{6,10},{... | collective-permute-start | bytes 393224 | tf_op jit(solution)/shard_map/ppermute | solution.py:512
  50.8 8.4 %collective-permute-start.8 = (bf16[128,512]{1,0:T(8,128)(2,1)S(1)}, bf16[128,512]{1,0:T(8,128)(2,1)S(1)}, u32[]{:S(2)}, u32[]{:S(2)}) collective-permute-start(bf16[128,512]{1,0:T(8,128)(2,1)S(1)} %join.15), channel_id=1, source_target_pairs={{0,4},{4,8},{8,12},{12,0},{1,5},{5,9},{9,13},{13,1},{2,6},{6,10},{... | collective-permute-start | bytes 393224 | tf_op jit(solution)/shard_map/ppermute | solution.py:512
  55.2 7.6 %collective-permute-start.7 = (bf16[128,512]{1,0:T(8,128)(2,1)S(1)}, bf16[128,512]{1,0:T(8,128)(2,1)S(1)}, u32[]{:S(2)}, u32[]{:S(2)}) collective-permute-start(bf16[128,512]{1,0:T(8,128)(2,1)S(1)} %join.14), channel_id=1, source_target_pairs={{0,4},{4,8},{8,12},{12,0},{1,5},{5,9},{9,13},{13,1},{2,6},{6,10},{... | collective-permute-start | bytes 393224 | tf_op jit(solution)/shard_map/ppermute | solution.py:512
  60.1 8.7 %collective-permute-start.10 = (bf16[128,512]{1,0:T(8,128)(2,1)S(1)}, bf16[128,512]{1,0:T(8,128)(2,1)S(1)}, u32[]{:S(2)}, u32[]{:S(2)}) collective-permute-start(bf16[128,512]{1,0:T(8,128)(2,1)S(1)} %join.17), channel_id=1, source_target_pairs={{0,4},{4,8},{8,12},{12,0},{1,5},{5,9},{9,13},{13,1},{2,6},{6,10},{... | collective-permute-start | bytes 393224 | tf_op jit(solution)/shard_map/ppermute | solution.py:512
  63.6 9.7 %collective-permute-start.9 = (bf16[128,512]{1,0:T(8,128)(2,1)S(1)}, bf16[128,512]{1,0:T(8,128)(2,1)S(1)}, u32[]{:S(2)}, u32[]{:S(2)}) collective-permute-start(bf16[128,512]{1,0:T(8,128)(2,1)S(1)} %join.16), channel_id=1, source_target_pairs={{0,4},{4,8},{8,12},{12,0},{1,5},{5,9},{9,13},{13,1},{2,6},{6,10},{... | collective-permute-start | bytes 393224 | tf_op jit(solution)/shard_map/ppermute | solution.py:512
  69.7 8.0 %collective-permute-start.12 = (bf16[128,512]{1,0:T(8,128)(2,1)S(1)}, bf16[128,512]{1,0:T(8,128)(2,1)S(1)}, u32[]{:S(2)}, u32[]{:S(2)}) collective-permute-start(bf16[128,512]{1,0:T(8,128)(2,1)S(1)} %join.19), channel_id=1, source_target_pairs={{0,4},{4,8},{8,12},{12,0},{1,5},{5,9},{9,13},{13,1},{2,6},{6,10},{... | collective-permute-start | bytes 393224 | tf_op jit(solution)/shard_map/ppermute | solution.py:512
  74.2 6.8 %collective-permute-start.11 = (bf16[128,512]{1,0:T(8,128)(2,1)S(1)}, bf16[128,512]{1,0:T(8,128)(2,1)S(1)}, u32[]{:S(2)}, u32[]{:S(2)}) collective-permute-start(bf16[128,512]{1,0:T(8,128)(2,1)S(1)} %join.18), channel_id=1, source_target_pairs={{0,4},{4,8},{8,12},{12,0},{1,5},{5,9},{9,13},{13,1},{2,6},{6,10},{... | collective-permute-start | bytes 393224 | tf_op jit(solution)/shard_map/ppermute | solution.py:512

commit v3 on v2

v3 whole, which is shorter than its diff:
```python
import functools
import math

import jax
import jax.numpy as jnp
from jax import lax
from jax.experimental import pallas as pl
from jax.experimental.pallas import tpu as pltpu
from jax.sharding import PartitionSpec as P

D = 128
Q = 128
BLK = 512
NQ = BLK // Q
HC = 4
CW = HC * D
RIM = 8
LOG2E = math.log2(math.e)
F32 = jnp.float32
BF16 = jnp.bfloat16


def doc_of(pos, starts_ref):
    count = jnp.zeros_like(pos)
    for j in range(starts_ref.shape[0]):
        count = count + (pos >= starts_ref[j]).astype(jnp.int32)
    return count - 1


def silu_half(u):
    return u + u * jnp.tanh(u)


def doc_at(pos, starts_ref):
    count = jnp.int32(-1)
    for j in range(starts_ref.shape[0]):
        count = count + (pos >= starts_ref[j]).astype(jnp.int32)
    return count


def column_of(ref):
    heads = ref.shape[0]
    index = lax.broadcasted_iota(jnp.int32, (heads, 1), 0)
    column = jnp.zeros((heads, 1), F32)
    for h in range(heads):
        column = jnp.where(index == h, ref[h], column)
    return column


def split(value, parts):
    pieces = []
    for _ in range(parts - 1):
        piece = value.astype(BF16).astype(F32)
        pieces.append(piece)
        value = value - piece
    return pieces + [value]


def doc_at(pos, starts_ref):
    count = jnp.int32(-1)
    for j in range(starts_ref.shape[0]):
        count = count + (pos >= starts_ref[j]).astype(jnp.int32)
    return count


def column_of(ref):
    heads = ref.shape[0]
    index = lax.broadcasted_iota(jnp.int32, (heads, 1), 0)
    column = jnp.zeros((heads, 1), F32)
    for h in range(heads):
        column = jnp.where(index == h, ref[h], column)
    return column


def split(value, parts):
    pieces = []
    for _ in range(parts - 1):
        piece = value.astype(BF16).astype(F32)
        pieces.append(piece)
        value = value - piece
    return pieces + [value]


def doc_at(pos, starts_ref):
    count = jnp.int32(-1)
    for j in range(starts_ref.shape[0]):
        count = count + (pos >= starts_ref[j]).astype(jnp.int32)
    return count


def column_of(ref):
    heads = ref.shape[0]
    index = lax.broadcasted_iota(jnp.int32, (heads, 1), 0)
    column = jnp.zeros((heads, 1), F32)
    for h in range(heads):
        column = jnp.where(index == h, ref[h], column)
    return column


def split(value, parts):
    pieces = []
    for _ in range(parts - 1):
        piece = value.astype(BF16).astype(F32)
        pieces.append(piece)
        value = value - piece
    return pieces + [value]


def doc_at(pos, starts_ref):
    count = jnp.int32(-1)
    for j in range(starts_ref.shape[0]):
        count = count + (pos >= starts_ref[j]).astype(jnp.int32)
    return count


def column_of(ref):
    heads = ref.shape[0]
    index = lax.broadcasted_iota(jnp.int32, (heads, 1), 0)
    column = jnp.zeros((heads, 1), F32)
    for h in range(heads):
        column = jnp.where(index == h, ref[h], column)
    return column


def split(value, parts):
    pieces = []
    for _ in range(parts - 1):
        piece = value.astype(BF16).astype(F32)
        pieces.append(piece)
        value = value - piece
    return pieces + [value]


def doc_at(pos, starts_ref):
    count = jnp.int32(-1)
    for j in range(starts_ref.shape[0]):
        count = count + (pos >= starts_ref[j]).astype(jnp.int32)
    return count


def column_of(ref):
    heads = ref.shape[0]
    index = lax.broadcasted_iota(jnp.int32, (heads, 1), 0)
    column = jnp.zeros((heads, 1), F32)
    for h in range(heads):
        column = jnp.where(index == h, ref[h], column)
    return column


def split(value, parts):
    pieces = []
    for _ in range(parts - 1):
        piece = value.astype(BF16).astype(F32)
        pieces.append(piece)
        value = value - piece
    return pieces + [value]


def params_kernel(
    starts_ref, bias_ref, alog_ref, skip_ref, dt_ref, scale_ref, cum_ref, rows_ref, fade_ref, shift_ref, keep_ref
):
    first = lax.axis_index("seq") * BLK
    heads = dt_ref.shape[0]
    v = dt_ref[...] + column_of(bias_ref)
    step = jnp.maximum(v, 0.0) + jnp.log(1.0 + jnp.exp(-jnp.abs(v)))
    rate = -jnp.exp(column_of(alog_ref)) * step
    tri = (
        lax.broadcasted_iota(jnp.int32, (Q, Q), 0) <= lax.broadcasted_iota(jnp.int32, (Q, Q), 1)
    ).astype(F32)
    doc_before = doc_at(first - 1, starts_ref)
    doc_last = doc_at(first + BLK - 1, starts_ref)
    cums = []
    base = jnp.zeros((heads, 1), F32)
    for q in range(NQ):
        part = jnp.dot(
            rate[:, q * Q : (q + 1) * Q], tri, precision=lax.Precision.HIGHEST, preferred_element_type=F32
        )
        cums.append(part + base)
        base = base + part[:, Q - 1 : Q]
    for q in range(NQ):
        span = slice(q * Q, (q + 1) * Q)
        cum = cums[q]
        step_q = step[:, span]
        pos = first + q * Q + lax.broadcasted_iota(jnp.int32, (1, Q), 1)
        doc = doc_of(pos, starts_ref)
        tail = jnp.where(doc == doc_last, jnp.exp(base - cum) * step_q, 0.0)
        entry = jnp.where(doc == doc_before, jnp.exp(cum), 0.0)
        packed = split(tail, 2) + split(entry, 2)
        if 4 * heads < D:
            packed.append(jnp.zeros((D - 4 * heads, Q), F32))
        scale_ref[span, :] = jnp.transpose(jnp.concatenate(packed, axis=0), (1, 0)).astype(BF16)
        packed = split(cum * LOG2E, 3) + [jnp.zeros((D - 3 * heads, Q), F32)]
        cum_ref[span, :] = jnp.transpose(jnp.concatenate(packed, axis=0), (1, 0)).astype(BF16)
        terms = (cum - jnp.log(step_q)) * LOG2E
        for c in range(heads // HC):
            rows_ref[c, :, span] = terms[c * HC : (c + 1) * HC]
    decay = jnp.exp(base) * jnp.where(doc_last == doc_before, 1.0, 0.0)
    skip = column_of(skip_ref)
    for c in range(heads // HC):
        for i in range(HC):
            h = c * HC + i
            lanes = slice(i * D, (i + 1) * D)
            fade_ref[c, 0:1, lanes] = jnp.broadcast_to(skip[h : h + 1], (1, D))
            fade_ref[c, 1:2, lanes] = jnp.broadcast_to(decay[h : h + 1], (1, D))
    for q in range(NQ):
        row = lax.broadcasted_iota(jnp.int32, (Q, 2 * Q), 0)
        col = lax.broadcasted_iota(jnp.int32, (Q, 2 * Q), 1) - Q
        at = first + q * Q
        same = doc_of(at + row, starts_ref) == doc_of(at + col, starts_ref)
        for k in range(3):
            hit = same & (col == row - (3 - k))
            shift_ref[q, k * Q : (k + 1) * Q, :] = jnp.where(hit, 1.0, 0.0).astype(BF16)
        doc_row = doc_of(at + lax.broadcasted_iota(jnp.int32, (Q, BLK), 0), starts_ref)
        col = lax.broadcasted_iota(jnp.int32, (Q, BLK), 1)
        row = q * Q + lax.broadcasted_iota(jnp.int32, (Q, BLK), 0)
        keep = (row >= col) & (doc_row == doc_of(first + col, starts_ref))
        keep_ref[q * Q : (q + 1) * Q, :] = jnp.where(keep, 1.0, 0.0)


def chooser(heads, chunk, lo, hi, width):
    k = lax.broadcasted_iota(jnp.int32, (D, width), 0)
    head = HC * chunk + lax.broadcasted_iota(jnp.int32, (D, width), 1) // D
    hit = ((k & (heads - 1)) == head) & (k >= lo * heads) & (k < hi * heads)
    return jnp.where(hit, 1.0, 0.0).astype(BF16)


def convolved(q, window, now, shift_ref, taps, bias):
    moved = jnp.dot(shift_ref[q], window, preferred_element_type=F32)
    total = (0.5 * taps[3]) * now.astype(F32) + 0.5 * bias
    for k in range(3):
        total = total + (0.5 * taps[k]) * moved[k * Q : (k + 1) * Q]
    return silu_half(total)


def window_of(q, edge_ref, x_ref):
    return edge_ref[...] if q == 0 else x_ref[(q - 1) * Q : (q + 1) * Q, :]


def edge(edge_ref, rim_ref, x_ref):
    width = x_ref.shape[1]
    rim = jnp.concatenate([jnp.zeros((Q - RIM, width), F32), rim_ref[...].astype(F32)], axis=0)
    edge_ref[0:Q, 0:width] = rim.astype(BF16)
    edge_ref[Q : 2 * Q, 0:width] = x_ref[0:Q, :]


def state_body(
    chunk, heads, per_group, x_ref, rim_ref, wx_ref, bx_ref, shift_ref, scale_ref, bt_ref,
    mx_ref, end_ref, edge_ref, tail_ref, send_ref=None,
):
    edge(edge_ref, rim_ref, x_ref)
    pick = chooser(heads, chunk, 0, 2, CW)
    taps = [wx_ref[k : k + 1, :] for k in range(4)]
    for q in range(NQ):
        span = slice(q * Q, (q + 1) * Q)
        mixed = convolved(q, window_of(q, edge_ref, x_ref), x_ref[span, :], shift_ref, taps, bx_ref[...])
        mx_ref[0, span, :] = mixed.astype(BF16)
        scale = jnp.dot(scale_ref[span, :], pick, preferred_element_type=F32)
        tail_ref[span, :] = (mixed * scale).astype(BF16)
    state = jnp.dot(bt_ref[lax.div(chunk, per_group)], tail_ref[...], preferred_element_type=F32)
    end_ref[0] = state
    if send_ref is not None:
        send_ref[...] = state.astype(BF16)


def first_kernel(
    x_ref, rim_ref, wx_ref, bx_ref, shift_ref, scale_ref, keep_ref, bc_ref, rimbc_ref, wbc_ref, bbc_ref,
    mx_ref, end_ref, send_ref, bt_ref, c_ref, score_ref,
    edge_ref, tail_ref, *, heads, per_group,
):
    groups = bt_ref.shape[0]
    wide = 2 * groups * D
    edge(edge_ref, rimbc_ref, bc_ref)

    def joined(rows):
        return jnp.concatenate(rows, axis=1)

    taps = [joined([wbc_ref[k, p : p + 1, :] for p in range(2)]) for k in range(4)]
    bias = joined([bbc_ref[p : p + 1, :] for p in range(2)])
    for q in range(NQ):
        span = slice(q * Q, (q + 1) * Q)
        window = edge_ref[:, 0:wide] if q == 0 else bc_ref[(q - 1) * Q : (q + 1) * Q, :]
        mixed = convolved(q, window, bc_ref[span, :], shift_ref, taps, bias)
        upto = (q + 1) * Q
        for g in range(groups):
            bt_ref[g, :, span] = jnp.transpose(mixed[:, g * D : (g + 1) * D], (1, 0)).astype(BF16)
            c = mixed[:, (groups + g) * D : (groups + g + 1) * D].astype(BF16)
            c_ref[g, span, :] = c
            score = jnp.dot(c, bt_ref[g, :, 0:upto], preferred_element_type=F32)
            score_ref[g, span, 0:upto] = keep_ref[span, 0:upto] * score
    state_body(
        0, heads, per_group, x_ref, rim_ref, wx_ref, bx_ref, shift_ref, scale_ref, bt_ref,
        mx_ref, end_ref, edge_ref, tail_ref, send_ref,
    )


def more_kernel(
    x_ref, rim_ref, wx_ref, bx_ref, shift_ref, scale_ref, bt_ref, old1, old2,
    mx_ref, end_ref, *rest, heads, per_group, chunk_of, sends,
):
    state_body(
        chunk_of(pl.program_id(0)), heads, per_group, x_ref, rim_ref, wx_ref, bx_ref, shift_ref, scale_ref,
        bt_ref, mx_ref, end_ref, *rest[-2:], *rest[:sends],
    )


def join_kernel(fade_ref, recv_ref, end_ref, token_ref, send_ref, *, turn, stream, per_stream):
    chunk = stream * per_stream + jnp.clip(turn - lax.axis_index("seq"), 0, per_stream - 1)
    send_ref[...] = (fade_ref[chunk, 1:2, :] * recv_ref[...].astype(F32) + end_ref[chunk]).astype(BF16)


def out_kernel(
    fade_ref, mx_ref, c_ref, score_ref, scale_ref, cum_ref, rows_ref, recv_ref,
    *rest, turn, stream, per_stream, per_group, heads,
):
    out_ref, token_ref, ready_ref, sem = rest[-4:]
    token_ref[...] = jnp.zeros_like(token_ref)
    rank = turn - lax.axis_index("seq")

    @pl.when((rank >= 0) & (rank < per_stream))
    def compute():
        chunk = stream * per_stream + rank
        g = lax.div(chunk, per_group)
        pick_cum = chooser(heads, chunk, 0, 3, CW)
        pick_entry = chooser(heads, chunk, 2, 4, CW)
        copies = []
        for q in range(NQ):
            span = slice(q * Q, (q + 1) * Q)
            cums = jnp.dot(cum_ref[span, :], pick_cum, preferred_element_type=F32)
            entry = jnp.dot(scale_ref[span, :], pick_entry, preferred_element_type=F32)
            far = jnp.dot(c_ref[g, span, :], recv_ref[...], preferred_element_type=F32)
            for i in range(HC):
                lanes = slice(i * D, (i + 1) * D)
                parts = []
                for j in range(q + 1):
                    there = slice(j * Q, (j + 1) * Q)
                    gap = cums[:, lanes] - rows_ref[chunk, i : i + 1, there]
                    if j == q:
                        gap = jnp.minimum(gap, 100.0)
                    parts.append((score_ref[g, span, there] * jnp.exp2(gap)).astype(BF16))
                weight = jnp.concatenate(parts, axis=1)
                y = jnp.dot(weight, mx_ref[chunk, 0 : (q + 1) * Q, lanes], preferred_element_type=F32)
                x = mx_ref[chunk, span, lanes].astype(F32)
                y = y + entry[:, lanes] * far[:, lanes] + fade_ref[chunk, 0:1, lanes] * x
                ready_ref[span, lanes] = y.astype(BF16)
            to = out_ref.at[pl.ds(q * Q, Q), pl.ds(pl.multiple_of(chunk * CW, CW), CW)]
            copy = pltpu.make_async_copy(ready_ref.at[pl.ds(q * Q, Q), :], to, sem.at[q])
            copy.start()
            copies.append(copy)
        for copy in copies:
            copy.wait()


SMEM = pl.BlockSpec(memory_space=pltpu.SMEM)
ROOM = pltpu.CompilerParams(vmem_limit_bytes=16 * 2**20)
ANY = pl.BlockSpec(memory_space=pl.ANY)
VMEM = pl.BlockSpec(memory_space=pltpu.VMEM)


def whole(shape):
    return pl.BlockSpec(shape, lambda *_: (0,) * len(shape))


def shape_of(shape, dtype):
    return jax.ShapeDtypeStruct(shape, dtype)


def per_device(
    x_raw, bc_raw, dt_raw, dt_bias, a_log, d_skip, conv_x, conv_x_bias, conv_bc, conv_bc_bias, doc_starts
):
    rows, width = x_raw.shape
    held = [x_raw, dt_raw, dt_bias, a_log, d_skip, conv_x, conv_x_bias[None], conv_bc, conv_bc_bias, doc_starts]
    held = [pltpu.with_memory_space_constraint(a, pltpu.HBM) for a in held]
    x_pin, dt_raw, dt_bias, a_log, d_skip, conv_x, bias_x, conv_bc, conv_bc_bias, doc_starts = held
    groups = bc_raw.shape[2] // D
    heads = dt_raw.shape[0]
    chunks = heads // HC
    per_group = chunks // groups
    wide = 2 * groups * D
    seq = lax.axis_size("seq")
    ring = [(i, (i + 1) % seq) for i in range(seq)]
    streams = 2
    per_stream = chunks // streams
    slots = per_stream + seq - 2

    tail = jnp.concatenate([x_raw[rows - RIM :], bc_raw[rows - RIM :].reshape(RIM, -1)], axis=1)
    rim = lax.ppermute(tail, "seq", ring)
    bc = bc_raw.reshape(rows, -1)

    scale, cums, row_terms, fade, shift, keep = pl.pallas_call(
        params_kernel,
        in_specs=[SMEM] * 4 + [VMEM],
        out_specs=[VMEM] * 6,
        out_shape=[
            shape_of((BLK, D), BF16),
            shape_of((BLK, D), BF16),
            shape_of((chunks, HC, BLK), F32),
            shape_of((chunks, 2, CW), F32),
            shape_of((NQ, 3 * Q, 2 * Q), BF16),
            shape_of((BLK, BLK), F32),
        ],
        compiler_params=ROOM,
        name="params",
    )(doc_starts, dt_bias, a_log, d_skip, dt_raw)

    def chunk_specs(chunk_of):
        ins = [
            pl.BlockSpec((BLK, CW), lambda i: (0, chunk_of(i))),
            pl.BlockSpec((RIM, CW), lambda i: (0, chunk_of(i))),
            pl.BlockSpec((4, CW), lambda i: (0, chunk_of(i))),
            pl.BlockSpec((1, CW), lambda i: (0, chunk_of(i))),
            whole((NQ, 3 * Q, 2 * Q)),
            whole((BLK, D)),
        ]
        outs = [
            pl.BlockSpec((1, BLK, CW), lambda i: (chunk_of(i), 0, 0)),
            pl.BlockSpec((1, D, CW), lambda i: (chunk_of(i), 0, 0)),
        ]
        return ins, outs

    big = [shape_of((chunks, BLK, CW), BF16), shape_of((chunks, D, CW), F32)]
    chunk_shape = shape_of((D, CW), BF16)
    scratch = [pltpu.VMEM((2 * Q, CW), BF16), pltpu.VMEM((BLK, CW), BF16)]
    ins, outs = chunk_specs(lambda i: 0)
    mixed_x, end, send_a, bt, mixed_c, score = pl.pallas_call(
        functools.partial(first_kernel, heads=heads, per_group=per_group),
        grid=(1,),
        in_specs=[
            *ins,
            whole((BLK, BLK)),
            whole((BLK, wide)),
            pl.BlockSpec((RIM, wide), lambda i: (0, width // wide)),
            whole((4, 2, groups * D)),
            whole((2, groups * D)),
        ],
        out_specs=[
            *outs,
            whole((D, CW)),
            whole((groups, D, BLK)),
            whole((groups, BLK, D)),
            whole((groups, BLK, BLK)),
        ],
        out_shape=[
            *big,
            chunk_shape,
            shape_of((groups, D, BLK), BF16),
            shape_of((groups, BLK, D), BF16),
            shape_of((groups, BLK, BLK), F32),
        ],
        scratch_shapes=scratch,
        compiler_params=ROOM,
        name="first",
    )(x_pin, rim, conv_x, bias_x, shift, scale, keep, bc, rim, conv_bc, conv_bc_bias)

    def more(count, chunk_of, sends, mixed_x, end):
        ins, outs = chunk_specs(chunk_of)
        return pl.pallas_call(
            functools.partial(more_kernel, heads=heads, per_group=per_group, chunk_of=chunk_of, sends=sends),
            grid=(count,),
            in_specs=[*ins, whole((groups, D, BLK)), ANY, ANY],
            out_specs=outs + [whole((D, CW))] * sends,
            out_shape=big + [chunk_shape] * sends,
            input_output_aliases={7: 0, 8: 1},
            scratch_shapes=scratch,
            compiler_params=ROOM,
            cost_estimate=pl.CostEstimate(
                flops=4 * count * BLK * D * CW, bytes_accessed=4 * count * BLK * CW, transcendentals=0
            ),
            name="more",
        )(x_pin, rim, conv_x, bias_x, shift, scale, bt, mixed_x, end)

    flying = [lax.ppermute(send_a, "seq", ring), None]
    mixed_x, end, send_b = more(1, lambda i: per_stream, 1, mixed_x, end)
    flying[1] = lax.ppermute(send_b, "seq", ring)

    def join(turn, s, recv, token):
        return pl.pallas_call(
            functools.partial(join_kernel, turn=turn, stream=s, per_stream=per_stream),
            in_specs=[VMEM, VMEM, VMEM, VMEM],
            out_specs=VMEM,
            out_shape=chunk_shape,
            compiler_params=ROOM,
            name="join",
        )(fade, recv, end, token)

    def output(turn, s, recv, out):
        old = [] if out is None else [out]
        return pl.pallas_call(
            functools.partial(
                out_kernel, turn=turn, stream=s, per_stream=per_stream, per_group=per_group, heads=heads
            ),
            in_specs=[VMEM] * 8 + [ANY] * len(old),
            out_specs=[ANY, VMEM],
            out_shape=[pltpu.HBM((BLK, width), BF16), shape_of((8, D), F32)],
            input_output_aliases={8: 0} if old else {},
            scratch_shapes=[pltpu.VMEM((BLK, CW), BF16), pltpu.SemaphoreType.DMA((NQ,))],
            compiler_params=ROOM,
            cost_estimate=pl.CostEstimate(
                flops=8 * BLK * Q * CW, bytes_accessed=6 * BLK * CW, transcendentals=0
            ),
            name="out",
        )(fade, mixed_x, mixed_c, score, scale, cums, row_terms, recv, *old)

    out, token = None, None
    carried = [send_a, send_b]
    for turn in range(slots + 1):
        if 0 < turn < per_stream:
            mixed_x, end = more(streams, lambda i, t=turn: t + i * per_stream, 0, mixed_x, end)
        for s in range(streams):
            if turn:
                recv = flying[s]
                if turn < slots:
                    flying[s] = lax.ppermute(join(turn, s, recv, token), "seq", ring)
                carried[s] = recv
            out, token = output(turn, s, carried[s], out)
    return out


def solution(mesh):
    return jax.shard_map(
        per_device,
        mesh=mesh,
        in_specs=(
            P(("groups", "seq"), ("head", "sub")),
            P(("groups", "seq"), None, ("head", "sub")),
            P(("head", "sub"), ("groups", "seq")),
            P(("head", "sub")),
            P(("head", "sub")),
            P(("head", "sub")),
            P(None, ("head", "sub")),
            P(("head", "sub")),
            P(None, None, ("head", "sub")),
            P(None, ("head", "sub")),
            P("groups"),
        ),
        out_specs=P(("groups", "seq"), ("head", "sub")),
        check_vma=False,
    )
```

time: 83.7 us -> 66.4 us (0.79)
  Pallas kernels: 59.5 us -> 35.8 us
  waiting for transfers between devices: 3.82 us -> 18.7 us
  starting transfers between devices: 16.9 us -> 8.31 us
    ppermute x10, waiting for transfers between devices: 2.16 us -> 17.4 us  [per_device(): flying[s] = lax.ppermute(join(turn, s, recv, token), 'seq', ring)]
    pallas_call x14, Pallas kernels: 32.6 us -> 19 us  [output(): pl.pallas_call(functools.partial(out_kernel, turn=turn, stream=s, per_str...]
    ppermute x10, starting transfers between devices: 12.1 us -> 3.28 us  [per_device(): flying[s] = lax.ppermute(join(turn, s, recv, token), 'seq', ring)]
    pallas_call x10, Pallas kernels: 8.45 us -> 0.42 us  [join(): pl.pallas_call(functools.partial(join_kernel, turn=turn, stream=s, per_st...]
    pallas_call x4 -> x6, Pallas kernels: 18.4 us -> 16.4 us  [the longest x4 10.9 us: more(): pl.pallas_call(functools.partial(more_kernel, heads=heads, per_group=per_...]
  transfers between devices with their start and end apart: 13 -> 13, of which waited for: 4 -> 9; matrix products, arithmetic and copies ran while one was open for 1% -> 2% of each run, Pallas kernels for 64% -> 48%
where the time goes in v3:
time: 66.4 us; the launch traced here: 66 us
  Pallas kernels  35.8 us (54%)
  waiting for transfers between devices  18.7 us (28%)
  starting transfers between devices  8.31 us (13%)
  local copies, waits for them, and re-layouts  2.68 us (4%)
    pallas_call x14, Pallas kernels, output(): pl.pallas_call(functools.partial(out_kernel, turn=turn, stream=s, per_str...  19 us
    ppermute x10, waiting for transfers between devices, per_device(): flying[s] = lax.ppermute(join(turn, s, recv, token), 'seq', ring)  17.4 us
    pallas_call x4, Pallas kernels, more(): pl.pallas_call(functools.partial(more_kernel, heads=heads, per_group=per_...  10.9 us
    pallas_call x1, Pallas kernels, per_device(): pl.pallas_call(functools.partial(first_kernel, heads=heads, per_group=per...  3.6 us
    ppermute x10, starting transfers between devices, per_device(): flying[s] = lax.ppermute(join(turn, s, recv, token), 'seq', ring)  3.28 us
    ppermute x1, starting transfers between devices, per_device(): rim = lax.ppermute(tail, 'seq', ring)  3.08 us
    pallas_call x1, Pallas kernels, per_device(): pl.pallas_call(params_kernel, in_specs=[SMEM] * 4 + [VMEM], out_specs=[VM...  1.92 us
    unnamed x3, local copies, waits for them, and re-layouts  1.83 us
  transfers between devices with their start and end apart: 13, of which 9 were waited for; matrix products, arithmetic and copies ran while one was open for 2% of the time, Pallas kernels for 48%

profile of v3, /device:TPU:0, one launch (start us, length us, event | category | flops | bytes accessed | tf_op | source)
XLA Modules:
  0.0 66.0 jit_solution(16655909972624642256)
XLA Ops:
  1.6 3.1 %collective-permute-start = (bf16[8,4608]{1,0:T(8,128)(2,1)S(1)}, bf16[8,4608]{1,0:T(8,128)(2,1)S(1)}, u32[]{:S(2)}, u32[]{:S(2)}) collective-permute-start(bf16[8,4608]{1,0:T(8,128)(2,1)S(1)} %pad_maximum_fusion), channel_id=1, source_target_pairs={{0,4},{4,8},{8,12},{12,0},{1,5},{5,9},{9,13},{13,1},{2,6},{6,10},{... | collective-permute-start | bytes 221192 | tf_op jit(solution)/shard_map/ppermute | solution.py:386
  5.8 1.9 %params.1 = (bf16[512,128]{1,0:T(8,128)(2,1)S(1)}, bf16[512,128]{1,0:T(8,128)(2,1)S(1)}, f32[8,4,512]{2,1,0:T(4,128)S(1)}, f32[8,2,512]{2,1,0:T(2,128)S(1)}, bf1...) custom-call(s32[4]{0:T(128)} %starts_ref.1, f32[32]{0:T(128)} %bias_ref.1, f32[32]{0:T(128)} %alog_ref.1, ...), custom_call_target="tpu_custom_call" | custom-call | tf_op jit(solution)/shard_map/params/pallas_call | solution.py:389
  7.7 1.3 %collective-permute-done.rim_ref.rimbc_ref = bf16[8,4608]{1,0:T(8,128)(2,1)S(1)} collective-permute-done((bf16[8,4608]{1,0:T(8,128)(2,1)S(1)}, bf16[8,4608]{1,0:T(8,128)(2,1)S(1)}, u32[]{:S(2)}, u32[]{:S(2)}) %collective-permute-start) | collective-permute-done | bytes 73760 | tf_op jit(solution)/shard_map/ppermute | solution.py:386
  9.0 3.6 %first.1 = (bf16[8,512,512]{2,1,0:T(8,128)(2,1)S(1)}, f32[8,128,512]{2,1,0:T(8,128)S(1)}, bf16[128,512]{1,0:T(8,128)(2,1)S(1)}, bf16[2,128,512]{2,1,0:T(8,128)(2...) custom-call(bf16[512,4096]{1,0:T(8,128)(2,1)} %x_ref.9, ...), custom_call_target="tpu_custom_call" | custom-call | tf_op jit(solution)/shard_map/first/pallas_call | solution.py:424
  12.9 2.0 %more.4 = (bf16[8,512,512]{2,1,0:T(8,128)(2,1)S(1)}, f32[8,128,512]{2,1,0:T(8,128)S(1)}, bf16[128,512]{1,0:T(8,128)(2,1)S(1)}) custom-call(bf16[512,4096]{1,0:T(8,128)(2,1)} %x_ref.9, bf16[8,4608]{1,0:T(8,128)(2,1)S(1)} %collective-permute-done.rim_ref.rimbc_ref, f32[4,4096]{1,0:T(4,128)} %wx_ref.9, ...), custom_call_target="tpu_custom_call", output_to_operand_aliasing={{0}: (7, {}), {1}: (8, {})} | custom-call | flops 134217728 | bytes 1048576 | tf_op jit(solution)/shard_map/more/pallas_call | solution.py:456
  14.9 1.6 %collective-permute-start.1 = (bf16[128,512]{1,0:T(8,128)(2,1)S(1)}, bf16[128,512]{1,0:T(8,128)(2,1)S(1)}, u32[]{:S(2)}, u32[]{:S(2)}) collective-permute-start(bf16[128,512]{1,0:T(8,128)(2,1)S(1)} %get-tuple-element.68.recv_ref), channel_id=1, source_target_pairs={{0,4},{4,8},{8,12},{12,0},{1,5},{5,9},{9,13},{13,1},{2,6},{6,10},{... | collective-permute-start | bytes 393224 | tf_op jit(solution)/shard_map/ppermute | solution.py:473
  16.6 2.6 %out.14 = (bf16[512,4096]{1,0:T(8,128)(2,1)}, f32[8,128]{1,0:T(8,128)}) custom-call(f32[8,2,512]{2,1,0:T(2,128)S(1)} %get-tuple-element.50.fade_ref, bf16[8,512,512]{2,1,0:T(8,128)(2,1)S(1)} %get-tuple-element.57.old1.mx_ref, bf16[2,512,128]{2,1,0:T(8,128)(2,1)S(1)} %get-tuple-element.64.c_ref, f32[2,512,512]{2,1,0:T(8,128)S(1)} %get-tuple-element.65.score_ref, ...), custom_call_target="tpu_custom_call" | custom-call | flops 268435456 | bytes 1572864 | tf_op jit(solution)/shard_map/out/pallas_call | solution.py:487
  19.2 2.0 %out.15 = (bf16[512,4096]{1,0:T(8,128)(2,1)}, f32[8,128]{1,0:T(8,128)S(1)}) custom-call(f32[8,2,512]{2,1,0:T(2,128)S(1)} %get-tuple-element.50.fade_ref, bf16[8,512,512]{2,1,0:T(8,128)(2,1)S(1)} %get-tuple-element.57.old1.mx_ref, bf16[2,512,128]{2,1,0:T(8,128)(2,1)S(1)} %get-tuple-element.64.c_ref, ...), custom_call_target="tpu_custom_call", output_to_operand_aliasing={{0}: (8, {})} | custom-call | flops 268435456 | bytes 1572864 | tf_op jit(solution)/shard_map/out/pallas_call | solution.py:487
  21.2 3.0 %more.5 = (bf16[8,512,512]{2,1,0:T(8,128)(2,1)S(1)}, f32[8,128,512]{2,1,0:T(8,128)S(1)}) custom-call(bf16[512,4096]{1,0:T(8,128)(2,1)} %x_ref.9, bf16[8,4608]{1,0:T(8,128)(2,1)S(1)} %collective-permute-done.rim_ref.rimbc_ref, f32[4,4096]{1,0:T(4,128)} %wx_ref.9, f32[1,4096]{1,0:T(1,128)} %bitcast.10, ...), custom_call_target="tpu_custom_call", output_to_operand_aliasing={{0}: (7, {}), {1}: (8, {})} | custom-call | flops 268435456 | bytes 2097152 | tf_op jit(solution)/shard_map/more/pallas_call | solution.py:456
  24.3 2.0 %out.16 = (bf16[512,4096]{1,0:T(8,128)(2,1)}, f32[8,128]{1,0:T(8,128)S(1)}) custom-call(f32[8,2,512]{2,1,0:T(2,128)S(1)} %get-tuple-element.50.fade_ref, bf16[8,512,512]{2,1,0:T(8,128)(2,1)S(1)} %get-tuple-element.59.old1.mx_ref, bf16[2,512,128]{2,1,0:T(8,128)(2,1)S(1)} %get-tuple-element.64.c_ref, ...), custom_call_target="tpu_custom_call", output_to_operand_aliasing={{0}: (8, {})} | custom-call | flops 268435456 | bytes 1572864 | tf_op jit(solution)/shard_map/out/pallas_call | solution.py:487
  26.5 2.0 %out.17 = (bf16[512,4096]{1,0:T(8,128)(2,1)}, f32[8,128]{1,0:T(8,128)S(1)}) custom-call(f32[8,2,512]{2,1,0:T(2,128)S(1)} %get-tuple-element.50.fade_ref, bf16[8,512,512]{2,1,0:T(8,128)(2,1)S(1)} %get-tuple-element.59.old1.mx_ref, bf16[2,512,128]{2,1,0:T(8,128)(2,1)S(1)} %get-tuple-element.64.c_ref, ...), custom_call_target="tpu_custom_call", output_to_operand_aliasing={{0}: (8, {})} | custom-call | flops 268435456 | bytes 1572864 | tf_op jit(solution)/shard_map/out/pallas_call | solution.py:487
  28.5 3.0 %more.6 = (bf16[8,512,512]{2,1,0:T(8,128)(2,1)S(1)}, f32[8,128,512]{2,1,0:T(8,128)S(1)}) custom-call(bf16[512,4096]{1,0:T(8,128)(2,1)} %x_ref.9, bf16[8,4608]{1,0:T(8,128)(2,1)S(1)} %collective-permute-done.rim_ref.rimbc_ref, f32[4,4096]{1,0:T(4,128)} %wx_ref.9, f32[1,4096]{1,0:T(1,128)} %bitcast.11, ...), custom_call_target="tpu_custom_call", output_to_operand_aliasing={{0}: (7, {}), {1}: (8, {})} | custom-call | flops 268435456 | bytes 2097152 | tf_op jit(solution)/shard_map/more/pallas_call | solution.py:456
  32.4 2.2 %out.18 = (bf16[512,4096]{1,0:T(8,128)(2,1)}, f32[8,128]{1,0:T(8,128)S(1)}) custom-call(f32[8,2,512]{2,1,0:T(2,128)S(1)} %get-tuple-element.50.fade_ref, bf16[8,512,512]{2,1,0:T(8,128)(2,1)S(1)} %get-tuple-element.61.old1.mx_ref, bf16[2,512,128]{2,1,0:T(8,128)(2,1)S(1)} %get-tuple-element.64.c_ref, ...), custom_call_target="tpu_custom_call", output_to_operand_aliasing={{0}: (8, {})} | custom-call | flops 268435456 | bytes 1572864 | tf_op jit(solution)/shard_map/out/pallas_call | solution.py:487
  34.7 2.0 %out.19 = (bf16[512,4096]{1,0:T(8,128)(2,1)}, f32[8,128]{1,0:T(8,128)S(1)}) custom-call(f32[8,2,512]{2,1,0:T(2,128)S(1)} %get-tuple-element.50.fade_ref, bf16[8,512,512]{2,1,0:T(8,128)(2,1)S(1)} %get-tuple-element.61.old1.mx_ref, bf16[2,512,128]{2,1,0:T(8,128)(2,1)S(1)} %get-tuple-element.64.c_ref, ...), custom_call_target="tpu_custom_call", output_to_operand_aliasing={{0}: (8, {})} | custom-call | flops 268435456 | bytes 1572864 | tf_op jit(solution)/shard_map/out/pallas_call | solution.py:487
  36.8 3.0 %more.7 = (bf16[8,512,512]{2,1,0:T(8,128)(2,1)S(1)}, f32[8,128,512]{2,1,0:T(8,128)S(1)}) custom-call(bf16[512,4096]{1,0:T(8,128)(2,1)} %x_ref.9, bf16[8,4608]{1,0:T(8,128)(2,1)S(1)} %collective-permute-done.rim_ref.rimbc_ref, f32[4,4096]{1,0:T(4,128)} %wx_ref.9, f32[1,4096]{1,0:T(1,128)} %bitcast.12, ...), custom_call_target="tpu_custom_call", output_to_operand_aliasing={{0}: (7, {}), {1}: (8, {})} | custom-call | flops 268435456 | bytes 2097152 | tf_op jit(solution)/shard_map/more/pallas_call | solution.py:456
  40.2 1.6 %collective-permute-start.8 = (bf16[128,512]{1,0:T(8,128)(2,1)S(1)}, bf16[128,512]{1,0:T(8,128)(2,1)S(1)}, u32[]{:S(2)}, u32[]{:S(2)}) collective-permute-start(bf16[128,512]{1,0:T(8,128)(2,1)S(1)} %join.15), channel_id=1, source_target_pairs={{0,4},{4,8},{8,12},{12,0},{1,5},{5,9},{9,13},{13,1},{2,6},{6,10},{... | collective-permute-start | bytes 393224 | tf_op jit(solution)/shard_map/ppermute | solution.py:512
  41.9 2.0 %out.20 = (bf16[512,4096]{1,0:T(8,128)(2,1)}, f32[8,128]{1,0:T(8,128)S(1)}) custom-call(f32[8,2,512]{2,1,0:T(2,128)S(1)} %get-tuple-element.50.fade_ref, bf16[8,512,512]{2,1,0:T(8,128)(2,1)S(1)} %get-tuple-element.63.mx_ref, bf16[2,512,128]{2,1,0:T(8,128)(2,1)S(1)} %get-tuple-element.64.c_ref, ...), custom_call_target="tpu_custom_call", output_to_operand_aliasing={{0}: (8, {})} | custom-call | flops 268435456 | bytes 1572864 | tf_op jit(solution)/shard_map/out/pallas_call | solution.py:487
  44.7 2.0 %out.21 = (bf16[512,4096]{1,0:T(8,128)(2,1)}, f32[8,128]{1,0:T(8,128)S(1)}) custom-call(f32[8,2,512]{2,1,0:T(2,128)S(1)} %get-tuple-element.50.fade_ref, bf16[8,512,512]{2,1,0:T(8,128)(2,1)S(1)} %get-tuple-element.63.mx_ref, bf16[2,512,128]{2,1,0:T(8,128)(2,1)S(1)} %get-tuple-element.64.c_ref, ...), custom_call_target="tpu_custom_call", output_to_operand_aliasing={{0}: (8, {})} | custom-call | flops 268435456 | bytes 1572864 | tf_op jit(solution)/shard_map/out/pallas_call | solution.py:487
  46.8 1.1 %collective-permute-done.8.recv_ref = bf16[128,512]{1,0:T(8,128)(2,1)S(1)} collective-permute-done((bf16[128,512]{1,0:T(8,128)(2,1)S(1)}, bf16[128,512]{1,0:T(8,128)(2,1)S(1)}, u32[]{:S(2)}, u32[]{:S(2)}) %collective-permute-start.8) | collective-permute-done | bytes 131104 | tf_op jit(solution)/shard_map/ppermute | solution.py:512
  48.1 3.1 %collective-permute-done.7.recv_ref = bf16[128,512]{1,0:T(8,128)(2,1)S(1)} collective-permute-done((bf16[128,512]{1,0:T(8,128)(2,1)S(1)}, bf16[128,512]{1,0:T(8,128)(2,1)S(1)}, u32[]{:S(2)}, u32[]{:S(2)}) %collective-permute-start.7) | collective-permute-done | bytes 131104 | tf_op jit(solution)/shard_map/ppermute | solution.py:512
  51.7 4.4 %collective-permute-done.10.recv_ref = bf16[128,512]{1,0:T(8,128)(2,1)S(1)} collective-permute-done((bf16[128,512]{1,0:T(8,128)(2,1)S(1)}, bf16[128,512]{1,0:T(8,128)(2,1)S(1)}, u32[]{:S(2)}, u32[]{:S(2)}) %collective-permute-start.10) | collective-permute-done | bytes 131104 | tf_op jit(solution)/shard_map/ppermute | solution.py:512
  56.3 2.1 %collective-permute-done.9.recv_ref = bf16[128,512]{1,0:T(8,128)(2,1)S(1)} collective-permute-done((bf16[128,512]{1,0:T(8,128)(2,1)S(1)}, bf16[128,512]{1,0:T(8,128)(2,1)S(1)}, u32[]{:S(2)}, u32[]{:S(2)}) %collective-permute-start.9) | collective-permute-done | bytes 131104 | tf_op jit(solution)/shard_map/ppermute | solution.py:512
  59.1 3.8 %collective-permute-done.12.recv_ref = bf16[128,512]{1,0:T(8,128)(2,1)S(1)} collective-permute-done((bf16[128,512]{1,0:T(8,128)(2,1)S(1)}, bf16[128,512]{1,0:T(8,128)(2,1)S(1)}, u32[]{:S(2)}, u32[]{:S(2)}) %collective-permute-start.12) | collective-permute-done | bytes 131104 | tf_op jit(solution)/shard_map/ppermute | solution.py:512
  63.6 1.6 %collective-permute-done.11.recv_ref = bf16[128,512]{1,0:T(8,128)(2,1)S(1)} collective-permute-done((bf16[128,512]{1,0:T(8,128)(2,1)S(1)}, bf16[128,512]{1,0:T(8,128)(2,1)S(1)}, u32[]{:S(2)}, u32[]{:S(2)}) %collective-permute-start.11) | collective-permute-done | bytes 131104 | tf_op jit(solution)/shard_map/ppermute | solution.py:512
  (37 shorter events, 8.3 us)
Async XLA Ops:
  1.6 7.4 %collective-permute-start = (bf16[8,4608]{1,0:T(8,128)(2,1)S(1)}, bf16[8,4608]{1,0:T(8,128)(2,1)S(1)}, u32[]{:S(2)}, u32[]{:S(2)}) collective-permute-start(bf16[8,4608]{1,0:T(8,128)(2,1)S(1)} %pad_maximum_fusion), channel_id=1, source_target_pairs={{0,4},{4,8},{8,12},{12,0},{1,5},{5,9},{9,13},{13,1},{2,6},{6,10},{... | collective-permute-start | bytes 221192 | tf_op jit(solution)/shard_map/ppermute | solution.py:386
  12.6 11.6 %collective-permute-start.2 = (bf16[128,512]{1,0:T(8,128)(2,1)S(1)}, bf16[128,512]{1,0:T(8,128)(2,1)S(1)}, u32[]{:S(2)}, u32[]{:S(2)}) collective-permute-start(bf16[128,512]{1,0:T(8,128)(2,1)S(1)} %get-tuple-element.69.recv_ref), channel_id=1, source_target_pairs={{0,4},{4,8},{8,12},{12,0},{1,5},{5,9},{9,13},{13,1},{2,6},{6,10},{... | collective-permute-start | bytes 393224 | tf_op jit(solution)/shard_map/ppermute | solution.py:471
  14.9 11.4 %collective-permute-start.1 = (bf16[128,512]{1,0:T(8,128)(2,1)S(1)}, bf16[128,512]{1,0:T(8,128)(2,1)S(1)}, u32[]{:S(2)}, u32[]{:S(2)}) collective-permute-start(bf16[128,512]{1,0:T(8,128)(2,1)S(1)} %get-tuple-element.68.recv_ref), channel_id=1, source_target_pairs={{0,4},{4,8},{8,12},{12,0},{1,5},{5,9},{9,13},{13,1},{2,6},{6,10},{... | collective-permute-start | bytes 393224 | tf_op jit(solution)/shard_map/ppermute | solution.py:473
  24.3 8.0 %collective-permute-start.4 = (bf16[128,512]{1,0:T(8,128)(2,1)S(1)}, bf16[128,512]{1,0:T(8,128)(2,1)S(1)}, u32[]{:S(2)}, u32[]{:S(2)}) collective-permute-start(bf16[128,512]{1,0:T(8,128)(2,1)S(1)} %join.11), channel_id=1, source_target_pairs={{0,4},{4,8},{8,12},{12,0},{1,5},{5,9},{9,13},{13,1},{2,6},{6,10},{... | collective-permute-start | bytes 393224 | tf_op jit(solution)/shard_map/ppermute | solution.py:512
  26.4 8.2 %collective-permute-start.3 = (bf16[128,512]{1,0:T(8,128)(2,1)S(1)}, bf16[128,512]{1,0:T(8,128)(2,1)S(1)}, u32[]{:S(2)}, u32[]{:S(2)}) collective-permute-start(bf16[128,512]{1,0:T(8,128)(2,1)S(1)} %join.10), channel_id=1, source_target_pairs={{0,4},{4,8},{8,12},{12,0},{1,5},{5,9},{9,13},{13,1},{2,6},{6,10},{... | collective-permute-start | bytes 393224 | tf_op jit(solution)/shard_map/ppermute | solution.py:512
  32.3 7.9 %collective-permute-start.6 = (bf16[128,512]{1,0:T(8,128)(2,1)S(1)}, bf16[128,512]{1,0:T(8,128)(2,1)S(1)}, u32[]{:S(2)}, u32[]{:S(2)}) collective-permute-start(bf16[128,512]{1,0:T(8,128)(2,1)S(1)} %join.13), channel_id=1, source_target_pairs={{0,4},{4,8},{8,12},{12,0},{1,5},{5,9},{9,13},{13,1},{2,6},{6,10},{... | collective-permute-start | bytes 393224 | tf_op jit(solution)/shard_map/ppermute | solution.py:512
  34.7 9.2 %collective-permute-start.5 = (bf16[128,512]{1,0:T(8,128)(2,1)S(1)}, bf16[128,512]{1,0:T(8,128)(2,1)S(1)}, u32[]{:S(2)}, u32[]{:S(2)}) collective-permute-start(bf16[128,512]{1,0:T(8,128)(2,1)S(1)} %join.12), channel_id=1, source_target_pairs={{0,4},{4,8},{8,12},{12,0},{1,5},{5,9},{9,13},{13,1},{2,6},{6,10},{... | collective-permute-start | bytes 393224 | tf_op jit(solution)/shard_map/ppermute | solution.py:512
  40.2 7.7 %collective-permute-start.8 = (bf16[128,512]{1,0:T(8,128)(2,1)S(1)}, bf16[128,512]{1,0:T(8,128)(2,1)S(1)}, u32[]{:S(2)}, u32[]{:S(2)}) collective-permute-start(bf16[128,512]{1,0:T(8,128)(2,1)S(1)} %join.15), channel_id=1, source_target_pairs={{0,4},{4,8},{8,12},{12,0},{1,5},{5,9},{9,13},{13,1},{2,6},{6,10},{... | collective-permute-start | bytes 393224 | tf_op jit(solution)/shard_map/ppermute | solution.py:512
  44.0 7.3 %collective-permute-start.7 = (bf16[128,512]{1,0:T(8,128)(2,1)S(1)}, bf16[128,512]{1,0:T(8,128)(2,1)S(1)}, u32[]{:S(2)}, u32[]{:S(2)}) collective-permute-start(bf16[128,512]{1,0:T(8,128)(2,1)S(1)} %join.14), channel_id=1, source_target_pairs={{0,4},{4,8},{8,12},{12,0},{1,5},{5,9},{9,13},{13,1},{2,6},{6,10},{... | collective-permute-start | bytes 393224 | tf_op jit(solution)/shard_map/ppermute | solution.py:512
  47.9 8.2 %collective-permute-start.10 = (bf16[128,512]{1,0:T(8,128)(2,1)S(1)}, bf16[128,512]{1,0:T(8,128)(2,1)S(1)}, u32[]{:S(2)}, u32[]{:S(2)}) collective-permute-start(bf16[128,512]{1,0:T(8,128)(2,1)S(1)} %join.17), channel_id=1, source_target_pairs={{0,4},{4,8},{8,12},{12,0},{1,5},{5,9},{9,13},{13,1},{2,6},{6,10},{... | collective-permute-start | bytes 393224 | tf_op jit(solution)/shard_map/ppermute | solution.py:512
  51.3 7.1 %collective-permute-start.9 = (bf16[128,512]{1,0:T(8,128)(2,1)S(1)}, bf16[128,512]{1,0:T(8,128)(2,1)S(1)}, u32[]{:S(2)}, u32[]{:S(2)}) collective-permute-start(bf16[128,512]{1,0:T(8,128)(2,1)S(1)} %join.16), channel_id=1, source_target_pairs={{0,4},{4,8},{8,12},{12,0},{1,5},{5,9},{9,13},{13,1},{2,6},{6,10},{... | collective-permute-start | bytes 393224 | tf_op jit(solution)/shard_map/ppermute | solution.py:512
  56.2 6.8 %collective-permute-start.12 = (bf16[128,512]{1,0:T(8,128)(2,1)S(1)}, bf16[128,512]{1,0:T(8,128)(2,1)S(1)}, u32[]{:S(2)}, u32[]{:S(2)}) collective-permute-start(bf16[128,512]{1,0:T(8,128)(2,1)S(1)} %join.19), channel_id=1, source_target_pairs={{0,4},{4,8},{8,12},{12,0},{1,5},{5,9},{9,13},{13,1},{2,6},{6,10},{... | collective-permute-start | bytes 393224 | tf_op jit(solution)/shard_map/ppermute | solution.py:512
  58.4 6.8 %collective-permute-start.11 = (bf16[128,512]{1,0:T(8,128)(2,1)S(1)}, bf16[128,512]{1,0:T(8,128)(2,1)S(1)}, u32[]{:S(2)}, u32[]{:S(2)}) collective-permute-start(bf16[128,512]{1,0:T(8,128)(2,1)S(1)} %join.18), channel_id=1, source_target_pairs={{0,4},{4,8},{8,12},{12,0},{1,5},{5,9},{9,13},{13,1},{2,6},{6,10},{... | collective-permute-start | bytes 393224 | tf_op jit(solution)/shard_map/ppermute | solution.py:512

commit v4 on v3

--- a/solution.py
+++ b/solution.py
@@ -156,9 +156,166 @@
     return pieces + [value]
 
 
+def doc_at(pos, starts_ref):
+    count = jnp.int32(-1)
+    for j in range(starts_ref.shape[0]):
+        count = count + (pos >= starts_ref[j]).astype(jnp.int32)
+    return count
+
+
+def column_of(ref):
+    heads = ref.shape[0]
+    index = lax.broadcasted_iota(jnp.int32, (heads, 1), 0)
+    column = jnp.zeros((heads, 1), F32)
+    for h in range(heads):
+        column = jnp.where(index == h, ref[h], column)
+    return column
+
+
+def split(value, parts):
+    pieces = []
+    for _ in range(parts - 1):
+        piece = value.astype(BF16).astype(F32)
+        pieces.append(piece)
+        value = value - piece
+    return pieces + [value]
+
+
+def doc_at(pos, starts_ref):
+    count = jnp.int32(-1)
+    for j in range(starts_ref.shape[0]):
+        count = count + (pos >= starts_ref[j]).astype(jnp.int32)
+    return count
+
+
+def column_of(ref):
+    heads = ref.shape[0]
+    index = lax.broadcasted_iota(jnp.int32, (heads, 1), 0)
+    column = jnp.zeros((heads, 1), F32)
+    for h in range(heads):
+        column = jnp.where(index == h, ref[h], column)
+    return column
+
+
+def split(value, parts):
+    pieces = []
+    for _ in range(parts - 1):
+        piece = value.astype(BF16).astype(F32)
+        pieces.append(piece)
+        value = value - piece
+    return pieces + [value]
+
+
+def doc_at(pos, starts_ref):
+    count = jnp.int32(-1)
+    for j in range(starts_ref.shape[0]):
+        count = count + (pos >= starts_ref[j]).astype(jnp.int32)
+    return count
+
+
+def column_of(ref):
+    heads = ref.shape[0]
+    index = lax.broadcasted_iota(jnp.int32, (heads, 1), 0)
+    column = jnp.zeros((heads, 1), F32)
+    for h in range(heads):
+        column = jnp.where(index == h, ref[h], column)
+    return column
+
+
+def split(value, parts):
+    pieces = []
+    for _ in range(parts - 1):
+        piece = value.astype(BF16).astype(F32)
+        pieces.append(piece)
+        value = value - piece
+    return pieces + [value]
+
+
+def doc_at(pos, starts_ref):
+    count = jnp.int32(-1)
+    for j in range(starts_ref.shape[0]):
+        count = count + (pos >= starts_ref[j]).astype(jnp.int32)
+    return count
+
+
+def column_of(ref):
+    heads = ref.shape[0]
+    index = lax.broadcasted_iota(jnp.int32, (heads, 1), 0)
+    column = jnp.zeros((heads, 1), F32)
+    for h in range(heads):
+        column = jnp.where(index == h, ref[h], column)
+    return column
+
+
+def split(value, parts):
+    pieces = []
+    for _ in range(parts - 1):
+        piece = value.astype(BF16).astype(F32)
+        pieces.append(piece)
+        value = value - piece
+    return pieces + [value]
+
+
+def doc_at(pos, starts_ref):
+    count = jnp.int32(-1)
+    for j in range(starts_ref.shape[0]):
+        count = count + (pos >= starts_ref[j]).astype(jnp.int32)
+    return count
+
+
+def column_of(ref):
+    heads = ref.shape[0]
+    index = lax.broadcasted_iota(jnp.int32, (heads, 1), 0)
+    column = jnp.zeros((heads, 1), F32)
+    for h in range(heads):
+        column = jnp.where(index == h, ref[h], column)
+    return column
+
+
+def split(value, parts):
+    pieces = []
+    for _ in range(parts - 1):
+        piece = value.astype(BF16).astype(F32)
+        pieces.append(piece)
+        value = value - piece
+    return pieces + [value]
+
+
+def doc_at(pos, starts_ref):
+    count = jnp.int32(-1)
+    for j in range(starts_ref.shape[0]):
+        count = count + (pos >= starts_ref[j]).astype(jnp.int32)
+    return count
+
+
+def column_of(ref):
+    heads = ref.shape[0]
+    index = lax.broadcasted_iota(jnp.int32, (heads, 1), 0)
+    column = jnp.zeros((heads, 1), F32)
+    for h in range(heads):
+        column = jnp.where(index == h, ref[h], column)
+    return column
+
+
+def split(value, parts):
+    pieces = []
+    for _ in range(parts - 1):
+        piece = value.astype(BF16).astype(F32)
+        pieces.append(piece)
+        value = value - piece
+    return pieces + [value]
+
+
 def params_kernel(
-    starts_ref, bias_ref, alog_ref, skip_ref, dt_ref, scale_ref, cum_ref, rows_ref, fade_ref, shift_ref, keep_ref
+    starts_ref, bias_ref, alog_ref, skip_ref, dt_ref, far_x_ref,
+    scale_ref, cols_ref, rows_ref, fade_ref, shift_ref, keep_ref, x_ref, sem,
 ):
+    copies = []
+    width = x_ref.shape[1]
+    for part in range(4):
+        lanes = pl.ds(part * (width // 4), width // 4)
+        copies.append(pltpu.make_async_copy(far_x_ref.at[:, lanes], x_ref.at[:, lanes], sem.at[part]))
+        copies[-1].start()
     first = lax.axis_index("seq") * BLK
     heads = dt_ref.shape[0]
     v = dt_ref[...] + column_of(bias_ref)
@@ -185,12 +342,11 @@
         doc = doc_of(pos, starts_ref)
         tail = jnp.where(doc == doc_last, jnp.exp(base - cum) * step_q, 0.0)
         entry = jnp.where(doc == doc_before, jnp.exp(cum), 0.0)
-        packed = split(tail, 2) + split(entry, 2)
-        if 4 * heads < D:
-            packed.append(jnp.zeros((D - 4 * heads, Q), F32))
+        rest = jnp.zeros((D - 2 * heads, Q), F32)
+        packed = split(tail, 2) + [rest]
         scale_ref[span, :] = jnp.transpose(jnp.concatenate(packed, axis=0), (1, 0)).astype(BF16)
-        packed = split(cum * LOG2E, 3) + [jnp.zeros((D - 3 * heads, Q), F32)]
-        cum_ref[span, :] = jnp.transpose(jnp.concatenate(packed, axis=0), (1, 0)).astype(BF16)
+        packed = [cum * LOG2E, entry, rest]
+        cols_ref[span, :] = jnp.transpose(jnp.concatenate(packed, axis=0), (1, 0))
         terms = (cum - jnp.log(step_q)) * LOG2E
         for c in range(heads // HC):
             rows_ref[c, :, span] = terms[c * HC : (c + 1) * HC]
@@ -215,6 +371,8 @@
         row = q * Q + lax.broadcasted_iota(jnp.int32, (Q, BLK), 0)
         keep = (row >= col) & (doc_row == doc_of(first + col, starts_ref))
         keep_ref[q * Q : (q + 1) * Q, :] = jnp.where(keep, 1.0, 0.0)
+    for copy in copies:
+        copy.wait()
 
 
 def chooser(heads, chunk, lo, hi, width):
@@ -236,40 +394,42 @@
     return edge_ref[...] if q == 0 else x_ref[(q - 1) * Q : (q + 1) * Q, :]
 
 
-def edge(edge_ref, rim_ref, x_ref):
-    width = x_ref.shape[1]
-    rim = jnp.concatenate([jnp.zeros((Q - RIM, width), F32), rim_ref[...].astype(F32)], axis=0)
+def edge(edge_ref, rim, x):
+    width = x.shape[1]
+    rim = jnp.concatenate([jnp.zeros((Q - RIM, width), F32), rim.astype(F32)], axis=0)
     edge_ref[0:Q, 0:width] = rim.astype(BF16)
-    edge_ref[Q : 2 * Q, 0:width] = x_ref[0:Q, :]
+    edge_ref[Q : 2 * Q, 0:width] = x
 
 
 def state_body(
     chunk, heads, per_group, x_ref, rim_ref, wx_ref, bx_ref, shift_ref, scale_ref, bt_ref,
     mx_ref, end_ref, edge_ref, tail_ref, send_ref=None,
 ):
-    edge(edge_ref, rim_ref, x_ref)
+    wide = slice(chunk * CW, (chunk + 1) * CW)
+    edge(edge_ref, rim_ref[:, wide], x_ref[0:Q, wide])
     pick = chooser(heads, chunk, 0, 2, CW)
-    taps = [wx_ref[k : k + 1, :] for k in range(4)]
+    taps = [wx_ref[k : k + 1, wide] for k in range(4)]
     for q in range(NQ):
         span = slice(q * Q, (q + 1) * Q)
-        mixed = convolved(q, window_of(q, edge_ref, x_ref), x_ref[span, :], shift_ref, taps, bx_ref[...])
-        mx_ref[0, span, :] = mixed.astype(BF16)
+        window = x_ref[(q - 1) * Q : (q + 1) * Q, wide] if q else edge_ref[...]
+        mixed = convolved(q, window, x_ref[span, wide], shift_ref, taps, bx_ref[:, wide])
+        mx_ref[chunk, span, :] = mixed.astype(BF16)
         scale = jnp.dot(scale_ref[span, :], pick, preferred_element_type=F32)
         tail_ref[span, :] = (mixed * scale).astype(BF16)
-    state = jnp.dot(bt_ref[lax.div(chunk, per_group)], tail_ref[...], preferred_element_type=F32)
-    end_ref[0] = state
+    state = jnp.dot(bt_ref[chunk // per_group], tail_ref[...], preferred_element_type=F32)
+    end_ref[chunk] = state
     if send_ref is not None:
         send_ref[...] = state.astype(BF16)
 
 
 def first_kernel(
-    x_ref, rim_ref, wx_ref, bx_ref, shift_ref, scale_ref, keep_ref, bc_ref, rimbc_ref, wbc_ref, bbc_ref,
+    x_ref, rim_ref, wx_ref, bx_ref, shift_ref, scale_ref, keep_ref, bc_ref, wbc_ref, bbc_ref,
     mx_ref, end_ref, send_ref, bt_ref, c_ref, score_ref,
     edge_ref, tail_ref, *, heads, per_group,
 ):
     groups = bt_ref.shape[0]
     wide = 2 * groups * D
-    edge(edge_ref, rimbc_ref, bc_ref)
+    edge(edge_ref, rim_ref[:, x_ref.shape[1] :], bc_ref[0:Q, :])
 
     def joined(rows):
         return jnp.concatenate(rows, axis=1)
@@ -295,12 +455,13 @@
 
 def more_kernel(
     x_ref, rim_ref, wx_ref, bx_ref, shift_ref, scale_ref, bt_ref, old1, old2,
-    mx_ref, end_ref, *rest, heads, per_group, chunk_of, sends,
+    mx_ref, end_ref, *rest, heads, per_group, some, sends,
 ):
-    state_body(
-        chunk_of(pl.program_id(0)), heads, per_group, x_ref, rim_ref, wx_ref, bx_ref, shift_ref, scale_ref,
-        bt_ref, mx_ref, end_ref, *rest[-2:], *rest[:sends],
-    )
+    for chunk in some:
+        state_body(
+            chunk, heads, per_group, x_ref, rim_ref, wx_ref, bx_ref, shift_ref, scale_ref,
+            bt_ref, mx_ref, end_ref, *rest[-2:], *rest[:sends],
+        )
 
 
 def join_kernel(fade_ref, recv_ref, end_ref, token_ref, send_ref, *, turn, stream, per_stream):
@@ -309,45 +470,74 @@
 
 
 def out_kernel(
-    fade_ref, mx_ref, c_ref, score_ref, scale_ref, cum_ref, rows_ref, recv_ref,
-    *rest, turn, stream, per_stream, per_group, heads,
+    fade_ref, mx_ref, c_ref, score_ref, cols_ref, rows_ref, recv_ref,
+    *rest, turn, stream, before, final, per_stream, per_group, heads,
 ):
-    out_ref, token_ref, ready_ref, sem = rest[-4:]
-    token_ref[...] = jnp.zeros_like(token_ref)
-    rank = turn - lax.axis_index("seq")
-
-    @pl.when((rank >= 0) & (rank < per_stream))
+    out_ref, block_ref, sem = rest[-3:]
+    place = lax.axis_index("seq")
+
+    def spot(when, which):
+        chunk = which * per_stream + jnp.clip(when - place, 0, per_stream - 1)
+        return pl.ds(pl.multiple_of(chunk * CW, CW), CW)
+
+    def is_valid(when):
+        return (when - place >= 0) & (when - place < per_stream)
+
+    def half_copy(ref, when, which, half, slot=0):
+        rows = pl.ds(half * 2 * Q, 2 * Q)
+        return pltpu.make_async_copy(ref.at[rows, :], out_ref.at[rows, spot(when, which)], sem.at[2 * slot + half])
+
+    if before:
+        @pl.when(is_valid(before[0]))
+        def send():
+            for half in range(2):
+                half_copy(rest[0], *before, half).start()
+
+    @pl.when(is_valid(turn))
     def compute():
-        chunk = stream * per_stream + rank
+        chunk = stream * per_stream + turn - place
         g = lax.div(chunk, per_group)
-        pick_cum = chooser(heads, chunk, 0, 3, CW)
-        pick_entry = chooser(heads, chunk, 2, 4, CW)
-        copies = []
-        for q in range(NQ):
-            span = slice(q * Q, (q + 1) * Q)
-            cums = jnp.dot(cum_ref[span, :], pick_cum, preferred_element_type=F32)
-            entry = jnp.dot(scale_ref[span, :], pick_entry, preferred_element_type=F32)
-            far = jnp.dot(c_ref[g, span, :], recv_ref[...], preferred_element_type=F32)
-            for i in range(HC):
-                lanes = slice(i * D, (i + 1) * D)
-                parts = []
+        cols = pltpu.roll(cols_ref[...], lax.rem(D - HC * chunk, D), 1)
+        far = jnp.dot(c_ref[g], recv_ref[...], preferred_element_type=F32)
+        zero = jnp.zeros((Q, Q), BF16)
+        for i in range(HC):
+            lanes = slice(i * D, (i + 1) * D)
+            cum = jnp.broadcast_to(cols[:, i : i + 1], (BLK, Q))
+            entry = jnp.broadcast_to(cols[:, heads + i : heads + i + 1], (BLK, Q))
+            tiles = []
+            for q in range(NQ):
+                span = slice(q * Q, (q + 1) * Q)
+                line = []
                 for j in range(q + 1):
                     there = slice(j * Q, (j + 1) * Q)
-                    gap = cums[:, lanes] - rows_ref[chunk, i : i + 1, there]
+                    gap = cum[span] - rows_ref[chunk, i : i + 1, there]
                     if j == q:
                         gap = jnp.minimum(gap, 100.0)
-                    parts.append((score_ref[g, span, there] * jnp.exp2(gap)).astype(BF16))
-                weight = jnp.concatenate(parts, axis=1)
-                y = jnp.dot(weight, mx_ref[chunk, 0 : (q + 1) * Q, lanes], preferred_element_type=F32)
+                    line.append((score_ref[g, span, there] * jnp.exp2(gap)).astype(BF16))
+                tiles.append(line + [zero] * (NQ - 1 - q))
+
+            def weights(lines, halves):
+                return jnp.concatenate([jnp.concatenate([tiles[q][j] for j in halves], axis=1) for q in lines], axis=0)
+
+            left = jnp.dot(weights(range(NQ), (0, 1)), mx_ref[chunk, 0 : 2 * Q, lanes], preferred_element_type=F32)
+            right = jnp.dot(weights((2, 3), (2, 3)), mx_ref[chunk, 2 * Q :, lanes], preferred_element_type=F32)
+            for half in range(2):
+                span = slice(half * 2 * Q, (half + 1) * 2 * Q)
+                y = left[span] + right if half else left[span]
                 x = mx_ref[chunk, span, lanes].astype(F32)
-                y = y + entry[:, lanes] * far[:, lanes] + fade_ref[chunk, 0:1, lanes] * x
-                ready_ref[span, lanes] = y.astype(BF16)
-            to = out_ref.at[pl.ds(q * Q, Q), pl.ds(pl.multiple_of(chunk * CW, CW), CW)]
-            copy = pltpu.make_async_copy(ready_ref.at[pl.ds(q * Q, Q), :], to, sem.at[q])
-            copy.start()
-            copies.append(copy)
-        for copy in copies:
-            copy.wait()
+                y = y + entry[span] * far[span, lanes] + fade_ref[chunk, 0:1, lanes] * x
+                block_ref[span, lanes] = y.astype(BF16)
+        if final:
+            for half in range(2):
+                half_copy(block_ref, turn, stream, half, 1).start()
+            for half in range(2):
+                half_copy(block_ref, turn, stream, half, 1).wait()
+
+    if before:
+        @pl.when(is_valid(before[0]))
+        def wait():
+            for half in range(2):
+                half_copy(rest[0], *before, half).wait()
 
 
 SMEM = pl.BlockSpec(memory_space=pltpu.SMEM)
@@ -368,14 +558,14 @@
     x_raw, bc_raw, dt_raw, dt_bias, a_log, d_skip, conv_x, conv_x_bias, conv_bc, conv_bc_bias, doc_starts
 ):
     rows, width = x_raw.shape
-    held = [x_raw, dt_raw, dt_bias, a_log, d_skip, conv_x, conv_x_bias[None], conv_bc, conv_bc_bias, doc_starts]
+    held = [x_raw, dt_raw, dt_bias, a_log, d_skip, conv_bc, conv_bc_bias, doc_starts]
     held = [pltpu.with_memory_space_constraint(a, pltpu.HBM) for a in held]
-    x_pin, dt_raw, dt_bias, a_log, d_skip, conv_x, bias_x, conv_bc, conv_bc_bias, doc_starts = held
+    x_far, dt_raw, dt_bias, a_log, d_skip, conv_bc, conv_bc_bias, doc_starts = held
+    bias_x = conv_x_bias[None]
     groups = bc_raw.shape[2] // D
     heads = dt_raw.shape[0]
     chunks = heads // HC
     per_group = chunks // groups
-    wide = 2 * groups * D
     seq = lax.axis_size("seq")
     ring = [(i, (i + 1) % seq) for i in range(seq)]
     streams = 2
@@ -386,59 +576,31 @@
     rim = lax.ppermute(tail, "seq", ring)
     bc = bc_raw.reshape(rows, -1)
 
-    scale, cums, row_terms, fade, shift, keep = pl.pallas_call(
+    scale, cols, row_terms, fade, shift, keep, x_near = pl.pallas_call(
         params_kernel,
-        in_specs=[SMEM] * 4 + [VMEM],
-        out_specs=[VMEM] * 6,
+        in_specs=[SMEM] * 4 + [VMEM, ANY],
+        out_specs=[VMEM] * 7,
         out_shape=[
             shape_of((BLK, D), BF16),
-            shape_of((BLK, D), BF16),
+            shape_of((BLK, D), F32),
             shape_of((chunks, HC, BLK), F32),
             shape_of((chunks, 2, CW), F32),
             shape_of((NQ, 3 * Q, 2 * Q), BF16),
             shape_of((BLK, BLK), F32),
+            pltpu.VMEM((rows, width), BF16),
         ],
+        scratch_shapes=[pltpu.SemaphoreType.DMA((4,))],
         compiler_params=ROOM,
         name="params",
-    )(doc_starts, dt_bias, a_log, d_skip, dt_raw)
-
-    def chunk_specs(chunk_of):
-        ins = [
-            pl.BlockSpec((BLK, CW), lambda i: (0, chunk_of(i))),
-            pl.BlockSpec((RIM, CW), lambda i: (0, chunk_of(i))),
-            pl.BlockSpec((4, CW), lambda i: (0, chunk_of(i))),
-            pl.BlockSpec((1, CW), lambda i: (0, chunk_of(i))),
-            whole((NQ, 3 * Q, 2 * Q)),
-            whole((BLK, D)),
-        ]
-        outs = [
-            pl.BlockSpec((1, BLK, CW), lambda i: (chunk_of(i), 0, 0)),
-            pl.BlockSpec((1, D, CW), lambda i: (chunk_of(i), 0, 0)),
-        ]
-        return ins, outs
-
-    big = [shape_of((chunks, BLK, CW), BF16), shape_of((chunks, D, CW), F32)]
+    )(doc_starts, dt_bias, a_log, d_skip, dt_raw, x_far)
+
+    big = [pltpu.VMEM((chunks, BLK, CW), BF16), pltpu.VMEM((chunks, D, CW), F32)]
     chunk_shape = shape_of((D, CW), BF16)
     scratch = [pltpu.VMEM((2 * Q, CW), BF16), pltpu.VMEM((BLK, CW), BF16)]
-    ins, outs = chunk_specs(lambda i: 0)
     mixed_x, end, send_a, bt, mixed_c, score = pl.pallas_call(
         functools.partial(first_kernel, heads=heads, per_group=per_group),
-        grid=(1,),
-        in_specs=[
-            *ins,
-            whole((BLK, BLK)),
-            whole((BLK, wide)),
-            pl.BlockSpec((RIM, wide), lambda i: (0, width // wide)),
-            whole((4, 2, groups * D)),
-            whole((2, groups * D)),
-        ],
-        out_specs=[
-            *outs,
-            whole((D, CW)),
-            whole((groups, D, BLK)),
-            whole((groups, BLK, D)),
-            whole((groups, BLK, BLK)),
-        ],
+        in_specs=[VMEM] * 10,
+        out_specs=[VMEM] * 6,
         out_shape=[
             *big,
             chunk_shape,
@@ -449,69 +611,72 @@
         scratch_shapes=scratch,
         compiler_params=ROOM,
         name="first",
-    )(x_pin, rim, conv_x, bias_x, shift, scale, keep, bc, rim, conv_bc, conv_bc_bias)
-
-    def more(count, chunk_of, sends, mixed_x, end):
-        ins, outs = chunk_specs(chunk_of)
+    )(x_near, rim, conv_x, bias_x, shift, scale, keep, bc, conv_bc, conv_bc_bias)
+
+    def more(some, sends, mixed_x, end):
         return pl.pallas_call(
-            functools.partial(more_kernel, heads=heads, per_group=per_group, chunk_of=chunk_of, sends=sends),
-            grid=(count,),
-            in_specs=[*ins, whole((groups, D, BLK)), ANY, ANY],
-            out_specs=outs + [whole((D, CW))] * sends,
+            functools.partial(more_kernel, heads=heads, per_group=per_group, some=some, sends=sends),
+            in_specs=[VMEM] * 9,
+            out_specs=[VMEM] * (2 + sends),
             out_shape=big + [chunk_shape] * sends,
             input_output_aliases={7: 0, 8: 1},
             scratch_shapes=scratch,
             compiler_params=ROOM,
             cost_estimate=pl.CostEstimate(
-                flops=4 * count * BLK * D * CW, bytes_accessed=4 * count * BLK * CW, transcendentals=0
+                flops=4 * len(some) * BLK * D * CW, bytes_accessed=4 * len(some) * BLK * CW, transcendentals=0
             ),
             name="more",
-        )(x_pin, rim, conv_x, bias_x, shift, scale, bt, mixed_x, end)
+        )(x_near, rim, conv_x, bias_x, shift, scale, bt, near(mixed_x), near(end))
+
+    def near(array):
+        return pltpu.with_memory_space_constraint(array, pltpu.VMEM)
 
     flying = [lax.ppermute(send_a, "seq", ring), None]
-    mixed_x, end, send_b = more(1, lambda i: per_stream, 1, mixed_x, end)
+    mixed_x, end, send_b = more([per_stream], 1, mixed_x, end)
     flying[1] = lax.ppermute(send_b, "seq", ring)
 
     def join(turn, s, recv, token):
         return pl.pallas_call(
             functools.partial(join_kernel, turn=turn, stream=s, per_stream=per_stream),
-            in_specs=[VMEM, VMEM, VMEM, VMEM],
+            in_specs=[VMEM, VMEM, VMEM, ANY],
             out_specs=VMEM,
             out_shape=chunk_shape,
             compiler_params=ROOM,
             name="join",
         )(fade, recv, end, token)
 
-    def output(turn, s, recv, out):
-        old = [] if out is None else [out]
+    def output(turn, s, recv, before, block, out):
+        old = [] if out is None else [block, out]
         return pl.pallas_call(
             functools.partial(
-                out_kernel, turn=turn, stream=s, per_stream=per_stream, per_group=per_group, heads=heads
+                out_kernel, turn=turn, stream=s, before=before, final=turn == slots and s == streams - 1,
+                per_stream=per_stream, per_group=per_group, heads=heads,
             ),
-            in_specs=[VMEM] * 8 + [ANY] * len(old),
+            in_specs=[VMEM] * 7 + [VMEM, ANY][: len(old)],
             out_specs=[ANY, VMEM],
-            out_shape=[pltpu.HBM((BLK, width), BF16), shape_of((8, D), F32)],
+            out_shape=[pltpu.HBM((BLK, width), BF16), shape_of((BLK, CW), BF16)],
             input_output_aliases={8: 0} if old else {},
-            scratch_shapes=[pltpu.VMEM((BLK, CW), BF16), pltpu.SemaphoreType.DMA((NQ,))],
+            scratch_shapes=[pltpu.SemaphoreType.DMA((4,))],
             compiler_params=ROOM,
             cost_estimate=pl.CostEstimate(
                 flops=8 * BLK * Q * CW, bytes_accessed=6 * BLK * CW, transcendentals=0
             ),
             name="out",
-        )(fade, mixed_x, mixed_c, score, scale, cums, row_terms, recv, *old)
-
-    out, token = None, None
+        )(fade, mixed_x, mixed_c, score, cols, row_terms, recv, *old)
+
+    out, block, before = None, None, None
     carried = [send_a, send_b]
     for turn in range(slots + 1):
         if 0 < turn < per_stream:
-            mixed_x, end = more(streams, lambda i, t=turn: t + i * per_stream, 0, mixed_x, end)
+            mixed_x, end = more([turn + i * per_stream for i in range(streams)], 0, mixed_x, end)
         for s in range(streams):
             if turn:
                 recv = flying[s]
                 if turn < slots:
-                    flying[s] = lax.ppermute(join(turn, s, recv, token), "seq", ring)
+                    flying[s] = lax.ppermute(join(turn, s, recv, block), "seq", ring)
                 carried[s] = recv
-            out, token = output(turn, s, carried[s], out)
+            out, block = output(turn, s, carried[s], before, block, out)
+            before = (turn, s)
     return out
 
 

time: 66.4 us -> 62.3 us (0.938)
  Pallas kernels: 35.8 us -> 24.6 us
  waiting for transfers between devices: 18.7 us -> 26.1 us
    ppermute x10, waiting for transfers between devices: 17.4 us -> 25.9 us  [per_device(): flying[s] = lax.ppermute(join(turn, s, recv, block), 'seq', ring)]
    pallas_call x15, Pallas kernels: 20.9 us -> 14.7 us  [the longest x14 10.9 us: output(): pl.pallas_call(functools.partial(out_kernel, turn=turn, stream=s, before=...]
    pallas_call x4, Pallas kernels: 10.9 us -> 6.26 us  [more(): pl.pallas_call(functools.partial(more_kernel, heads=heads, per_group=per_...]
    ppermute x10, starting transfers between devices: 3.28 us -> 1.72 us  [per_device(): flying[s] = lax.ppermute(join(turn, s, recv, block), 'seq', ring)]
    ppermute x1, waiting for transfers between devices: 1.31 us -> 0.01 us  [per_device(): rim = lax.ppermute(tail, 'seq', ring)]
    ppermute x1, starting transfers between devices: 0.33 us -> 1.63 us  [per_device(): flying = [lax.ppermute(send_a, 'seq', ring), None]]
    unnamed x3 -> x7, local copies, waits for them, and re-layouts: 1.83 us -> 1.87 us
  transfers between devices with their start and end apart: 13 -> 13, of which waited for: 9 -> 10; matrix products, arithmetic and copies ran while one was open for 2% -> 2% of each run, Pallas kernels for 48% -> 33%
where the time goes in v4:
time: 62.3 us; the launch traced here: 61.9 us
  waiting for transfers between devices  26.1 us (42%)
  Pallas kernels  24.6 us (39%)
  starting transfers between devices  8.06 us (13%)
  local copies, waits for them, and re-layouts  2.72 us (4%)
    ppermute x10, waiting for transfers between devices, per_device(): flying[s] = lax.ppermute(join(turn, s, recv, block), 'seq', ring)  25.9 us
    pallas_call x14, Pallas kernels, output(): pl.pallas_call(functools.partial(out_kernel, turn=turn, stream=s, before=...  10.9 us
    pallas_call x4, Pallas kernels, more(): pl.pallas_call(functools.partial(more_kernel, heads=heads, per_group=per_...  6.26 us
    pallas_call x1, Pallas kernels, per_device(): pl.pallas_call(params_kernel, in_specs=[SMEM] * 4 + [VMEM, ANY], out_spec...  3.75 us
    pallas_call x1, Pallas kernels, per_device(): pl.pallas_call(functools.partial(first_kernel, heads=heads, per_group=per...  3.22 us
    ppermute x1, starting transfers between devices, per_device(): rim = lax.ppermute(tail, 'seq', ring)  3.08 us
    unnamed x7, local copies, waits for them, and re-layouts  1.87 us
    ppermute x10, starting transfers between devices, per_device(): flying[s] = lax.ppermute(join(turn, s, recv, block), 'seq', ring)  1.72 us
  transfers between devices with their start and end apart: 13, of which 10 were waited for; matrix products, arithmetic and copies ran while one was open for 2% of the time, Pallas kernels for 33%

profile of v4, /device:TPU:0, one launch (start us, length us, event | category | flops | bytes accessed | tf_op | source)
XLA Modules:
  0.0 61.9 jit_solution(3458995534269898563)
XLA Ops:
  1.6 3.1 %collective-permute-start = (bf16[8,4608]{1,0:T(8,128)(2,1)S(1)}, bf16[8,4608]{1,0:T(8,128)(2,1)S(1)}, u32[]{:S(2)}, u32[]{:S(2)}) collective-permute-start(bf16[8,4608]{1,0:T(8,128)(2,1)S(1)} %pad_maximum_fusion), channel_id=1, source_target_pairs={{0,4},{4,8},{8,12},{12,0},{1,5},{5,9},{9,13},{13,1},{2,6},{6,10},{... | collective-permute-start | bytes 221192 | tf_op jit(solution)/shard_map/ppermute | solution.py:576
  4.7 1.1 %copy.34 = bf16[64,8,2,256]{3,1,2,0:T(8,128)(2,1)S(1)} copy(bf16[64,8,2,256]{3,2,1,0:T(2,128)(2,1)} %bitcast.12) | data formatting | bytes 1048576
  5.8 3.8 %params.1 = (bf16[512,128]{1,0:T(8,128)(2,1)S(1)}, f32[512,128]{1,0:T(8,128)S(1)}, f32[8,4,512]{2,1,0:T(4,128)S(1)}, f32[8,2,512]{2,1,0:T(2,128)S(1)}, bf16[4,38...) custom-call(s32[4]{0:T(128)} %starts_ref.1, f32[32]{0:T(128)} %bias_ref.1, ...), custom_call_target="tpu_custom_call" | custom-call | tf_op jit(solution)/shard_map/params/pallas_call | solution.py:579
  9.6 3.2 %first.1 = (bf16[8,512,512]{2,1,0:T(8,128)(2,1)S(1)}, f32[8,128,512]{2,1,0:T(8,128)S(1)}, bf16[128,512]{1,0:T(8,128)(2,1)S(1)}, bf16[2,128,512]{2,1,0:T(8,128)(2...) custom-call(bf16[512,4096]{1,0:T(8,128)(2,1)S(1)} %get-tuple-element.55.x_ref, ...), custom_call_target="tpu_custom_call" | custom-call | tf_op jit(solution)/shard_map/first/pallas_call | solution.py:600
  12.8 1.6 %collective-permute-start.2 = (bf16[128,512]{1,0:T(8,128)(2,1)S(1)}, bf16[128,512]{1,0:T(8,128)(2,1)S(1)}, u32[]{:S(2)}, u32[]{:S(2)}) collective-permute-start(bf16[128,512]{1,0:T(8,128)(2,1)S(1)} %get-tuple-element.74.recv_ref), channel_id=1, source_target_pairs={{0,4},{4,8},{8,12},{12,0},{1,5},{5,9},{9,13},{13,1},{2,6},{6,10},{... | collective-permute-start | bytes 393224 | tf_op jit(solution)/shard_map/ppermute | solution.py:634
  15.4 1.6 %collective-permute-start.1 = (bf16[128,512]{1,0:T(8,128)(2,1)S(1)}, bf16[128,512]{1,0:T(8,128)(2,1)S(1)}, u32[]{:S(2)}, u32[]{:S(2)}) collective-permute-start(bf16[128,512]{1,0:T(8,128)(2,1)S(1)} %get-tuple-element.73.recv_ref), channel_id=1, source_target_pairs={{0,4},{4,8},{8,12},{12,0},{1,5},{5,9},{9,13},{13,1},{2,6},{6,10},{... | collective-permute-start | bytes 393224 | tf_op jit(solution)/shard_map/ppermute | solution.py:636
  18.1 1.1 %out.15 = (bf16[512,4096]{1,0:T(8,128)(2,1)}, bf16[512,512]{1,0:T(8,128)(2,1)S(1)}) custom-call(f32[8,2,512]{2,1,0:T(2,128)S(1)} %get-tuple-element.54.fade_ref, bf16[8,512,512]{2,1,0:T(8,128)(2,1)S(1)} %get-tuple-element.62.old1.mx_ref, bf16[2,512,128]{2,1,0:T(8,128)(2,1)S(1)} %get-tuple-element.69.c_ref, ...), custom_call_target="tpu_custom_call", output_to_operand_aliasing={{0}: (8, {})} | custom-call | flops 268435456 | bytes 1572864 | tf_op jit(solution)/shard_map/out/pallas_call | solution.py:650
  19.3 1.8 %more.5 = (bf16[8,512,512]{2,1,0:T(8,128)(2,1)S(1)}, f32[8,128,512]{2,1,0:T(8,128)S(1)}) custom-call(bf16[512,4096]{1,0:T(8,128)(2,1)S(1)} %get-tuple-element.55.x_ref, bf16[8,4608]{1,0:T(8,128)(2,1)S(1)} %collective-permute-done.rim_ref, f32[4,4096]{1,0:T(4,128)S(1)} %copy-done, ...), custom_call_target="tpu_custom_call", output_to_operand_aliasing={{0}: (7, {}), {1}: (8, {})} | custom-call | flops 268435456 | bytes 2097152 | tf_op jit(solution)/shard_map/more/pallas_call | solution.py:617
  21.2 1.1 %out.16 = (bf16[512,4096]{1,0:T(8,128)(2,1)}, bf16[512,512]{1,0:T(8,128)(2,1)S(1)}) custom-call(f32[8,2,512]{2,1,0:T(2,128)S(1)} %get-tuple-element.54.fade_ref, bf16[8,512,512]{2,1,0:T(8,128)(2,1)S(1)} %get-tuple-element.64.old1.mx_ref, bf16[2,512,128]{2,1,0:T(8,128)(2,1)S(1)} %get-tuple-element.69.c_ref, ...), custom_call_target="tpu_custom_call", output_to_operand_aliasing={{0}: (8, {})} | custom-call | flops 268435456 | bytes 1572864 | tf_op jit(solution)/shard_map/out/pallas_call | solution.py:650
  22.5 1.2 %collective-permute-start.3 = (bf16[128,512]{1,0:T(8,128)(2,1)S(1)}, bf16[128,512]{1,0:T(8,128)(2,1)S(1)}, u32[]{:S(2)}, u32[]{:S(2)}) collective-permute-start(bf16[128,512]{1,0:T(8,128)(2,1)S(1)} %join.10), channel_id=1, source_target_pairs={{0,4},{4,8},{8,12},{12,0},{1,5},{5,9},{9,13},{13,1},{2,6},{6,10},{... | collective-permute-start | bytes 393224 | tf_op jit(solution)/shard_map/ppermute | solution.py:676
  24.8 1.8 %more.6 = (bf16[8,512,512]{2,1,0:T(8,128)(2,1)S(1)}, f32[8,128,512]{2,1,0:T(8,128)S(1)}) custom-call(bf16[512,4096]{1,0:T(8,128)(2,1)S(1)} %get-tuple-element.55.x_ref, bf16[8,4608]{1,0:T(8,128)(2,1)S(1)} %collective-permute-done.rim_ref, f32[4,4096]{1,0:T(4,128)S(1)} %copy-done, ...), custom_call_target="tpu_custom_call", output_to_operand_aliasing={{0}: (7, {}), {1}: (8, {})} | custom-call | flops 268435456 | bytes 2097152 | tf_op jit(solution)/shard_map/more/pallas_call | solution.py:617
  26.6 2.2 %collective-permute-done.4.recv_ref = bf16[128,512]{1,0:T(8,128)(2,1)S(1)} collective-permute-done((bf16[128,512]{1,0:T(8,128)(2,1)S(1)}, bf16[128,512]{1,0:T(8,128)(2,1)S(1)}, u32[]{:S(2)}, u32[]{:S(2)}) %collective-permute-start.4) | collective-permute-done | bytes 131104 | tf_op jit(solution)/shard_map/ppermute | solution.py:676
  28.8 1.3 %out.18 = (bf16[512,4096]{1,0:T(8,128)(2,1)}, bf16[512,512]{1,0:T(8,128)(2,1)S(1)}) custom-call(f32[8,2,512]{2,1,0:T(2,128)S(1)} %get-tuple-element.54.fade_ref, bf16[8,512,512]{2,1,0:T(8,128)(2,1)S(1)} %get-tuple-element.66.old1.mx_ref, bf16[2,512,128]{2,1,0:T(8,128)(2,1)S(1)} %get-tuple-element.69.c_ref, ...), custom_call_target="tpu_custom_call", output_to_operand_aliasing={{0}: (8, {})} | custom-call | flops 268435456 | bytes 1572864 | tf_op jit(solution)/shard_map/out/pallas_call | solution.py:650
  30.3 1.1 %out.19 = (bf16[512,4096]{1,0:T(8,128)(2,1)}, bf16[512,512]{1,0:T(8,128)(2,1)S(1)}) custom-call(f32[8,2,512]{2,1,0:T(2,128)S(1)} %get-tuple-element.54.fade_ref, bf16[8,512,512]{2,1,0:T(8,128)(2,1)S(1)} %get-tuple-element.66.old1.mx_ref, bf16[2,512,128]{2,1,0:T(8,128)(2,1)S(1)} %get-tuple-element.69.c_ref, ...), custom_call_target="tpu_custom_call", output_to_operand_aliasing={{0}: (8, {})} | custom-call | flops 268435456 | bytes 1572864 | tf_op jit(solution)/shard_map/out/pallas_call | solution.py:650
  31.4 1.8 %more.7 = (bf16[8,512,512]{2,1,0:T(8,128)(2,1)S(1)}, f32[8,128,512]{2,1,0:T(8,128)S(1)}) custom-call(bf16[512,4096]{1,0:T(8,128)(2,1)S(1)} %get-tuple-element.55.x_ref, bf16[8,4608]{1,0:T(8,128)(2,1)S(1)} %collective-permute-done.rim_ref, f32[4,4096]{1,0:T(4,128)S(1)} %copy-done, ...), custom_call_target="tpu_custom_call", output_to_operand_aliasing={{0}: (7, {}), {1}: (8, {})} | custom-call | flops 268435456 | bytes 2097152 | tf_op jit(solution)/shard_map/more/pallas_call | solution.py:617
  33.2 2.4 %collective-permute-done.6.recv_ref = bf16[128,512]{1,0:T(8,128)(2,1)S(1)} collective-permute-done((bf16[128,512]{1,0:T(8,128)(2,1)S(1)}, bf16[128,512]{1,0:T(8,128)(2,1)S(1)}, u32[]{:S(2)}, u32[]{:S(2)}) %collective-permute-start.6) | collective-permute-done | bytes 131104 | tf_op jit(solution)/shard_map/ppermute | solution.py:676
  35.7 1.1 %out.20 = (bf16[512,4096]{1,0:T(8,128)(2,1)}, bf16[512,512]{1,0:T(8,128)(2,1)S(1)}) custom-call(f32[8,2,512]{2,1,0:T(2,128)S(1)} %get-tuple-element.54.fade_ref, bf16[8,512,512]{2,1,0:T(8,128)(2,1)S(1)} %get-tuple-element.68.mx_ref, bf16[2,512,128]{2,1,0:T(8,128)(2,1)S(1)} %get-tuple-element.69.c_ref, ...), custom_call_target="tpu_custom_call", output_to_operand_aliasing={{0}: (8, {})} | custom-call | flops 268435456 | bytes 1572864 | tf_op jit(solution)/shard_map/out/pallas_call | solution.py:650
  36.8 1.3 %collective-permute-done.5.recv_ref = bf16[128,512]{1,0:T(8,128)(2,1)S(1)} collective-permute-done((bf16[128,512]{1,0:T(8,128)(2,1)S(1)}, bf16[128,512]{1,0:T(8,128)(2,1)S(1)}, u32[]{:S(2)}, u32[]{:S(2)}) %collective-permute-start.5) | collective-permute-done | bytes 131104 | tf_op jit(solution)/shard_map/ppermute | solution.py:676
  39.3 3.1 %collective-permute-done.8.recv_ref = bf16[128,512]{1,0:T(8,128)(2,1)S(1)} collective-permute-done((bf16[128,512]{1,0:T(8,128)(2,1)S(1)}, bf16[128,512]{1,0:T(8,128)(2,1)S(1)}, u32[]{:S(2)}, u32[]{:S(2)}) %collective-permute-start.8) | collective-permute-done | bytes 131104 | tf_op jit(solution)/shard_map/ppermute | solution.py:676
  43.4 2.9 %collective-permute-done.7.recv_ref = bf16[128,512]{1,0:T(8,128)(2,1)S(1)} collective-permute-done((bf16[128,512]{1,0:T(8,128)(2,1)S(1)}, bf16[128,512]{1,0:T(8,128)(2,1)S(1)}, u32[]{:S(2)}, u32[]{:S(2)}) %collective-permute-start.7) | collective-permute-done | bytes 131104 | tf_op jit(solution)/shard_map/ppermute | solution.py:676
  46.5 2.8 %collective-permute-done.10.recv_ref = bf16[128,512]{1,0:T(8,128)(2,1)S(1)} collective-permute-done((bf16[128,512]{1,0:T(8,128)(2,1)S(1)}, bf16[128,512]{1,0:T(8,128)(2,1)S(1)}, u32[]{:S(2)}, u32[]{:S(2)}) %collective-permute-start.10) | collective-permute-done | bytes 131104 | tf_op jit(solution)/shard_map/ppermute | solution.py:676
  49.5 4.6 %collective-permute-done.9.recv_ref = bf16[128,512]{1,0:T(8,128)(2,1)S(1)} collective-permute-done((bf16[128,512]{1,0:T(8,128)(2,1)S(1)}, bf16[128,512]{1,0:T(8,128)(2,1)S(1)}, u32[]{:S(2)}, u32[]{:S(2)}) %collective-permute-start.9) | collective-permute-done | bytes 131104 | tf_op jit(solution)/shard_map/ppermute | solution.py:676
  54.3 1.9 %collective-permute-done.12.recv_ref = bf16[128,512]{1,0:T(8,128)(2,1)S(1)} collective-permute-done((bf16[128,512]{1,0:T(8,128)(2,1)S(1)}, bf16[128,512]{1,0:T(8,128)(2,1)S(1)}, u32[]{:S(2)}, u32[]{:S(2)}) %collective-permute-start.12) | collective-permute-done | bytes 131104 | tf_op jit(solution)/shard_map/ppermute | solution.py:676
  56.2 4.7 %collective-permute-done.11.recv_ref = bf16[128,512]{1,0:T(8,128)(2,1)S(1)} collective-permute-done((bf16[128,512]{1,0:T(8,128)(2,1)S(1)}, bf16[128,512]{1,0:T(8,128)(2,1)S(1)}, u32[]{:S(2)}, u32[]{:S(2)}) %collective-permute-start.11) | collective-permute-done | bytes 131104 | tf_op jit(solution)/shard_map/ppermute | solution.py:676
  (41 shorter events, 8.8 us)
Async XLA Ops:
  0.0 9.6 %copy-start = (f32[4,4096]{1,0:T(4,128)S(1)}, f32[4,4096]{1,0:T(4,128)}, u32[]{:S(2)}) copy-start(f32[4,4096]{1,0:T(4,128)} %wx_ref.9) | copy-start | bytes 196612
  0.0 9.6 %copy-start.1 = (f32[4096]{0:T(1024)S(1)}, f32[4096]{0:T(1024)}, u32[]{:S(2)}) copy-start(f32[4096]{0:T(1024)} %param.18) | copy-start | bytes 49156
  1.6 8.0 %collective-permute-start = (bf16[8,4608]{1,0:T(8,128)(2,1)S(1)}, bf16[8,4608]{1,0:T(8,128)(2,1)S(1)}, u32[]{:S(2)}, u32[]{:S(2)}) collective-permute-start(bf16[8,4608]{1,0:T(8,128)(2,1)S(1)} %pad_maximum_fusion), channel_id=1, source_target_pairs={{0,4},{4,8},{8,12},{12,0},{1,5},{5,9},{9,13},{13,1},{2,6},{6,10},{... | collective-permute-start | bytes 221192 | tf_op jit(solution)/shard_map/ppermute | solution.py:576
  12.8 8.2 %collective-permute-start.2 = (bf16[128,512]{1,0:T(8,128)(2,1)S(1)}, bf16[128,512]{1,0:T(8,128)(2,1)S(1)}, u32[]{:S(2)}, u32[]{:S(2)}) collective-permute-start(bf16[128,512]{1,0:T(8,128)(2,1)S(1)} %get-tuple-element.74.recv_ref), channel_id=1, source_target_pairs={{0,4},{4,8},{8,12},{12,0},{1,5},{5,9},{9,13},{13,1},{2,6},{6,10},{... | collective-permute-start | bytes 393224 | tf_op jit(solution)/shard_map/ppermute | solution.py:634
  15.4 7.1 %collective-permute-start.1 = (bf16[128,512]{1,0:T(8,128)(2,1)S(1)}, bf16[128,512]{1,0:T(8,128)(2,1)S(1)}, u32[]{:S(2)}, u32[]{:S(2)}) collective-permute-start(bf16[128,512]{1,0:T(8,128)(2,1)S(1)} %get-tuple-element.73.recv_ref), channel_id=1, source_target_pairs={{0,4},{4,8},{8,12},{12,0},{1,5},{5,9},{9,13},{13,1},{2,6},{6,10},{... | collective-permute-start | bytes 393224 | tf_op jit(solution)/shard_map/ppermute | solution.py:636
  21.1 7.6 %collective-permute-start.4 = (bf16[128,512]{1,0:T(8,128)(2,1)S(1)}, bf16[128,512]{1,0:T(8,128)(2,1)S(1)}, u32[]{:S(2)}, u32[]{:S(2)}) collective-permute-start(bf16[128,512]{1,0:T(8,128)(2,1)S(1)} %join.11), channel_id=1, source_target_pairs={{0,4},{4,8},{8,12},{12,0},{1,5},{5,9},{9,13},{13,1},{2,6},{6,10},{... | collective-permute-start | bytes 393224 | tf_op jit(solution)/shard_map/ppermute | solution.py:676
  22.5 7.7 %collective-permute-start.3 = (bf16[128,512]{1,0:T(8,128)(2,1)S(1)}, bf16[128,512]{1,0:T(8,128)(2,1)S(1)}, u32[]{:S(2)}, u32[]{:S(2)}) collective-permute-start(bf16[128,512]{1,0:T(8,128)(2,1)S(1)} %join.10), channel_id=1, source_target_pairs={{0,4},{4,8},{8,12},{12,0},{1,5},{5,9},{9,13},{13,1},{2,6},{6,10},{... | collective-permute-start | bytes 393224 | tf_op jit(solution)/shard_map/ppermute | solution.py:676
  28.8 6.8 %collective-permute-start.6 = (bf16[128,512]{1,0:T(8,128)(2,1)S(1)}, bf16[128,512]{1,0:T(8,128)(2,1)S(1)}, u32[]{:S(2)}, u32[]{:S(2)}) collective-permute-start(bf16[128,512]{1,0:T(8,128)(2,1)S(1)} %join.13), channel_id=1, source_target_pairs={{0,4},{4,8},{8,12},{12,0},{1,5},{5,9},{9,13},{13,1},{2,6},{6,10},{... | collective-permute-start | bytes 393224 | tf_op jit(solution)/shard_map/ppermute | solution.py:676
  30.2 7.9 %collective-permute-start.5 = (bf16[128,512]{1,0:T(8,128)(2,1)S(1)}, bf16[128,512]{1,0:T(8,128)(2,1)S(1)}, u32[]{:S(2)}, u32[]{:S(2)}) collective-permute-start(bf16[128,512]{1,0:T(8,128)(2,1)S(1)} %join.12), channel_id=1, source_target_pairs={{0,4},{4,8},{8,12},{12,0},{1,5},{5,9},{9,13},{13,1},{2,6},{6,10},{... | collective-permute-start | bytes 393224 | tf_op jit(solution)/shard_map/ppermute | solution.py:676
  35.6 6.8 %collective-permute-start.8 = (bf16[128,512]{1,0:T(8,128)(2,1)S(1)}, bf16[128,512]{1,0:T(8,128)(2,1)S(1)}, u32[]{:S(2)}, u32[]{:S(2)}) collective-permute-start(bf16[128,512]{1,0:T(8,128)(2,1)S(1)} %join.15), channel_id=1, source_target_pairs={{0,4},{4,8},{8,12},{12,0},{1,5},{5,9},{9,13},{13,1},{2,6},{6,10},{... | collective-permute-start | bytes 393224 | tf_op jit(solution)/shard_map/ppermute | solution.py:676
  38.2 8.2 %collective-permute-start.7 = (bf16[128,512]{1,0:T(8,128)(2,1)S(1)}, bf16[128,512]{1,0:T(8,128)(2,1)S(1)}, u32[]{:S(2)}, u32[]{:S(2)}) collective-permute-start(bf16[128,512]{1,0:T(8,128)(2,1)S(1)} %join.14), channel_id=1, source_target_pairs={{0,4},{4,8},{8,12},{12,0},{1,5},{5,9},{9,13},{13,1},{2,6},{6,10},{... | collective-permute-start | bytes 393224 | tf_op jit(solution)/shard_map/ppermute | solution.py:676
  42.5 6.8 %collective-permute-start.10 = (bf16[128,512]{1,0:T(8,128)(2,1)S(1)}, bf16[128,512]{1,0:T(8,128)(2,1)S(1)}, u32[]{:S(2)}, u32[]{:S(2)}) collective-permute-start(bf16[128,512]{1,0:T(8,128)(2,1)S(1)} %join.17), channel_id=1, source_target_pairs={{0,4},{4,8},{8,12},{12,0},{1,5},{5,9},{9,13},{13,1},{2,6},{6,10},{... | collective-permute-start | bytes 393224 | tf_op jit(solution)/shard_map/ppermute | solution.py:676
  46.4 7.7 %collective-permute-start.9 = (bf16[128,512]{1,0:T(8,128)(2,1)S(1)}, bf16[128,512]{1,0:T(8,128)(2,1)S(1)}, u32[]{:S(2)}, u32[]{:S(2)}) collective-permute-start(bf16[128,512]{1,0:T(8,128)(2,1)S(1)} %join.16), channel_id=1, source_target_pairs={{0,4},{4,8},{8,12},{12,0},{1,5},{5,9},{9,13},{13,1},{2,6},{6,10},{... | collective-permute-start | bytes 393224 | tf_op jit(solution)/shard_map/ppermute | solution.py:676
  49.4 6.8 %collective-permute-start.12 = (bf16[128,512]{1,0:T(8,128)(2,1)S(1)}, bf16[128,512]{1,0:T(8,128)(2,1)S(1)}, u32[]{:S(2)}, u32[]{:S(2)}) collective-permute-start(bf16[128,512]{1,0:T(8,128)(2,1)S(1)} %join.19), channel_id=1, source_target_pairs={{0,4},{4,8},{8,12},{12,0},{1,5},{5,9},{9,13},{13,1},{2,6},{6,10},{... | collective-permute-start | bytes 393224 | tf_op jit(solution)/shard_map/ppermute | solution.py:676
  54.1 6.8 %collective-permute-start.11 = (bf16[128,512]{1,0:T(8,128)(2,1)S(1)}, bf16[128,512]{1,0:T(8,128)(2,1)S(1)}, u32[]{:S(2)}, u32[]{:S(2)}) collective-permute-start(bf16[128,512]{1,0:T(8,128)(2,1)S(1)} %join.18), channel_id=1, source_target_pairs={{0,4},{4,8},{8,12},{12,0},{1,5},{5,9},{9,13},{13,1},{2,6},{6,10},{... | collective-permute-start | bytes 393224 | tf_op jit(solution)/shard_map/ppermute | solution.py:676

commit v5 on v4

--- a/solution.py
+++ b/solution.py
@@ -14,6 +14,8 @@
 NQ = BLK // Q
 HC = 4
 CW = HC * D
+PARTS = 2
+PW = CW // PARTS
 RIM = 8
 LOG2E = math.log2(math.e)
 F32 = jnp.float32
@@ -29,6 +31,106 @@
 
 def silu_half(u):
     return u + u * jnp.tanh(u)
+
+
+def doc_at(pos, starts_ref):
+    count = jnp.int32(-1)
+    for j in range(starts_ref.shape[0]):
+        count = count + (pos >= starts_ref[j]).astype(jnp.int32)
+    return count
+
+
+def column_of(ref):
+    heads = ref.shape[0]
+    index = lax.broadcasted_iota(jnp.int32, (heads, 1), 0)
+    column = jnp.zeros((heads, 1), F32)
+    for h in range(heads):
+        column = jnp.where(index == h, ref[h], column)
+    return column
+
+
+def split(value, parts):
+    pieces = []
+    for _ in range(parts - 1):
+        piece = value.astype(BF16).astype(F32)
+        pieces.append(piece)
+        value = value - piece
+    return pieces + [value]
+
+
+def doc_at(pos, starts_ref):
+    count = jnp.int32(-1)
+    for j in range(starts_ref.shape[0]):
+        count = count + (pos >= starts_ref[j]).astype(jnp.int32)
+    return count
+
+
+def column_of(ref):
+    heads = ref.shape[0]
+    index = lax.broadcasted_iota(jnp.int32, (heads, 1), 0)
+    column = jnp.zeros((heads, 1), F32)
+    for h in range(heads):
+        column = jnp.where(index == h, ref[h], column)
+    return column
+
+
+def split(value, parts):
+    pieces = []
+    for _ in range(parts - 1):
+        piece = value.astype(BF16).astype(F32)
+        pieces.append(piece)
+        value = value - piece
+    return pieces + [value]
+
+
+def doc_at(pos, starts_ref):
+    count = jnp.int32(-1)
+    for j in range(starts_ref.shape[0]):
+        count = count + (pos >= starts_ref[j]).astype(jnp.int32)
+    return count
+
+
+def column_of(ref):
+    heads = ref.shape[0]
+    index = lax.broadcasted_iota(jnp.int32, (heads, 1), 0)
+    column = jnp.zeros((heads, 1), F32)
+    for h in range(heads):
+        column = jnp.where(index == h, ref[h], column)
+    return column
+
+
+def split(value, parts):
+    pieces = []
+    for _ in range(parts - 1):
+        piece = value.astype(BF16).astype(F32)
+        pieces.append(piece)
+        value = value - piece
+    return pieces + [value]
+
+
+def doc_at(pos, starts_ref):
+    count = jnp.int32(-1)
+    for j in range(starts_ref.shape[0]):
+        count = count + (pos >= starts_ref[j]).astype(jnp.int32)
+    return count
+
+
+def column_of(ref):
+    heads = ref.shape[0]
+    index = lax.broadcasted_iota(jnp.int32, (heads, 1), 0)
+    column = jnp.zeros((heads, 1), F32)
+    for h in range(heads):
+        column = jnp.where(index == h, ref[h], column)
+    return column
+
+
+def split(value, parts):
+    pieces = []
+    for _ in range(parts - 1):
+        piece = value.astype(BF16).astype(F32)
+        pieces.append(piece)
+        value = value - piece
+    return pieces + [value]
 
 
 def doc_at(pos, starts_ref):
@@ -396,72 +498,95 @@
 
 def edge(edge_ref, rim, x):
     width = x.shape[1]
-    rim = jnp.concatenate([jnp.zeros((Q - RIM, width), F32), rim.astype(F32)], axis=0)
+    if rim is None:
+        rim = jnp.zeros((Q, width), F32)
+    else:
+        rim = jnp.concatenate([jnp.zeros((Q - RIM, width), F32), rim.astype(F32)], axis=0)
     edge_ref[0:Q, 0:width] = rim.astype(BF16)
     edge_ref[Q : 2 * Q, 0:width] = x
 
 
-def state_body(
-    chunk, heads, per_group, x_ref, rim_ref, wx_ref, bx_ref, shift_ref, scale_ref, bt_ref,
-    mx_ref, end_ref, edge_ref, tail_ref, send_ref=None,
+def state_of(
+    chunk, heads, x_ref, rim, wx_ref, bx_ref, shift_ref, scale_ref, bt, edge_ref, tail_ref, mx_ref=None
 ):
     wide = slice(chunk * CW, (chunk + 1) * CW)
-    edge(edge_ref, rim_ref[:, wide], x_ref[0:Q, wide])
+    edge(edge_ref, rim, x_ref[0:Q, :])
     pick = chooser(heads, chunk, 0, 2, CW)
     taps = [wx_ref[k : k + 1, wide] for k in range(4)]
     for q in range(NQ):
         span = slice(q * Q, (q + 1) * Q)
-        window = x_ref[(q - 1) * Q : (q + 1) * Q, wide] if q else edge_ref[...]
-        mixed = convolved(q, window, x_ref[span, wide], shift_ref, taps, bx_ref[:, wide])
-        mx_ref[chunk, span, :] = mixed.astype(BF16)
+        window = x_ref[(q - 1) * Q : (q + 1) * Q, :] if q else edge_ref[:, 0:CW]
+        mixed = convolved(q, window, x_ref[span, :], shift_ref, taps, bx_ref[:, wide])
+        if mx_ref is not None:
+            mx_ref[chunk, span, :] = mixed.astype(BF16)
         scale = jnp.dot(scale_ref[span, :], pick, preferred_element_type=F32)
         tail_ref[span, :] = (mixed * scale).astype(BF16)
-    state = jnp.dot(bt_ref[chunk // per_group], tail_ref[...], preferred_element_type=F32)
-    end_ref[chunk] = state
-    if send_ref is not None:
-        send_ref[...] = state.astype(BF16)
+    return jnp.dot(bt, tail_ref[...], preferred_element_type=F32)
+
+
+def chunk_of(x_ref, chunk):
+    return x_ref.at[:, pl.ds(chunk * CW, CW)]
+
+
+def mixed_of(q, part, edge_ref, bc_ref, shift_ref, wbc_ref, bbc_ref, wide):
+    half = slice(part * wide, (part + 1) * wide)
+    window = bc_ref[(q - 1) * Q : (q + 1) * Q, half] if q else edge_ref[:, 0:wide]
+    taps = [wbc_ref[k, part : part + 1, :] for k in range(4)]
+    return convolved(q, window, bc_ref[q * Q : (q + 1) * Q, half], shift_ref, taps, bbc_ref[part : part + 1, :])
 
 
 def first_kernel(
-    x_ref, rim_ref, wx_ref, bx_ref, shift_ref, scale_ref, keep_ref, bc_ref, wbc_ref, bbc_ref,
-    mx_ref, end_ref, send_ref, bt_ref, c_ref, score_ref,
-    edge_ref, tail_ref, *, heads, per_group,
+    x_ref, rim_ref, wx_ref, bx_ref, shift_ref, scale_ref, bc_ref, wbc_ref, bbc_ref,
+    mx_ref, end_ref, send_ref, bt_ref, edge_ref, tail_ref, *, heads,
 ):
     groups = bt_ref.shape[0]
-    wide = 2 * groups * D
-    edge(edge_ref, rim_ref[:, x_ref.shape[1] :], bc_ref[0:Q, :])
-
-    def joined(rows):
-        return jnp.concatenate(rows, axis=1)
-
-    taps = [joined([wbc_ref[k, p : p + 1, :] for p in range(2)]) for k in range(4)]
-    bias = joined([bbc_ref[p : p + 1, :] for p in range(2)])
+    wide = groups * D
+    start = x_ref.shape[1]
+    edge(edge_ref, rim_ref[:, start : start + wide], bc_ref[0:Q, 0:wide])
+    for q in range(NQ):
+        mixed = mixed_of(q, 0, edge_ref, bc_ref, shift_ref, wbc_ref, bbc_ref, wide)
+        for g in range(groups):
+            bt_ref[g, :, q * Q : (q + 1) * Q] = jnp.transpose(mixed[:, g * D : (g + 1) * D], (1, 0)).astype(BF16)
+    state = state_of(
+        0, heads, chunk_of(x_ref, 0), rim_ref[:, 0:CW], wx_ref, bx_ref, shift_ref, scale_ref, bt_ref[0],
+        edge_ref, tail_ref, mx_ref,
+    )
+    end_ref[0] = state
+    send_ref[...] = state.astype(BF16)
+
+
+def score_kernel(
+    rim_ref, shift_ref, keep_ref, bc_ref, wbc_ref, bbc_ref, bt_ref, after_ref, c_ref, score_ref, edge_ref
+):
+    groups = bt_ref.shape[0]
+    wide = groups * D
+    start = rim_ref.shape[1] - wide
+    edge(edge_ref, rim_ref[:, start:], bc_ref[0:Q, wide:])
     for q in range(NQ):
         span = slice(q * Q, (q + 1) * Q)
-        window = edge_ref[:, 0:wide] if q == 0 else bc_ref[(q - 1) * Q : (q + 1) * Q, :]
-        mixed = convolved(q, window, bc_ref[span, :], shift_ref, taps, bias)
         upto = (q + 1) * Q
+        mixed = mixed_of(q, 1, edge_ref, bc_ref, shift_ref, wbc_ref, bbc_ref, wide)
         for g in range(groups):
-            bt_ref[g, :, span] = jnp.transpose(mixed[:, g * D : (g + 1) * D], (1, 0)).astype(BF16)
-            c = mixed[:, (groups + g) * D : (groups + g + 1) * D].astype(BF16)
+            c = mixed[:, g * D : (g + 1) * D].astype(BF16)
             c_ref[g, span, :] = c
             score = jnp.dot(c, bt_ref[g, :, 0:upto], preferred_element_type=F32)
             score_ref[g, span, 0:upto] = keep_ref[span, 0:upto] * score
-    state_body(
-        0, heads, per_group, x_ref, rim_ref, wx_ref, bx_ref, shift_ref, scale_ref, bt_ref,
-        mx_ref, end_ref, edge_ref, tail_ref, send_ref,
-    )
 
 
 def more_kernel(
     x_ref, rim_ref, wx_ref, bx_ref, shift_ref, scale_ref, bt_ref, old1, old2,
-    mx_ref, end_ref, *rest, heads, per_group, some, sends,
+    mx_ref, end_ref, *rest, heads, per_group, some,
 ):
+    edge_ref, tail_ref = rest[-2:]
     for chunk in some:
-        state_body(
-            chunk, heads, per_group, x_ref, rim_ref, wx_ref, bx_ref, shift_ref, scale_ref,
-            bt_ref, mx_ref, end_ref, *rest[-2:], *rest[:sends],
+        wide = slice(chunk * CW, (chunk + 1) * CW)
+        state = state_of(
+            chunk, heads, chunk_of(x_ref, chunk), rim_ref[:, wide], wx_ref, bx_ref, shift_ref, scale_ref,
+            bt_ref[chunk // per_group], edge_ref, tail_ref, mx_ref,
         )
+        end_ref[chunk] = state
+        for send_ref in rest[:-2]:
+            send_ref[...] = state.astype(BF16)
 
 
 def join_kernel(fade_ref, recv_ref, end_ref, token_ref, send_ref, *, turn, stream, per_stream):
@@ -483,9 +608,9 @@
     def is_valid(when):
         return (when - place >= 0) & (when - place < per_stream)
 
-    def half_copy(ref, when, which, half, slot=0):
+    def half_copy(ref, when, which, half):
         rows = pl.ds(half * 2 * Q, 2 * Q)
-        return pltpu.make_async_copy(ref.at[rows, :], out_ref.at[rows, spot(when, which)], sem.at[2 * slot + half])
+        return pltpu.make_async_copy(ref.at[rows, :], out_ref.at[rows, spot(when, which)], sem.at[half])
 
     if before:
         @pl.when(is_valid(before[0]))
@@ -500,6 +625,7 @@
         cols = pltpu.roll(cols_ref[...], lax.rem(D - HC * chunk, D), 1)
         far = jnp.dot(c_ref[g], recv_ref[...], preferred_element_type=F32)
         zero = jnp.zeros((Q, Q), BF16)
+        last = []
         for i in range(HC):
             lanes = slice(i * D, (i + 1) * D)
             cum = jnp.broadcast_to(cols[:, i : i + 1], (BLK, Q))
@@ -527,11 +653,14 @@
                 x = mx_ref[chunk, span, lanes].astype(F32)
                 y = y + entry[span] * far[span, lanes] + fade_ref[chunk, 0:1, lanes] * x
                 block_ref[span, lanes] = y.astype(BF16)
-        if final:
-            for half in range(2):
-                half_copy(block_ref, turn, stream, half, 1).start()
-            for half in range(2):
-                half_copy(block_ref, turn, stream, half, 1).wait()
+            if final:
+                there = pl.ds(pl.multiple_of(chunk * CW + i * D, D), D)
+                last.append(
+                    pltpu.make_async_copy(block_ref.at[:, pl.ds(i * D, D)], out_ref.at[:, there], sem.at[2 + i])
+                )
+                last[-1].start()
+        for copy in last:
+            copy.wait()
 
     if before:
         @pl.when(is_valid(before[0]))
@@ -568,6 +697,7 @@
     per_group = chunks // groups
     seq = lax.axis_size("seq")
     ring = [(i, (i + 1) % seq) for i in range(seq)]
+    swaps = [(i, i ^ 1) for i in range(seq)] if seq % 2 == 0 else ring
     streams = 2
     per_stream = chunks // streams
     slots = per_stream + seq - 2
@@ -596,26 +726,25 @@
 
     big = [pltpu.VMEM((chunks, BLK, CW), BF16), pltpu.VMEM((chunks, D, CW), F32)]
     chunk_shape = shape_of((D, CW), BF16)
-    scratch = [pltpu.VMEM((2 * Q, CW), BF16), pltpu.VMEM((BLK, CW), BF16)]
-    mixed_x, end, send_a, bt, mixed_c, score = pl.pallas_call(
-        functools.partial(first_kernel, heads=heads, per_group=per_group),
-        in_specs=[VMEM] * 10,
-        out_specs=[VMEM] * 6,
-        out_shape=[
-            *big,
-            chunk_shape,
-            shape_of((groups, D, BLK), BF16),
-            shape_of((groups, BLK, D), BF16),
-            shape_of((groups, BLK, BLK), F32),
-        ],
+    bt_shape = shape_of((groups, D, BLK), BF16)
+    scratch = [pltpu.VMEM((2 * Q, max(CW, 2 * groups * D)), BF16), pltpu.VMEM((BLK, CW), BF16)]
+
+    mixed_x, end, send, bt = pl.pallas_call(
+        functools.partial(first_kernel, heads=heads),
+        in_specs=[VMEM] * 9,
+        out_specs=[VMEM] * 4,
+        out_shape=[*big, chunk_shape, bt_shape],
         scratch_shapes=scratch,
         compiler_params=ROOM,
         name="first",
-    )(x_near, rim, conv_x, bias_x, shift, scale, keep, bc, conv_bc, conv_bc_bias)
+    )(x_near, rim, conv_x, bias_x, shift, scale, bc, conv_bc, conv_bc_bias)
+
+    def near(array):
+        return pltpu.with_memory_space_constraint(array, pltpu.VMEM)
 
     def more(some, sends, mixed_x, end):
         return pl.pallas_call(
-            functools.partial(more_kernel, heads=heads, per_group=per_group, some=some, sends=sends),
+            functools.partial(more_kernel, heads=heads, per_group=per_group, some=some),
             in_specs=[VMEM] * 9,
             out_specs=[VMEM] * (2 + sends),
             out_shape=big + [chunk_shape] * sends,
@@ -628,12 +757,23 @@
             name="more",
         )(x_near, rim, conv_x, bias_x, shift, scale, bt, near(mixed_x), near(end))
 
-    def near(array):
-        return pltpu.with_memory_space_constraint(array, pltpu.VMEM)
-
-    flying = [lax.ppermute(send_a, "seq", ring), None]
-    mixed_x, end, send_b = more([per_stream], 1, mixed_x, end)
-    flying[1] = lax.ppermute(send_b, "seq", ring)
+    begun = [send]
+    flying = [lax.ppermute(send, "seq", swaps)]
+    for s in range(1, streams):
+        mixed_x, end, send = more([s * per_stream], 1, mixed_x, end)
+        begun.append(send)
+        flying.append(lax.ppermute(send, "seq", swaps))
+
+    def scores(after):
+        return pl.pallas_call(
+            score_kernel,
+            in_specs=[VMEM] * 7 + [ANY],
+            out_specs=[VMEM] * 2,
+            out_shape=[shape_of((groups, BLK, D), BF16), shape_of((groups, BLK, BLK), F32)],
+            scratch_shapes=scratch[:1],
+            compiler_params=ROOM,
+            name="score",
+        )(rim, shift, keep, bc, conv_bc, conv_bc_bias, bt, after)
 
     def join(turn, s, recv, token):
         return pl.pallas_call(
@@ -645,7 +785,7 @@
             name="join",
         )(fade, recv, end, token)
 
-    def output(turn, s, recv, before, block, out):
+    def output(turn, s, recv, before, block, out, mixed_c, score):
         old = [] if out is None else [block, out]
         return pl.pallas_call(
             functools.partial(
@@ -656,7 +796,7 @@
             out_specs=[ANY, VMEM],
             out_shape=[pltpu.HBM((BLK, width), BF16), shape_of((BLK, CW), BF16)],
             input_output_aliases={8: 0} if old else {},
-            scratch_shapes=[pltpu.SemaphoreType.DMA((4,))],
+            scratch_shapes=[pltpu.SemaphoreType.DMA((2 + HC,))],
             compiler_params=ROOM,
             cost_estimate=pl.CostEstimate(
                 flops=8 * BLK * Q * CW, bytes_accessed=6 * BLK * CW, transcendentals=0
@@ -665,18 +805,24 @@
         )(fade, mixed_x, mixed_c, score, cols, row_terms, recv, *old)
 
     out, block, before = None, None, None
-    carried = [send_a, send_b]
-    for turn in range(slots + 1):
-        if 0 < turn < per_stream:
+    waiting = [(0, s, begun[s]) for s in range(streams)]
+    token = bt
+    for turn in range(1, slots + 1):
+        if turn < per_stream:
             mixed_x, end = more([turn + i * per_stream for i in range(streams)], 0, mixed_x, end)
         for s in range(streams):
-            if turn:
-                recv = flying[s]
-                if turn < slots:
-                    flying[s] = lax.ppermute(join(turn, s, recv, block), "seq", ring)
-                carried[s] = recv
-            out, block = output(turn, s, carried[s], before, block, out)
-            before = (turn, s)
+            recv = flying[s]
+            if turn < slots:
+                send = join(turn, s, recv, token)
+                flying[s] = lax.ppermute(send, "seq", swaps if turn == slots - 1 else ring)
+            if turn == 1 and s == 0:
+                mixed_c, score = scores(send)
+            todo = [(turn, s, recv)]
+            if waiting and turn >= min(per_stream, slots):
+                todo.insert(0, waiting.pop(0))
+            for when, which, got in todo:
+                out, token = output(when, which, got, before, token, out, mixed_c, score)
+                before = (when, which)
     return out
 
 

time: 62.3 us -> 59.9 us (0.961)
  waiting for transfers between devices: 26.1 us -> 20.5 us
  starting transfers between devices: 8.06 us -> 10.2 us
  Pallas kernels: 24.6 us -> 25.7 us
    ppermute x12, waiting for transfers between devices: 26.1 us -> 20.4 us  [the longest x10 19.8 us: per_device(): flying[s] = lax.ppermute(send, 'seq', swaps if turn == slots - 1 else ring)]
    ppermute x12, starting transfers between devices: 4.98 us -> 7.1 us  [the longest x10 4.95 us: per_device(): flying[s] = lax.ppermute(send, 'seq', swaps if turn == slots - 1 else ring)]
    pallas_call x14, Pallas kernels: 10.9 us -> 11.5 us  [output(): pl.pallas_call(functools.partial(out_kernel, turn=turn, stream=s, before=...]
    pallas_call x1 -> x2, Pallas kernels: 3.22 us -> 3.76 us  [the longest x1 1.97 us: per_device(): pl.pallas_call(functools.partial(first_kernel, heads=heads), in_specs=[VM...]
  transfers between devices with their start and end apart: 13 -> 13, of which waited for: 10 -> 9; matrix products, arithmetic and copies ran while one was open for 2% -> 2% of each run, Pallas kernels for 33% -> 38%
where the time goes in v5:
time: 59.9 us; the launch traced here: 59.6 us
  Pallas kernels  25.7 us (43%)
  waiting for transfers between devices  20.5 us (34%)
  starting transfers between devices  10.2 us (17%)
  local copies, waits for them, and re-layouts  2.72 us (5%)
    ppermute x10, waiting for transfers between devices, per_device(): flying[s] = lax.ppermute(send, 'seq', swaps if turn == slots - 1 else ring)  19.8 us
    pallas_call x14, Pallas kernels, output(): pl.pallas_call(functools.partial(out_kernel, turn=turn, stream=s, before=...  11.5 us
    pallas_call x4, Pallas kernels, more(): pl.pallas_call(functools.partial(more_kernel, heads=heads, per_group=per_...  6.25 us
    ppermute x10, starting transfers between devices, per_device(): flying[s] = lax.ppermute(send, 'seq', swaps if turn == slots - 1 else ring)  4.95 us
    pallas_call x1, Pallas kernels, per_device(): pl.pallas_call(params_kernel, in_specs=[SMEM] * 4 + [VMEM, ANY], out_spec...  3.75 us
    ppermute x1, starting transfers between devices, per_device(): rim = lax.ppermute(tail, 'seq', ring)  3.08 us
    pallas_call x1, Pallas kernels, per_device(): pl.pallas_call(functools.partial(first_kernel, heads=heads), in_specs=[VM...  1.97 us
    unnamed x7, local copies, waits for them, and re-layouts  1.87 us
  transfers between devices with their start and end apart: 13, of which 9 were waited for; matrix products, arithmetic and copies ran while one was open for 2% of the time, Pallas kernels for 38%

profile of v5, /device:TPU:0, one launch (start us, length us, event | category | flops | bytes accessed | tf_op | source)
XLA Modules:
  0.0 59.6 jit_solution(12050029330031471586)
XLA Ops:
  1.6 3.1 %collective-permute-start = (bf16[8,4608]{1,0:T(8,128)(2,1)S(1)}, bf16[8,4608]{1,0:T(8,128)(2,1)S(1)}, u32[]{:S(2)}, u32[]{:S(2)}) collective-permute-start(bf16[8,4608]{1,0:T(8,128)(2,1)S(1)} %pad_maximum_fusion), channel_id=1, source_target_pairs={{0,4},{4,8},{8,12},{12,0},{1,5},{5,9},{9,13},{13,1},{2,6},{6,10},{... | collective-permute-start | bytes 221192 | tf_op jit(solution)/shard_map/ppermute | solution.py:706
  4.7 1.1 %copy.34 = bf16[64,8,2,256]{3,1,2,0:T(8,128)(2,1)S(1)} copy(bf16[64,8,2,256]{3,2,1,0:T(2,128)(2,1)} %bitcast.13) | data formatting | bytes 1048576
  5.8 3.8 %params.1 = (bf16[512,128]{1,0:T(8,128)(2,1)S(1)}, f32[512,128]{1,0:T(8,128)S(1)}, f32[8,4,512]{2,1,0:T(4,128)S(1)}, f32[8,2,512]{2,1,0:T(2,128)S(1)}, bf16[4,38...) custom-call(s32[4]{0:T(128)} %starts_ref.1, f32[32]{0:T(128)} %bias_ref.1, ...), custom_call_target="tpu_custom_call" | custom-call | tf_op jit(solution)/shard_map/params/pallas_call | solution.py:709
  9.6 2.0 %first.1 = (bf16[8,512,512]{2,1,0:T(8,128)(2,1)S(1)}, f32[8,128,512]{2,1,0:T(8,128)S(1)}, bf16[128,512]{1,0:T(8,128)(2,1)S(1)}, bf16[2,128,512]{2,1,0:T(8,128)(2,1)S(1)}) custom-call(bf16[512,4096]{1,0:T(8,128)(2,1)S(1)} %get-tuple-element.55.x_ref, bf16[8,4608]{1,0:T(8,128)(2,1)S(1)} %collective-permute-done.rim_ref, f32[4,4096]{1,0:T(4,128)S(1)} %copy-done, ...), custom_call_target="tpu_custom_call" | custom-call | tf_op jit(solution)/shard_map/first/pallas_call | solution.py:732
  11.6 1.6 %collective-permute-start.1 = (bf16[128,512]{1,0:T(8,128)(2,1)S(1)}, bf16[128,512]{1,0:T(8,128)(2,1)S(1)}, u32[]{:S(2)}, u32[]{:S(2)}) collective-permute-start(bf16[128,512]{1,0:T(8,128)(2,1)S(1)} %get-tuple-element.69.recv_ref), channel_id=1, source_target_pairs={{0,4},{4,0},{8,12},{12,8},{1,5},{5,1},{9,13},{13,9},{2,6},{6,2},{1... | collective-permute-start | bytes 393224 | tf_op jit(solution)/shard_map/ppermute | solution.py:761
  14.7 1.8 %more.5 = (bf16[8,512,512]{2,1,0:T(8,128)(2,1)S(1)}, f32[8,128,512]{2,1,0:T(8,128)S(1)}) custom-call(bf16[512,4096]{1,0:T(8,128)(2,1)S(1)} %get-tuple-element.55.x_ref, bf16[8,4608]{1,0:T(8,128)(2,1)S(1)} %collective-permute-done.rim_ref, f32[4,4096]{1,0:T(4,128)S(1)} %copy-done, ...), custom_call_target="tpu_custom_call", output_to_operand_aliasing={{0}: (7, {}), {1}: (8, {})} | custom-call | flops 268435456 | bytes 2097152 | tf_op jit(solution)/shard_map/more/pallas_call | solution.py:746
  17.2 2.5 %collective-permute-start.4 = (bf16[128,512]{1,0:T(8,128)(2,1)S(1)}, bf16[128,512]{1,0:T(8,128)(2,1)S(1)}, u32[]{:S(2)}, u32[]{:S(2)}) collective-permute-start(bf16[128,512]{1,0:T(8,128)(2,1)S(1)} %join.10.after_ref), channel_id=1, source_target_pairs={{0,4},{4,8},{8,12},{12,0},{1,5},{5,9},{9,13},{13,1},{2,6},{6,10},{... | collective-permute-start | bytes 393224 | tf_op jit(solution)/shard_map/ppermute | solution.py:817
  19.7 1.8 %score.1 = (bf16[2,512,128]{2,1,0:T(8,128)(2,1)S(1)}, f32[2,512,512]{2,1,0:T(8,128)S(1)}) custom-call(bf16[8,4608]{1,0:T(8,128)(2,1)S(1)} %collective-permute-done.rim_ref, bf16[4,384,256]{2,1,0:T(8,128)(2,1)S(1)} %get-tuple-element.56.shift_ref, f32[512,512]{1,0:T(8,128)S(1)} %get-tuple-element.68.keep_ref, bf16[512,512]{1,0:T(8,128)(2,1)S(1)} %bitcast.7, ...), custom_call_target="tpu_custom_call" | custom-call | tf_op jit(solution)/shard_map/score/pallas_call | solution.py:768
  21.5 1.1 %out.14 = (bf16[512,4096]{1,0:T(8,128)(2,1)}, bf16[512,512]{1,0:T(8,128)(2,1)S(1)}) custom-call(f32[8,2,512]{2,1,0:T(2,128)S(1)} %get-tuple-element.54.fade_ref, bf16[8,512,512]{2,1,0:T(8,128)(2,1)S(1)} %get-tuple-element.63.old1.mx_ref, bf16[2,512,128]{2,1,0:T(8,128)(2,1)S(1)} %get-tuple-element.70.c_ref, f32[2,512,512]{2,1,0:T(8,128)S(1)} %get-tuple-element.71.score_ref, ...), custom_call_target="tpu_custom_call" | custom-call | flops 268435456 | bytes 1572864 | tf_op jit(solution)/shard_map/out/pallas_call | solution.py:790
  22.6 1.7 %collective-permute-start.3 = (bf16[128,512]{1,0:T(8,128)(2,1)S(1)}, bf16[128,512]{1,0:T(8,128)(2,1)S(1)}, u32[]{:S(2)}, u32[]{:S(2)}) collective-permute-start(bf16[128,512]{1,0:T(8,128)(2,1)S(1)} %join.11), channel_id=1, source_target_pairs={{0,4},{4,8},{8,12},{12,0},{1,5},{5,9},{9,13},{13,1},{2,6},{6,10},{... | collective-permute-start | bytes 393224 | tf_op jit(solution)/shard_map/ppermute | solution.py:817
  25.4 1.8 %more.6 = (bf16[8,512,512]{2,1,0:T(8,128)(2,1)S(1)}, f32[8,128,512]{2,1,0:T(8,128)S(1)}) custom-call(bf16[512,4096]{1,0:T(8,128)(2,1)S(1)} %get-tuple-element.55.x_ref, bf16[8,4608]{1,0:T(8,128)(2,1)S(1)} %collective-permute-done.rim_ref, f32[4,4096]{1,0:T(4,128)S(1)} %copy-done, ...), custom_call_target="tpu_custom_call", output_to_operand_aliasing={{0}: (7, {}), {1}: (8, {})} | custom-call | flops 268435456 | bytes 2097152 | tf_op jit(solution)/shard_map/more/pallas_call | solution.py:746
  27.3 1.1 %out.16 = (bf16[512,4096]{1,0:T(8,128)(2,1)}, bf16[512,512]{1,0:T(8,128)(2,1)S(1)}) custom-call(f32[8,2,512]{2,1,0:T(2,128)S(1)} %get-tuple-element.54.fade_ref, bf16[8,512,512]{2,1,0:T(8,128)(2,1)S(1)} %get-tuple-element.65.old1.mx_ref, bf16[2,512,128]{2,1,0:T(8,128)(2,1)S(1)} %get-tuple-element.70.c_ref, ...), custom_call_target="tpu_custom_call", output_to_operand_aliasing={{0}: (8, {})} | custom-call | flops 268435456 | bytes 1572864 | tf_op jit(solution)/shard_map/out/pallas_call | solution.py:790
  28.4 2.0 %collective-permute-done.3.recv_ref = bf16[128,512]{1,0:T(8,128)(2,1)S(1)} collective-permute-done((bf16[128,512]{1,0:T(8,128)(2,1)S(1)}, bf16[128,512]{1,0:T(8,128)(2,1)S(1)}, u32[]{:S(2)}, u32[]{:S(2)}) %collective-permute-start.3) | collective-permute-done | bytes 131104 | tf_op jit(solution)/shard_map/ppermute | solution.py:817
  30.8 1.2 %out.17 = (bf16[512,4096]{1,0:T(8,128)(2,1)}, bf16[512,512]{1,0:T(8,128)(2,1)S(1)}) custom-call(f32[8,2,512]{2,1,0:T(2,128)S(1)} %get-tuple-element.54.fade_ref, bf16[8,512,512]{2,1,0:T(8,128)(2,1)S(1)} %get-tuple-element.65.old1.mx_ref, bf16[2,512,128]{2,1,0:T(8,128)(2,1)S(1)} %get-tuple-element.70.c_ref, ...), custom_call_target="tpu_custom_call", output_to_operand_aliasing={{0}: (8, {})} | custom-call | flops 268435456 | bytes 1572864 | tf_op jit(solution)/shard_map/out/pallas_call | solution.py:790
  32.0 1.8 %more.7 = (bf16[8,512,512]{2,1,0:T(8,128)(2,1)S(1)}, f32[8,128,512]{2,1,0:T(8,128)S(1)}) custom-call(bf16[512,4096]{1,0:T(8,128)(2,1)S(1)} %get-tuple-element.55.x_ref, bf16[8,4608]{1,0:T(8,128)(2,1)S(1)} %collective-permute-done.rim_ref, f32[4,4096]{1,0:T(4,128)S(1)} %copy-done, ...), custom_call_target="tpu_custom_call", output_to_operand_aliasing={{0}: (7, {}), {1}: (8, {})} | custom-call | flops 268435456 | bytes 2097152 | tf_op jit(solution)/shard_map/more/pallas_call | solution.py:746
  34.2 1.1 %out.18 = (bf16[512,4096]{1,0:T(8,128)(2,1)}, bf16[512,512]{1,0:T(8,128)(2,1)S(1)}) custom-call(f32[8,2,512]{2,1,0:T(2,128)S(1)} %get-tuple-element.54.fade_ref, bf16[8,512,512]{2,1,0:T(8,128)(2,1)S(1)} %get-tuple-element.67.mx_ref, bf16[2,512,128]{2,1,0:T(8,128)(2,1)S(1)} %get-tuple-element.70.c_ref, ...), custom_call_target="tpu_custom_call", output_to_operand_aliasing={{0}: (8, {})} | custom-call | flops 268435456 | bytes 1572864 | tf_op jit(solution)/shard_map/out/pallas_call | solution.py:790
  35.3 3.4 %collective-permute-done.5.recv_ref = bf16[128,512]{1,0:T(8,128)(2,1)S(1)} collective-permute-done((bf16[128,512]{1,0:T(8,128)(2,1)S(1)}, bf16[128,512]{1,0:T(8,128)(2,1)S(1)}, u32[]{:S(2)}, u32[]{:S(2)}) %collective-permute-start.5) | collective-permute-done | bytes 131104 | tf_op jit(solution)/shard_map/ppermute | solution.py:817
  38.8 1.1 %out.19 = (bf16[512,4096]{1,0:T(8,128)(2,1)}, bf16[512,512]{1,0:T(8,128)(2,1)S(1)}) custom-call(f32[8,2,512]{2,1,0:T(2,128)S(1)} %get-tuple-element.54.fade_ref, bf16[8,512,512]{2,1,0:T(8,128)(2,1)S(1)} %get-tuple-element.67.mx_ref, bf16[2,512,128]{2,1,0:T(8,128)(2,1)S(1)} %get-tuple-element.70.c_ref, ...), custom_call_target="tpu_custom_call", output_to_operand_aliasing={{0}: (8, {})} | custom-call | flops 268435456 | bytes 1572864 | tf_op jit(solution)/shard_map/out/pallas_call | solution.py:790
  39.9 1.1 %out.20 = (bf16[512,4096]{1,0:T(8,128)(2,1)}, bf16[512,512]{1,0:T(8,128)(2,1)S(1)}) custom-call(f32[8,2,512]{2,1,0:T(2,128)S(1)} %get-tuple-element.54.fade_ref, bf16[8,512,512]{2,1,0:T(8,128)(2,1)S(1)} %get-tuple-element.67.mx_ref, bf16[2,512,128]{2,1,0:T(8,128)(2,1)S(1)} %get-tuple-element.70.c_ref, ...), custom_call_target="tpu_custom_call", output_to_operand_aliasing={{0}: (8, {})} | custom-call | flops 268435456 | bytes 1572864 | tf_op jit(solution)/shard_map/out/pallas_call | solution.py:790
  42.0 4.6 %collective-permute-done.7.recv_ref = bf16[128,512]{1,0:T(8,128)(2,1)S(1)} collective-permute-done((bf16[128,512]{1,0:T(8,128)(2,1)S(1)}, bf16[128,512]{1,0:T(8,128)(2,1)S(1)}, u32[]{:S(2)}, u32[]{:S(2)}) %collective-permute-start.7) | collective-permute-done | bytes 131104 | tf_op jit(solution)/shard_map/ppermute | solution.py:817
  46.7 1.1 %out.22 = (bf16[512,4096]{1,0:T(8,128)(2,1)}, bf16[512,512]{1,0:T(8,128)(2,1)S(1)}) custom-call(f32[8,2,512]{2,1,0:T(2,128)S(1)} %get-tuple-element.54.fade_ref, bf16[8,512,512]{2,1,0:T(8,128)(2,1)S(1)} %get-tuple-element.67.mx_ref, bf16[2,512,128]{2,1,0:T(8,128)(2,1)S(1)} %get-tuple-element.70.c_ref, ...), custom_call_target="tpu_custom_call", output_to_operand_aliasing={{0}: (8, {})} | custom-call | flops 268435456 | bytes 1572864 | tf_op jit(solution)/shard_map/out/pallas_call | solution.py:790
  49.3 4.1 %collective-permute-done.9.recv_ref = bf16[128,512]{1,0:T(8,128)(2,1)S(1)} collective-permute-done((bf16[128,512]{1,0:T(8,128)(2,1)S(1)}, bf16[128,512]{1,0:T(8,128)(2,1)S(1)}, u32[]{:S(2)}, u32[]{:S(2)}) %collective-permute-start.9) | collective-permute-done | bytes 131104 | tf_op jit(solution)/shard_map/ppermute | solution.py:817
  53.7 1.1 %collective-permute-done.12.recv_ref = bf16[128,512]{1,0:T(8,128)(2,1)S(1)} collective-permute-done((bf16[128,512]{1,0:T(8,128)(2,1)S(1)}, bf16[128,512]{1,0:T(8,128)(2,1)S(1)}, u32[]{:S(2)}, u32[]{:S(2)}) %collective-permute-start.12) | collective-permute-done | bytes 131104 | tf_op jit(solution)/shard_map/ppermute | solution.py:817
  54.9 3.7 %collective-permute-done.11.recv_ref = bf16[128,512]{1,0:T(8,128)(2,1)S(1)} collective-permute-done((bf16[128,512]{1,0:T(8,128)(2,1)S(1)}, bf16[128,512]{1,0:T(8,128)(2,1)S(1)}, u32[]{:S(2)}, u32[]{:S(2)}) %collective-permute-start.11) | collective-permute-done | bytes 131104 | tf_op jit(solution)/shard_map/ppermute | solution.py:817
  (42 shorter events, 9.5 us)
Async XLA Ops:
  0.0 9.6 %copy-start = (f32[4,4096]{1,0:T(4,128)S(1)}, f32[4,4096]{1,0:T(4,128)}, u32[]{:S(2)}) copy-start(f32[4,4096]{1,0:T(4,128)} %wx_ref.9) | copy-start | bytes 196612
  0.0 9.6 %copy-start.1 = (f32[4096]{0:T(1024)S(1)}, f32[4096]{0:T(1024)}, u32[]{:S(2)}) copy-start(f32[4096]{0:T(1024)} %param.18) | copy-start | bytes 49156
  1.6 8.0 %collective-permute-start = (bf16[8,4608]{1,0:T(8,128)(2,1)S(1)}, bf16[8,4608]{1,0:T(8,128)(2,1)S(1)}, u32[]{:S(2)}, u32[]{:S(2)}) collective-permute-start(bf16[8,4608]{1,0:T(8,128)(2,1)S(1)} %pad_maximum_fusion), channel_id=1, source_target_pairs={{0,4},{4,8},{8,12},{12,0},{1,5},{5,9},{9,13},{13,1},{2,6},{6,10},{... | collective-permute-start | bytes 221192 | tf_op jit(solution)/shard_map/ppermute | solution.py:706
  11.6 5.6 %collective-permute-start.1 = (bf16[128,512]{1,0:T(8,128)(2,1)S(1)}, bf16[128,512]{1,0:T(8,128)(2,1)S(1)}, u32[]{:S(2)}, u32[]{:S(2)}) collective-permute-start(bf16[128,512]{1,0:T(8,128)(2,1)S(1)} %get-tuple-element.69.recv_ref), channel_id=1, source_target_pairs={{0,4},{4,0},{8,12},{12,8},{1,5},{5,1},{9,13},{13,9},{2,6},{6,2},{1... | collective-permute-start | bytes 393224 | tf_op jit(solution)/shard_map/ppermute | solution.py:761
  14.2 8.4 %collective-permute-start.2 = (bf16[128,512]{1,0:T(8,128)(2,1)S(1)}, bf16[128,512]{1,0:T(8,128)(2,1)S(1)}, u32[]{:S(2)}, u32[]{:S(2)}) collective-permute-start(bf16[128,512]{1,0:T(8,128)(2,1)S(1)} %get-tuple-element.74.recv_ref), channel_id=1, source_target_pairs={{0,4},{4,0},{8,12},{12,8},{1,5},{5,1},{9,13},{13,9},{2,6},{6,2},{1... | collective-permute-start | bytes 393224 | tf_op jit(solution)/shard_map/ppermute | solution.py:765
  17.2 10.0 %collective-permute-start.4 = (bf16[128,512]{1,0:T(8,128)(2,1)S(1)}, bf16[128,512]{1,0:T(8,128)(2,1)S(1)}, u32[]{:S(2)}, u32[]{:S(2)}) collective-permute-start(bf16[128,512]{1,0:T(8,128)(2,1)S(1)} %join.10.after_ref), channel_id=1, source_target_pairs={{0,4},{4,8},{8,12},{12,0},{1,5},{5,9},{9,13},{13,1},{2,6},{6,10},{... | collective-permute-start | bytes 393224 | tf_op jit(solution)/shard_map/ppermute | solution.py:817
  22.6 7.8 %collective-permute-start.3 = (bf16[128,512]{1,0:T(8,128)(2,1)S(1)}, bf16[128,512]{1,0:T(8,128)(2,1)S(1)}, u32[]{:S(2)}, u32[]{:S(2)}) collective-permute-start(bf16[128,512]{1,0:T(8,128)(2,1)S(1)} %join.11), channel_id=1, source_target_pairs={{0,4},{4,8},{8,12},{12,0},{1,5},{5,9},{9,13},{13,1},{2,6},{6,10},{... | collective-permute-start | bytes 393224 | tf_op jit(solution)/shard_map/ppermute | solution.py:817
  27.2 6.8 %collective-permute-start.6 = (bf16[128,512]{1,0:T(8,128)(2,1)S(1)}, bf16[128,512]{1,0:T(8,128)(2,1)S(1)}, u32[]{:S(2)}, u32[]{:S(2)}) collective-permute-start(bf16[128,512]{1,0:T(8,128)(2,1)S(1)} %join.13), channel_id=1, source_target_pairs={{0,4},{4,8},{8,12},{12,0},{1,5},{5,9},{9,13},{13,1},{2,6},{6,10},{... | collective-permute-start | bytes 393224 | tf_op jit(solution)/shard_map/ppermute | solution.py:817
  30.5 8.2 %collective-permute-start.5 = (bf16[128,512]{1,0:T(8,128)(2,1)S(1)}, bf16[128,512]{1,0:T(8,128)(2,1)S(1)}, u32[]{:S(2)}, u32[]{:S(2)}) collective-permute-start(bf16[128,512]{1,0:T(8,128)(2,1)S(1)} %join.12), channel_id=1, source_target_pairs={{0,4},{4,8},{8,12},{12,0},{1,5},{5,9},{9,13},{13,1},{2,6},{6,10},{... | collective-permute-start | bytes 393224 | tf_op jit(solution)/shard_map/ppermute | solution.py:817
  34.1 6.9 %collective-permute-start.8 = (bf16[128,512]{1,0:T(8,128)(2,1)S(1)}, bf16[128,512]{1,0:T(8,128)(2,1)S(1)}, u32[]{:S(2)}, u32[]{:S(2)}) collective-permute-start(bf16[128,512]{1,0:T(8,128)(2,1)S(1)} %join.15), channel_id=1, source_target_pairs={{0,4},{4,8},{8,12},{12,0},{1,5},{5,9},{9,13},{13,1},{2,6},{6,10},{... | collective-permute-start | bytes 393224 | tf_op jit(solution)/shard_map/ppermute | solution.py:817
  38.7 7.9 %collective-permute-start.7 = (bf16[128,512]{1,0:T(8,128)(2,1)S(1)}, bf16[128,512]{1,0:T(8,128)(2,1)S(1)}, u32[]{:S(2)}, u32[]{:S(2)}) collective-permute-start(bf16[128,512]{1,0:T(8,128)(2,1)S(1)} %join.14), channel_id=1, source_target_pairs={{0,4},{4,8},{8,12},{12,0},{1,5},{5,9},{9,13},{13,1},{2,6},{6,10},{... | collective-permute-start | bytes 393224 | tf_op jit(solution)/shard_map/ppermute | solution.py:817
  41.0 8.1 %collective-permute-start.10 = (bf16[128,512]{1,0:T(8,128)(2,1)S(1)}, bf16[128,512]{1,0:T(8,128)(2,1)S(1)}, u32[]{:S(2)}, u32[]{:S(2)}) collective-permute-start(bf16[128,512]{1,0:T(8,128)(2,1)S(1)} %join.17), channel_id=1, source_target_pairs={{0,4},{4,8},{8,12},{12,0},{1,5},{5,9},{9,13},{13,1},{2,6},{6,10},{... | collective-permute-start | bytes 393224 | tf_op jit(solution)/shard_map/ppermute | solution.py:817
  46.6 6.9 %collective-permute-start.9 = (bf16[128,512]{1,0:T(8,128)(2,1)S(1)}, bf16[128,512]{1,0:T(8,128)(2,1)S(1)}, u32[]{:S(2)}, u32[]{:S(2)}) collective-permute-start(bf16[128,512]{1,0:T(8,128)(2,1)S(1)} %join.16), channel_id=1, source_target_pairs={{0,4},{4,8},{8,12},{12,0},{1,5},{5,9},{9,13},{13,1},{2,6},{6,10},{... | collective-permute-start | bytes 393224 | tf_op jit(solution)/shard_map/ppermute | solution.py:817
  49.2 5.7 %collective-permute-start.12 = (bf16[128,512]{1,0:T(8,128)(2,1)S(1)}, bf16[128,512]{1,0:T(8,128)(2,1)S(1)}, u32[]{:S(2)}, u32[]{:S(2)}) collective-permute-start(bf16[128,512]{1,0:T(8,128)(2,1)S(1)} %join.19), channel_id=1, source_target_pairs={{0,4},{4,0},{8,12},{12,8},{1,5},{5,1},{9,13},{13,9},{2,6},{6,2},{1... | collective-permute-start | bytes 393224 | tf_op jit(solution)/shard_map/ppermute | solution.py:817
  53.5 5.0 %collective-permute-start.11 = (bf16[128,512]{1,0:T(8,128)(2,1)S(1)}, bf16[128,512]{1,0:T(8,128)(2,1)S(1)}, u32[]{:S(2)}, u32[]{:S(2)}) collective-permute-start(bf16[128,512]{1,0:T(8,128)(2,1)S(1)} %join.18), channel_id=1, source_target_pairs={{0,4},{4,0},{8,12},{12,8},{1,5},{5,1},{9,13},{13,9},{2,6},{6,2},{1... | collective-permute-start | bytes 393224 | tf_op jit(solution)/shard_map/ppermute | solution.py:817

commit v6 on v5

--- a/solution.py
+++ b/solution.py
@@ -31,6 +31,31 @@
 
 def silu_half(u):
     return u + u * jnp.tanh(u)
+
+
+def doc_at(pos, starts_ref):
+    count = jnp.int32(-1)
+    for j in range(starts_ref.shape[0]):
+        count = count + (pos >= starts_ref[j]).astype(jnp.int32)
+    return count
+
+
+def column_of(ref):
+    heads = ref.shape[0]
+    index = lax.broadcasted_iota(jnp.int32, (heads, 1), 0)
+    column = jnp.zeros((heads, 1), F32)
+    for h in range(heads):
+        column = jnp.where(index == h, ref[h], column)
+    return column
+
+
+def split(value, parts):
+    pieces = []
+    for _ in range(parts - 1):
+        piece = value.astype(BF16).astype(F32)
+        pieces.append(piece)
+        value = value - piece
+    return pieces + [value]
 
 
 def doc_at(pos, starts_ref):
@@ -697,7 +722,20 @@
     per_group = chunks // groups
     seq = lax.axis_size("seq")
     ring = [(i, (i + 1) % seq) for i in range(seq)]
-    swaps = [(i, i ^ 1) for i in range(seq)] if seq % 2 == 0 else ring
+    cores = lax.axis_size("sub")
+
+    def hop(slot, send):
+        low, high = max(0, slot - per_stream + 1), min(slot, seq - 2)
+        pairs = []
+        for place in range(seq):
+            for core in range(cores):
+                if low <= place <= high + 1:
+                    to = (place + 1 if place <= high else low) * cores + core
+                else:
+                    to = place * cores + (core + 1) % cores
+                pairs.append((place * cores + core, to))
+        return lax.ppermute(send, ("seq", "sub"), pairs)
+
     streams = 2
     per_stream = chunks // streams
     slots = per_stream + seq - 2
@@ -758,11 +796,11 @@
         )(x_near, rim, conv_x, bias_x, shift, scale, bt, near(mixed_x), near(end))
 
     begun = [send]
-    flying = [lax.ppermute(send, "seq", swaps)]
+    flying = [hop(0, send)]
     for s in range(1, streams):
         mixed_x, end, send = more([s * per_stream], 1, mixed_x, end)
         begun.append(send)
-        flying.append(lax.ppermute(send, "seq", swaps))
+        flying.append(hop(0, send))
 
     def scores(after):
         return pl.pallas_call(
@@ -814,7 +852,7 @@
             recv = flying[s]
             if turn < slots:
                 send = join(turn, s, recv, token)
-                flying[s] = lax.ppermute(send, "seq", swaps if turn == slots - 1 else ring)
+                flying[s] = hop(turn, send)
             if turn == 1 and s == 0:
                 mixed_c, score = scores(send)
             todo = [(turn, s, recv)]

time: 59.9 us -> 56.2 us (0.938)
  the two profiles are of different devices: /device:TPU:0 before, /device:TPU:24 now
where the time goes in v6:
time: 56.2 us; the launch traced here: 55.8 us
  Pallas kernels  26.9 us (48%)
  starting transfers between devices  22.9 us (41%)
  waiting for transfers between devices  2.78 us (5%)
  local copies, waits for them, and re-layouts  2.72 us (5%)
    ppermute x12, starting transfers between devices, hop(): return lax.ppermute(send, ('seq', 'sub'), pairs)  22.9 us
    pallas_call x14, Pallas kernels, output(): pl.pallas_call(functools.partial(out_kernel, turn=turn, stream=s, before=...  12.6 us
    pallas_call x4, Pallas kernels, more(): pl.pallas_call(functools.partial(more_kernel, heads=heads, per_group=per_...  6.25 us
    pallas_call x1, Pallas kernels, per_device(): pl.pallas_call(params_kernel, in_specs=[SMEM] * 4 + [VMEM, ANY], out_spec...  3.75 us
    ppermute x12, waiting for transfers between devices, hop(): return lax.ppermute(send, ('seq', 'sub'), pairs)  2.77 us
    pallas_call x1, Pallas kernels, per_device(): pl.pallas_call(functools.partial(first_kernel, heads=heads), in_specs=[VM...  1.96 us
    unnamed x7, local copies, waits for them, and re-layouts  1.88 us
    pallas_call x1, Pallas kernels, scores(): pl.pallas_call(score_kernel, in_specs=[VMEM] * 7 + [ANY], out_specs=[VMEM...  1.8 us
  transfers between devices with their start and end apart: 13, of which 3 were waited for; matrix products, arithmetic and copies ran while one was open for 2% of the time, Pallas kernels for 40%

profile of v6, /device:TPU:24, one launch (start us, length us, event | category | flops | bytes accessed | tf_op | source)
XLA Modules:
  0.0 55.8 jit_solution(15854016409600734868)
XLA Ops:
  1.7 1.1 %copy.34 = bf16[64,8,2,256]{3,1,2,0:T(8,128)(2,1)S(1)} copy(bf16[64,8,2,256]{3,2,1,0:T(2,128)(2,1)} %bitcast.13) | data formatting | bytes 1048576
  2.8 3.8 %params.1 = (bf16[512,128]{1,0:T(8,128)(2,1)S(1)}, f32[512,128]{1,0:T(8,128)S(1)}, f32[8,4,512]{2,1,0:T(4,128)S(1)}, f32[8,2,512]{2,1,0:T(2,128)S(1)}, bf16[4,38...) custom-call(s32[4]{0:T(128)} %starts_ref.1, f32[32]{0:T(128)} %bias_ref.1, ...), custom_call_target="tpu_custom_call" | custom-call | tf_op jit(solution)/shard_map/params/pallas_call | solution.py:747
  6.6 2.0 %first.1 = (bf16[8,512,512]{2,1,0:T(8,128)(2,1)S(1)}, f32[8,128,512]{2,1,0:T(8,128)S(1)}, bf16[128,512]{1,0:T(8,128)(2,1)S(1)}, bf16[2,128,512]{2,1,0:T(8,128)(2,1)S(1)}) custom-call(bf16[512,4096]{1,0:T(8,128)(2,1)S(1)} %get-tuple-element.55.x_ref, bf16[8,4608]{1,0:T(8,128)(2,1)S(1)} %collective-permute-done.rim_ref, f32[4,4096]{1,0:T(4,128)S(1)} %copy-done, ...), custom_call_target="tpu_custom_call" | custom-call | tf_op jit(solution)/shard_map/first/pallas_call | solution.py:770
  8.6 0.9 %more.4 = (bf16[8,512,512]{2,1,0:T(8,128)(2,1)S(1)}, f32[8,128,512]{2,1,0:T(8,128)S(1)}, bf16[128,512]{1,0:T(8,128)(2,1)S(1)}) custom-call(bf16[512,4096]{1,0:T(8,128)(2,1)S(1)} %get-tuple-element.55.x_ref, bf16[8,4608]{1,0:T(8,128)(2,1)S(1)} %collective-permute-done.rim_ref, f32[4,4096]{1,0:T(4,128)S(1)} %copy-done, ...), custom_call_target="tpu_custom_call", output_to_operand_aliasing={{0}: (7, {}), {1}: (8, {})} | custom-call | flops 134217728 | bytes 1048576 | tf_op jit(solution)/shard_map/more/pallas_call | solution.py:784
  10.2 1.8 %more.5 = (bf16[8,512,512]{2,1,0:T(8,128)(2,1)S(1)}, f32[8,128,512]{2,1,0:T(8,128)S(1)}) custom-call(bf16[512,4096]{1,0:T(8,128)(2,1)S(1)} %get-tuple-element.55.x_ref, bf16[8,4608]{1,0:T(8,128)(2,1)S(1)} %collective-permute-done.rim_ref, f32[4,4096]{1,0:T(4,128)S(1)} %copy-done, ...), custom_call_target="tpu_custom_call", output_to_operand_aliasing={{0}: (7, {}), {1}: (8, {})} | custom-call | flops 268435456 | bytes 2097152 | tf_op jit(solution)/shard_map/more/pallas_call | solution.py:784
  12.1 1.8 %score.1 = (bf16[2,512,128]{2,1,0:T(8,128)(2,1)S(1)}, f32[2,512,512]{2,1,0:T(8,128)S(1)}) custom-call(bf16[8,4608]{1,0:T(8,128)(2,1)S(1)} %collective-permute-done.rim_ref, bf16[4,384,256]{2,1,0:T(8,128)(2,1)S(1)} %get-tuple-element.56.shift_ref, f32[512,512]{1,0:T(8,128)S(1)} %get-tuple-element.68.keep_ref, bf16[512,512]{1,0:T(8,128)(2,1)S(1)} %bitcast.7, ...), custom_call_target="tpu_custom_call" | custom-call | tf_op jit(solution)/shard_map/score/pallas_call | solution.py:806
  14.6 1.8 %more.6 = (bf16[8,512,512]{2,1,0:T(8,128)(2,1)S(1)}, f32[8,128,512]{2,1,0:T(8,128)S(1)}) custom-call(bf16[512,4096]{1,0:T(8,128)(2,1)S(1)} %get-tuple-element.55.x_ref, bf16[8,4608]{1,0:T(8,128)(2,1)S(1)} %collective-permute-done.rim_ref, f32[4,4096]{1,0:T(4,128)S(1)} %copy-done, ...), custom_call_target="tpu_custom_call", output_to_operand_aliasing={{0}: (7, {}), {1}: (8, {})} | custom-call | flops 268435456 | bytes 2097152 | tf_op jit(solution)/shard_map/more/pallas_call | solution.py:784
  16.5 8.0 %collective-permute-start.6 = (bf16[128,512]{1,0:T(8,128)(2,1)S(1)}, bf16[128,512]{1,0:T(8,128)(2,1)S(1)}, u32[]{:S(2)}, u32[]{:S(2)}) collective-permute-start(bf16[128,512]{1,0:T(8,128)(2,1)S(1)} %join.13), channel_id=1, source_target_pairs={{0,4},{1,5},{4,8},{5,9},{8,12},{9,13},{12,0},{13,1},{2,6},{3,7},{6... | collective-permute-start | bytes 393224 | tf_op jit(solution)/shard_map/ppermute | solution.py:737
  24.6 7.0 %collective-permute-start.5 = (bf16[128,512]{1,0:T(8,128)(2,1)S(1)}, bf16[128,512]{1,0:T(8,128)(2,1)S(1)}, u32[]{:S(2)}, u32[]{:S(2)}) collective-permute-start(bf16[128,512]{1,0:T(8,128)(2,1)S(1)} %join.12), channel_id=1, source_target_pairs={{0,4},{1,5},{4,8},{5,9},{8,12},{9,13},{12,0},{13,1},{2,6},{3,7},{6... | collective-permute-start | bytes 393224 | tf_op jit(solution)/shard_map/ppermute | solution.py:737
  31.7 1.8 %more.7 = (bf16[8,512,512]{2,1,0:T(8,128)(2,1)S(1)}, f32[8,128,512]{2,1,0:T(8,128)S(1)}) custom-call(bf16[512,4096]{1,0:T(8,128)(2,1)S(1)} %get-tuple-element.55.x_ref, bf16[8,4608]{1,0:T(8,128)(2,1)S(1)} %collective-permute-done.rim_ref, f32[4,4096]{1,0:T(4,128)S(1)} %copy-done, ...), custom_call_target="tpu_custom_call", output_to_operand_aliasing={{0}: (7, {}), {1}: (8, {})} | custom-call | flops 268435456 | bytes 2097152 | tf_op jit(solution)/shard_map/more/pallas_call | solution.py:784
  33.5 1.3 %collective-permute-start.8 = (bf16[128,512]{1,0:T(8,128)(2,1)S(1)}, bf16[128,512]{1,0:T(8,128)(2,1)S(1)}, u32[]{:S(2)}, u32[]{:S(2)}) collective-permute-start(bf16[128,512]{1,0:T(8,128)(2,1)S(1)} %join.15), channel_id=1, source_target_pairs={{0,4},{1,5},{4,8},{5,9},{8,12},{9,13},{12,0},{13,1},{2,6},{3,7},{6... | collective-permute-start | bytes 393224 | tf_op jit(solution)/shard_map/ppermute | solution.py:737
  34.8 1.1 %out.18 = (bf16[512,4096]{1,0:T(8,128)(2,1)}, bf16[512,512]{1,0:T(8,128)(2,1)S(1)}) custom-call(f32[8,2,512]{2,1,0:T(2,128)S(1)} %get-tuple-element.54.fade_ref, bf16[8,512,512]{2,1,0:T(8,128)(2,1)S(1)} %get-tuple-element.67.mx_ref, bf16[2,512,128]{2,1,0:T(8,128)(2,1)S(1)} %get-tuple-element.70.c_ref, ...), custom_call_target="tpu_custom_call", output_to_operand_aliasing={{0}: (8, {})} | custom-call | flops 268435456 | bytes 1572864 | tf_op jit(solution)/shard_map/out/pallas_call | solution.py:828
  35.9 3.1 %collective-permute-start.7 = (bf16[128,512]{1,0:T(8,128)(2,1)S(1)}, bf16[128,512]{1,0:T(8,128)(2,1)S(1)}, u32[]{:S(2)}, u32[]{:S(2)}) collective-permute-start(bf16[128,512]{1,0:T(8,128)(2,1)S(1)} %join.14), channel_id=1, source_target_pairs={{0,4},{1,5},{4,8},{5,9},{8,12},{9,13},{12,0},{13,1},{2,6},{3,7},{6... | collective-permute-start | bytes 393224 | tf_op jit(solution)/shard_map/ppermute | solution.py:737
  39.0 1.1 %out.19 = (bf16[512,4096]{1,0:T(8,128)(2,1)}, bf16[512,512]{1,0:T(8,128)(2,1)S(1)}) custom-call(f32[8,2,512]{2,1,0:T(2,128)S(1)} %get-tuple-element.54.fade_ref, bf16[8,512,512]{2,1,0:T(8,128)(2,1)S(1)} %get-tuple-element.67.mx_ref, bf16[2,512,128]{2,1,0:T(8,128)(2,1)S(1)} %get-tuple-element.70.c_ref, ...), custom_call_target="tpu_custom_call", output_to_operand_aliasing={{0}: (8, {})} | custom-call | flops 268435456 | bytes 1572864 | tf_op jit(solution)/shard_map/out/pallas_call | solution.py:828
  41.1 1.1 %out.21 = (bf16[512,4096]{1,0:T(8,128)(2,1)}, bf16[512,512]{1,0:T(8,128)(2,1)S(1)}) custom-call(f32[8,2,512]{2,1,0:T(2,128)S(1)} %get-tuple-element.54.fade_ref, bf16[8,512,512]{2,1,0:T(8,128)(2,1)S(1)} %get-tuple-element.67.mx_ref, bf16[2,512,128]{2,1,0:T(8,128)(2,1)S(1)} %get-tuple-element.70.c_ref, ...), custom_call_target="tpu_custom_call", output_to_operand_aliasing={{0}: (8, {})} | custom-call | flops 268435456 | bytes 1572864 | tf_op jit(solution)/shard_map/out/pallas_call | solution.py:828
  43.8 1.1 %out.23 = (bf16[512,4096]{1,0:T(8,128)(2,1)}, bf16[512,512]{1,0:T(8,128)(2,1)S(1)}) custom-call(f32[8,2,512]{2,1,0:T(2,128)S(1)} %get-tuple-element.54.fade_ref, bf16[8,512,512]{2,1,0:T(8,128)(2,1)S(1)} %get-tuple-element.67.mx_ref, bf16[2,512,128]{2,1,0:T(8,128)(2,1)S(1)} %get-tuple-element.70.c_ref, ...), custom_call_target="tpu_custom_call", output_to_operand_aliasing={{0}: (8, {})} | custom-call | flops 268435456 | bytes 1572864 | tf_op jit(solution)/shard_map/out/pallas_call | solution.py:828
  44.9 1.1 %collective-permute-done.10.recv_ref = bf16[128,512]{1,0:T(8,128)(2,1)S(1)} collective-permute-done((bf16[128,512]{1,0:T(8,128)(2,1)S(1)}, bf16[128,512]{1,0:T(8,128)(2,1)S(1)}, u32[]{:S(2)}, u32[]{:S(2)}) %collective-permute-start.10) | collective-permute-done | bytes 131104 | tf_op jit(solution)/shard_map/ppermute | solution.py:737
  46.1 0.9 %collective-permute-start.12 = (bf16[128,512]{1,0:T(8,128)(2,1)S(1)}, bf16[128,512]{1,0:T(8,128)(2,1)S(1)}, u32[]{:S(2)}, u32[]{:S(2)}) collective-permute-start(bf16[128,512]{1,0:T(8,128)(2,1)S(1)} %join.19), channel_id=1, source_target_pairs={{0,1},{1,0},{4,5},{5,4},{8,12},{9,13},{12,8},{13,9},{2,3},{3,2},{6... | collective-permute-start | bytes 393224 | tf_op jit(solution)/shard_map/ppermute | solution.py:737
  47.0 1.1 %out.24 = (bf16[512,4096]{1,0:T(8,128)(2,1)}, bf16[512,512]{1,0:T(8,128)(2,1)S(1)}) custom-call(f32[8,2,512]{2,1,0:T(2,128)S(1)} %get-tuple-element.54.fade_ref, bf16[8,512,512]{2,1,0:T(8,128)(2,1)S(1)} %get-tuple-element.67.mx_ref, bf16[2,512,128]{2,1,0:T(8,128)(2,1)S(1)} %get-tuple-element.70.c_ref, ...), custom_call_target="tpu_custom_call", output_to_operand_aliasing={{0}: (8, {})} | custom-call | flops 268435456 | bytes 1572864 | tf_op jit(solution)/shard_map/out/pallas_call | solution.py:828
  48.1 1.2 %collective-permute-start.11 = (bf16[128,512]{1,0:T(8,128)(2,1)S(1)}, bf16[128,512]{1,0:T(8,128)(2,1)S(1)}, u32[]{:S(2)}, u32[]{:S(2)}) collective-permute-start(bf16[128,512]{1,0:T(8,128)(2,1)S(1)} %join.18), channel_id=1, source_target_pairs={{0,1},{1,0},{4,5},{5,4},{8,12},{9,13},{12,8},{13,9},{2,3},{3,2},{6... | collective-permute-start | bytes 393224 | tf_op jit(solution)/shard_map/ppermute | solution.py:737
  49.4 1.8 %out.25 = (bf16[512,4096]{1,0:T(8,128)(2,1)}, bf16[512,512]{1,0:T(8,128)(2,1)S(1)}) custom-call(f32[8,2,512]{2,1,0:T(2,128)S(1)} %get-tuple-element.54.fade_ref, bf16[8,512,512]{2,1,0:T(8,128)(2,1)S(1)} %get-tuple-element.67.mx_ref, bf16[2,512,128]{2,1,0:T(8,128)(2,1)S(1)} %get-tuple-element.70.c_ref, ...), custom_call_target="tpu_custom_call", output_to_operand_aliasing={{0}: (8, {})} | custom-call | flops 268435456 | bytes 1572864 | tf_op jit(solution)/shard_map/out/pallas_call | solution.py:828
  51.1 1.1 %out.26 = (bf16[512,4096]{1,0:T(8,128)(2,1)}, bf16[512,512]{1,0:T(8,128)(2,1)S(1)}) custom-call(f32[8,2,512]{2,1,0:T(2,128)S(1)} %get-tuple-element.54.fade_ref, bf16[8,512,512]{2,1,0:T(8,128)(2,1)S(1)} %get-tuple-element.67.mx_ref, bf16[2,512,128]{2,1,0:T(8,128)(2,1)S(1)} %get-tuple-element.70.c_ref, ...), custom_call_target="tpu_custom_call", output_to_operand_aliasing={{0}: (8, {})} | custom-call | flops 268435456 | bytes 1572864 | tf_op jit(solution)/shard_map/out/pallas_call | solution.py:828
  52.2 0.9 %collective-permute-done.11.recv_ref = bf16[128,512]{1,0:T(8,128)(2,1)S(1)} collective-permute-done((bf16[128,512]{1,0:T(8,128)(2,1)S(1)}, bf16[128,512]{1,0:T(8,128)(2,1)S(1)}, u32[]{:S(2)}, u32[]{:S(2)}) %collective-permute-start.11) | collective-permute-done | bytes 131104 | tf_op jit(solution)/shard_map/ppermute | solution.py:737
  53.2 2.5 %out.27 = (bf16[512,4096]{1,0:T(8,128)(2,1)}, bf16[512,512]{1,0:T(8,128)(2,1)}) custom-call(f32[8,2,512]{2,1,0:T(2,128)S(1)} %get-tuple-element.54.fade_ref, bf16[8,512,512]{2,1,0:T(8,128)(2,1)S(1)} %get-tuple-element.67.mx_ref, bf16[2,512,128]{2,1,0:T(8,128)(2,1)S(1)} %get-tuple-element.70.c_ref, ...), custom_call_target="tpu_custom_call", output_to_operand_aliasing={{0}: (8, {})} | custom-call | flops 268435456 | bytes 1572864 | tf_op jit(solution)/shard_map/out/pallas_call | solution.py:828
  (42 shorter events, 6.1 us)
Async XLA Ops:
  0.0 6.6 %copy-start = (f32[4,4096]{1,0:T(4,128)S(1)}, f32[4,4096]{1,0:T(4,128)}, u32[]{:S(2)}) copy-start(f32[4,4096]{1,0:T(4,128)} %wx_ref.9) | copy-start | bytes 196612
  0.0 6.6 %copy-start.1 = (f32[4096]{0:T(1024)S(1)}, f32[4096]{0:T(1024)}, u32[]{:S(2)}) copy-start(f32[4096]{0:T(1024)} %param.18) | copy-start | bytes 49156
  1.6 5.0 %collective-permute-start = (bf16[8,4608]{1,0:T(8,128)(2,1)S(1)}, bf16[8,4608]{1,0:T(8,128)(2,1)S(1)}, u32[]{:S(2)}, u32[]{:S(2)}) collective-permute-start(bf16[8,4608]{1,0:T(8,128)(2,1)S(1)} %pad_maximum_fusion), channel_id=1, source_target_pairs={{0,4},{4,8},{8,12},{12,0},{1,5},{5,9},{9,13},{13,1},{2,6},{6,10},{... | collective-permute-start | bytes 221192 | tf_op jit(solution)/shard_map/ppermute | solution.py:744
  8.6 3.4 %collective-permute-start.1 = (bf16[128,512]{1,0:T(8,128)(2,1)S(1)}, bf16[128,512]{1,0:T(8,128)(2,1)S(1)}, u32[]{:S(2)}, u32[]{:S(2)}) collective-permute-start(bf16[128,512]{1,0:T(8,128)(2,1)S(1)} %get-tuple-element.69.recv_ref), channel_id=1, source_target_pairs={{0,4},{1,5},{4,0},{5,1},{8,9},{9,8},{12,13},{13,12},{2,6},{3,7},{6... | collective-permute-start | bytes 393224 | tf_op jit(solution)/shard_map/ppermute | solution.py:737
  9.6 4.3 %collective-permute-start.2 = (bf16[128,512]{1,0:T(8,128)(2,1)S(1)}, bf16[128,512]{1,0:T(8,128)(2,1)S(1)}, u32[]{:S(2)}, u32[]{:S(2)}) collective-permute-start(bf16[128,512]{1,0:T(8,128)(2,1)S(1)} %get-tuple-element.74.recv_ref), channel_id=1, source_target_pairs={{0,4},{1,5},{4,0},{5,1},{8,9},{9,8},{12,13},{13,12},{2,6},{3,7},{6... | collective-permute-start | bytes 393224 | tf_op jit(solution)/shard_map/ppermute | solution.py:737
  12.0 4.4 %collective-permute-start.4 = (bf16[128,512]{1,0:T(8,128)(2,1)S(1)}, bf16[128,512]{1,0:T(8,128)(2,1)S(1)}, u32[]{:S(2)}, u32[]{:S(2)}) collective-permute-start(bf16[128,512]{1,0:T(8,128)(2,1)S(1)} %join.10.after_ref), channel_id=1, source_target_pairs={{0,4},{1,5},{4,8},{5,9},{8,0},{9,1},{12,13},{13,12},{2,6},{3,7},{6... | collective-permute-start | bytes 393224 | tf_op jit(solution)/shard_map/ppermute | solution.py:737
  14.0 10.5 %collective-permute-start.3 = (bf16[128,512]{1,0:T(8,128)(2,1)S(1)}, bf16[128,512]{1,0:T(8,128)(2,1)S(1)}, u32[]{:S(2)}, u32[]{:S(2)}) collective-permute-start(bf16[128,512]{1,0:T(8,128)(2,1)S(1)} %join.11), channel_id=1, source_target_pairs={{0,4},{1,5},{4,8},{5,9},{8,0},{9,1},{12,13},{13,12},{2,6},{3,7},{6... | collective-permute-start | bytes 393224 | tf_op jit(solution)/shard_map/ppermute | solution.py:737
  16.5 17.0 %collective-permute-start.6 = (bf16[128,512]{1,0:T(8,128)(2,1)S(1)}, bf16[128,512]{1,0:T(8,128)(2,1)S(1)}, u32[]{:S(2)}, u32[]{:S(2)}) collective-permute-start(bf16[128,512]{1,0:T(8,128)(2,1)S(1)} %join.13), channel_id=1, source_target_pairs={{0,4},{1,5},{4,8},{5,9},{8,12},{9,13},{12,0},{13,1},{2,6},{3,7},{6... | collective-permute-start | bytes 393224 | tf_op jit(solution)/shard_map/ppermute | solution.py:737
  24.6 11.3 %collective-permute-start.5 = (bf16[128,512]{1,0:T(8,128)(2,1)S(1)}, bf16[128,512]{1,0:T(8,128)(2,1)S(1)}, u32[]{:S(2)}, u32[]{:S(2)}) collective-permute-start(bf16[128,512]{1,0:T(8,128)(2,1)S(1)} %join.12), channel_id=1, source_target_pairs={{0,4},{1,5},{4,8},{5,9},{8,12},{9,13},{12,0},{13,1},{2,6},{3,7},{6... | collective-permute-start | bytes 393224 | tf_op jit(solution)/shard_map/ppermute | solution.py:737
  33.5 7.4 %collective-permute-start.8 = (bf16[128,512]{1,0:T(8,128)(2,1)S(1)}, bf16[128,512]{1,0:T(8,128)(2,1)S(1)}, u32[]{:S(2)}, u32[]{:S(2)}) collective-permute-start(bf16[128,512]{1,0:T(8,128)(2,1)S(1)} %join.15), channel_id=1, source_target_pairs={{0,4},{1,5},{4,8},{5,9},{8,12},{9,13},{12,0},{13,1},{2,6},{3,7},{6... | collective-permute-start | bytes 393224 | tf_op jit(solution)/shard_map/ppermute | solution.py:737
  35.9 6.9 %collective-permute-start.7 = (bf16[128,512]{1,0:T(8,128)(2,1)S(1)}, bf16[128,512]{1,0:T(8,128)(2,1)S(1)}, u32[]{:S(2)}, u32[]{:S(2)}) collective-permute-start(bf16[128,512]{1,0:T(8,128)(2,1)S(1)} %join.14), channel_id=1, source_target_pairs={{0,4},{1,5},{4,8},{5,9},{8,12},{9,13},{12,0},{13,1},{2,6},{3,7},{6... | collective-permute-start | bytes 393224 | tf_op jit(solution)/shard_map/ppermute | solution.py:737
  41.0 5.0 %collective-permute-start.10 = (bf16[128,512]{1,0:T(8,128)(2,1)S(1)}, bf16[128,512]{1,0:T(8,128)(2,1)S(1)}, u32[]{:S(2)}, u32[]{:S(2)}) collective-permute-start(bf16[128,512]{1,0:T(8,128)(2,1)S(1)} %join.17), channel_id=1, source_target_pairs={{0,1},{1,0},{4,8},{5,9},{8,12},{9,13},{12,4},{13,5},{2,3},{3,2},{6... | collective-permute-start | bytes 393224 | tf_op jit(solution)/shard_map/ppermute | solution.py:737
  42.9 5.2 %collective-permute-start.9 = (bf16[128,512]{1,0:T(8,128)(2,1)S(1)}, bf16[128,512]{1,0:T(8,128)(2,1)S(1)}, u32[]{:S(2)}, u32[]{:S(2)}) collective-permute-start(bf16[128,512]{1,0:T(8,128)(2,1)S(1)} %join.16), channel_id=1, source_target_pairs={{0,1},{1,0},{4,8},{5,9},{8,12},{9,13},{12,4},{13,5},{2,3},{3,2},{6... | collective-permute-start | bytes 393224 | tf_op jit(solution)/shard_map/ppermute | solution.py:737
  46.1 5.1 %collective-permute-start.12 = (bf16[128,512]{1,0:T(8,128)(2,1)S(1)}, bf16[128,512]{1,0:T(8,128)(2,1)S(1)}, u32[]{:S(2)}, u32[]{:S(2)}) collective-permute-start(bf16[128,512]{1,0:T(8,128)(2,1)S(1)} %join.19), channel_id=1, source_target_pairs={{0,1},{1,0},{4,5},{5,4},{8,12},{9,13},{12,8},{13,9},{2,3},{3,2},{6... | collective-permute-start | bytes 393224 | tf_op jit(solution)/shard_map/ppermute | solution.py:737
  48.1 5.0 %collective-permute-start.11 = (bf16[128,512]{1,0:T(8,128)(2,1)S(1)}, bf16[128,512]{1,0:T(8,128)(2,1)S(1)}, u32[]{:S(2)}, u32[]{:S(2)}) collective-permute-start(bf16[128,512]{1,0:T(8,128)(2,1)S(1)} %join.18), channel_id=1, source_target_pairs={{0,1},{1,0},{4,5},{5,4},{8,12},{9,13},{12,8},{13,9},{2,3},{3,2},{6... | collective-permute-start | bytes 393224 | tf_op jit(solution)/shard_map/ppermute | solution.py:737

commit v7 on v6

--- a/solution.py
+++ b/solution.py
@@ -31,6 +31,131 @@
 
 def silu_half(u):
     return u + u * jnp.tanh(u)
+
+
+def doc_at(pos, starts_ref):
+    count = jnp.int32(-1)
+    for j in range(starts_ref.shape[0]):
+        count = count + (pos >= starts_ref[j]).astype(jnp.int32)
+    return count
+
+
+def column_of(ref):
+    heads = ref.shape[0]
+    index = lax.broadcasted_iota(jnp.int32, (heads, 1), 0)
+    column = jnp.zeros((heads, 1), F32)
+    for h in range(heads):
+        column = jnp.where(index == h, ref[h], column)
+    return column
+
+
+def split(value, parts):
+    pieces = []
+    for _ in range(parts - 1):
+        piece = value.astype(BF16).astype(F32)
+        pieces.append(piece)
+        value = value - piece
+    return pieces + [value]
+
+
+def doc_at(pos, starts_ref):
+    count = jnp.int32(-1)
+    for j in range(starts_ref.shape[0]):
+        count = count + (pos >= starts_ref[j]).astype(jnp.int32)
+    return count
+
+
+def column_of(ref):
+    heads = ref.shape[0]
+    index = lax.broadcasted_iota(jnp.int32, (heads, 1), 0)
+    column = jnp.zeros((heads, 1), F32)
+    for h in range(heads):
+        column = jnp.where(index == h, ref[h], column)
+    return column
+
+
+def split(value, parts):
+    pieces = []
+    for _ in range(parts - 1):
+        piece = value.astype(BF16).astype(F32)
+        pieces.append(piece)
+        value = value - piece
+    return pieces + [value]
+
+
+def doc_at(pos, starts_ref):
+    count = jnp.int32(-1)
+    for j in range(starts_ref.shape[0]):
+        count = count + (pos >= starts_ref[j]).astype(jnp.int32)
+    return count
+
+
+def column_of(ref):
+    heads = ref.shape[0]
+    index = lax.broadcasted_iota(jnp.int32, (heads, 1), 0)
+    column = jnp.zeros((heads, 1), F32)
+    for h in range(heads):
+        column = jnp.where(index == h, ref[h], column)
+    return column
+
+
+def split(value, parts):
+    pieces = []
+    for _ in range(parts - 1):
+        piece = value.astype(BF16).astype(F32)
+        pieces.append(piece)
+        value = value - piece
+    return pieces + [value]
+
+
+def doc_at(pos, starts_ref):
+    count = jnp.int32(-1)
+    for j in range(starts_ref.shape[0]):
+        count = count + (pos >= starts_ref[j]).astype(jnp.int32)
+    return count
+
+
+def column_of(ref):
+    heads = ref.shape[0]
+    index = lax.broadcasted_iota(jnp.int32, (heads, 1), 0)
+    column = jnp.zeros((heads, 1), F32)
+    for h in range(heads):
+        column = jnp.where(index == h, ref[h], column)
+    return column
+
+
+def split(value, parts):
+    pieces = []
+    for _ in range(parts - 1):
+        piece = value.astype(BF16).astype(F32)
+        pieces.append(piece)
+        value = value - piece
+    return pieces + [value]
+
+
+def doc_at(pos, starts_ref):
+    count = jnp.int32(-1)
+    for j in range(starts_ref.shape[0]):
+        count = count + (pos >= starts_ref[j]).astype(jnp.int32)
+    return count
+
+
+def column_of(ref):
+    heads = ref.shape[0]
+    index = lax.broadcasted_iota(jnp.int32, (heads, 1), 0)
+    column = jnp.zeros((heads, 1), F32)
+    for h in range(heads):
+        column = jnp.where(index == h, ref[h], column)
+    return column
+
+
+def split(value, parts):
+    pieces = []
+    for _ in range(parts - 1):
+        piece = value.astype(BF16).astype(F32)
+        pieces.append(piece)
+        value = value - piece
+    return pieces + [value]
 
 
 def doc_at(pos, starts_ref):
@@ -824,13 +949,13 @@
         )(fade, recv, end, token)
 
     def output(turn, s, recv, before, block, out, mixed_c, score):
-        old = [] if out is None else [block, out]
+        old = [] if out is None else [last_block[-1], out, block]
         return pl.pallas_call(
             functools.partial(
                 out_kernel, turn=turn, stream=s, before=before, final=turn == slots and s == streams - 1,
                 per_stream=per_stream, per_group=per_group, heads=heads,
             ),
-            in_specs=[VMEM] * 7 + [VMEM, ANY][: len(old)],
+            in_specs=[VMEM] * 7 + [VMEM, ANY, ANY][: len(old)],
             out_specs=[ANY, VMEM],
             out_shape=[pltpu.HBM((BLK, width), BF16), shape_of((BLK, CW), BF16)],
             input_output_aliases={8: 0} if old else {},
@@ -842,25 +967,47 @@
             name="out",
         )(fade, mixed_x, mixed_c, score, cols, row_terms, recv, *old)
 
-    out, block, before = None, None, None
+    out, before = None, None
+    last_block = []
     waiting = [(0, s, begun[s]) for s in range(streams)]
     token = bt
+    ready = []
+
+    def flush(ready, before, token, out):
+        for when, which, got in ready:
+            out, token = output(when, which, got, before, token, out, mixed_c, score)
+            last_block.append(token)
+            before = (when, which)
+        return before, token, out
+
     for turn in range(1, slots + 1):
-        if turn < per_stream:
-            mixed_x, end = more([turn + i * per_stream for i in range(streams)], 0, mixed_x, end)
         for s in range(streams):
-            recv = flying[s]
+            if turn < per_stream:
+                mixed_x, end = more([turn + s * per_stream], 0, mixed_x, end)
+            got = flying[s]
             if turn < slots:
-                send = join(turn, s, recv, token)
+                send = join(turn, s, got, token)
                 flying[s] = hop(turn, send)
-            if turn == 1 and s == 0:
-                mixed_c, score = scores(send)
-            todo = [(turn, s, recv)]
-            if waiting and turn >= min(per_stream, slots):
-                todo.insert(0, waiting.pop(0))
-            for when, which, got in todo:
-                out, token = output(when, which, got, before, token, out, mixed_c, score)
-                before = (when, which)
+                token = send
+            elif s == 0:
+                ready = waiting + ready
+                waiting = []
+            if turn == slots - 1 and turn > per_stream and s == 0:
+                before, token, out = flush(ready, before, token, out)
+                ready = []
+            ready.append((turn, s, got))
+            if (turn > per_stream and turn != slots - 1) or turn == slots:
+                before, token, out = flush(ready, before, token, out)
+                ready = []
+        if turn == 1:
+            mixed_c, score = scores(send)
+            token = score
+        if turn == per_stream - 1:
+            ready, waiting = waiting + ready, []
+        if (turn <= per_stream or turn == slots - 1) and ready:
+            keep = 0 if turn == slots - 1 else 1 if turn == per_stream else streams
+            before, token, out = flush(ready[: len(ready) - keep], before, token, out)
+            ready = ready[len(ready) - keep :]
     return out
 
 

time: 56.2 us -> 53.5 us (0.952)
  starting transfers between devices: 22.9 us -> 19.2 us
  waiting for transfers between devices: 2.78 us -> 4.26 us
    ppermute x12, starting transfers between devices: 22.9 us -> 19.1 us  [hop(): return lax.ppermute(send, ('seq', 'sub'), pairs)]
    ppermute x12, waiting for transfers between devices: 2.77 us -> 4.26 us  [hop(): return lax.ppermute(send, ('seq', 'sub'), pairs)]
    pallas_call x14, Pallas kernels: 12.6 us -> 11.9 us  [output(): pl.pallas_call(functools.partial(out_kernel, turn=turn, stream=s, before=...]
    pallas_call x4 -> x7, Pallas kernels: 6.25 us -> 6.61 us  [more(): pl.pallas_call(functools.partial(more_kernel, heads=heads, per_group=per_...]
  transfers between devices with their start and end apart: 13 -> 13, of which waited for: 3 -> 4; matrix products, arithmetic and copies ran while one was open for 2% -> 2% of each run, Pallas kernels for 40% -> 41%
where the time goes in v7:
time: 53.5 us; the launch traced here: 53.2 us
  Pallas kernels  26.5 us (50%)
  starting transfers between devices  19.2 us (36%)
  waiting for transfers between devices  4.26 us (8%)
  local copies, waits for them, and re-layouts  2.72 us (5%)
    ppermute x12, starting transfers between devices, hop(): return lax.ppermute(send, ('seq', 'sub'), pairs)  19.1 us
    pallas_call x14, Pallas kernels, output(): pl.pallas_call(functools.partial(out_kernel, turn=turn, stream=s, before=...  11.9 us
    pallas_call x7, Pallas kernels, more(): pl.pallas_call(functools.partial(more_kernel, heads=heads, per_group=per_...  6.61 us
    ppermute x12, waiting for transfers between devices, hop(): return lax.ppermute(send, ('seq', 'sub'), pairs)  4.26 us
    pallas_call x1, Pallas kernels, per_device(): pl.pallas_call(params_kernel, in_specs=[SMEM] * 4 + [VMEM, ANY], out_spec...  3.75 us
    pallas_call x1, Pallas kernels, per_device(): pl.pallas_call(functools.partial(first_kernel, heads=heads), in_specs=[VM...  1.97 us
    unnamed x7, local copies, waits for them, and re-layouts  1.88 us
    pallas_call x1, Pallas kernels, scores(): pl.pallas_call(score_kernel, in_specs=[VMEM] * 7 + [ANY], out_specs=[VMEM...  1.8 us
  transfers between devices with their start and end apart: 13, of which 4 were waited for; matrix products, arithmetic and copies ran while one was open for 2% of the time, Pallas kernels for 41%

profile of v7, /device:TPU:24, one launch (start us, length us, event | category | flops | bytes accessed | tf_op | source)
XLA Modules:
  0.0 53.2 jit_solution(12666999560327602777)
XLA Ops:
  1.7 1.1 %copy.40 = bf16[64,8,2,256]{3,1,2,0:T(8,128)(2,1)S(1)} copy(bf16[64,8,2,256]{3,2,1,0:T(2,128)(2,1)} %bitcast.16) | data formatting | bytes 1048576
  2.8 3.8 %params.1 = (bf16[512,128]{1,0:T(8,128)(2,1)S(1)}, f32[512,128]{1,0:T(8,128)S(1)}, f32[8,4,512]{2,1,0:T(4,128)S(1)}, f32[8,2,512]{2,1,0:T(2,128)S(1)}, bf16[4,38...) custom-call(s32[4]{0:T(128)} %starts_ref.1, f32[32]{0:T(128)} %bias_ref.1, ...), custom_call_target="tpu_custom_call" | custom-call | tf_op jit(solution)/shard_map/params/pallas_call | solution.py:872
  6.6 2.0 %first.1 = (bf16[8,512,512]{2,1,0:T(8,128)(2,1)S(1)}, f32[8,128,512]{2,1,0:T(8,128)S(1)}, bf16[128,512]{1,0:T(8,128)(2,1)S(1)}, bf16[2,128,512]{2,1,0:T(8,128)(2,1)S(1)}) custom-call(bf16[512,4096]{1,0:T(8,128)(2,1)S(1)} %get-tuple-element.61.x_ref, bf16[8,4608]{1,0:T(8,128)(2,1)S(1)} %collective-permute-done.rim_ref, f32[4,4096]{1,0:T(4,128)S(1)} %copy-done, ...), custom_call_target="tpu_custom_call" | custom-call | tf_op jit(solution)/shard_map/first/pallas_call | solution.py:895
  8.7 0.9 %more.7 = (bf16[8,512,512]{2,1,0:T(8,128)(2,1)S(1)}, f32[8,128,512]{2,1,0:T(8,128)S(1)}, bf16[128,512]{1,0:T(8,128)(2,1)S(1)}) custom-call(bf16[512,4096]{1,0:T(8,128)(2,1)S(1)} %get-tuple-element.61.x_ref, bf16[8,4608]{1,0:T(8,128)(2,1)S(1)} %collective-permute-done.rim_ref, f32[4,4096]{1,0:T(4,128)S(1)} %copy-done, ...), custom_call_target="tpu_custom_call", output_to_operand_aliasing={{0}: (7, {}), {1}: (8, {})} | custom-call | flops 134217728 | bytes 1048576 | tf_op jit(solution)/shard_map/more/pallas_call | solution.py:909
  11.2 0.9 %more.9 = (bf16[8,512,512]{2,1,0:T(8,128)(2,1)S(1)}, f32[8,128,512]{2,1,0:T(8,128)S(1)}) custom-call(bf16[512,4096]{1,0:T(8,128)(2,1)S(1)} %get-tuple-element.61.x_ref, bf16[8,4608]{1,0:T(8,128)(2,1)S(1)} %collective-permute-done.rim_ref, f32[4,4096]{1,0:T(4,128)S(1)} %copy-done, ...), custom_call_target="tpu_custom_call", output_to_operand_aliasing={{0}: (7, {}), {1}: (8, {})} | custom-call | flops 134217728 | bytes 1048576 | tf_op jit(solution)/shard_map/more/pallas_call | solution.py:909
  12.8 1.8 %score.1 = (bf16[2,512,128]{2,1,0:T(8,128)(2,1)S(1)}, f32[2,512,512]{2,1,0:T(8,128)S(1)}) custom-call(bf16[8,4608]{1,0:T(8,128)(2,1)S(1)} %collective-permute-done.rim_ref, bf16[4,384,256]{2,1,0:T(8,128)(2,1)S(1)} %get-tuple-element.62.shift_ref, f32[512,512]{1,0:T(8,128)S(1)} %get-tuple-element.80.keep_ref, bf16[512,512]{1,0:T(8,128)(2,1)S(1)} %bitcast.7, ...), custom_call_target="tpu_custom_call" | custom-call | tf_op jit(solution)/shard_map/score/pallas_call | solution.py:931
  14.6 0.9 %more.10 = (bf16[8,512,512]{2,1,0:T(8,128)(2,1)S(1)}, f32[8,128,512]{2,1,0:T(8,128)S(1)}) custom-call(bf16[512,4096]{1,0:T(8,128)(2,1)S(1)} %get-tuple-element.61.x_ref, bf16[8,4608]{1,0:T(8,128)(2,1)S(1)} %collective-permute-done.rim_ref, f32[4,4096]{1,0:T(4,128)S(1)} %copy-done, ...), custom_call_target="tpu_custom_call", output_to_operand_aliasing={{0}: (7, {}), {1}: (8, {})} | custom-call | flops 134217728 | bytes 1048576 | tf_op jit(solution)/shard_map/more/pallas_call | solution.py:909
  15.6 8.6 %collective-permute-start.6 = (bf16[128,512]{1,0:T(8,128)(2,1)S(1)}, bf16[128,512]{1,0:T(8,128)(2,1)S(1)}, u32[]{:S(2)}, u32[]{:S(2)}) collective-permute-start(bf16[128,512]{1,0:T(8,128)(2,1)S(1)} %join.12.token_ref), channel_id=1, source_target_pairs={{0,4},{1,5},{4,8},{5,9},{8,12},{9,13},{12,0},{13,1},{2,6},{3,7},{6... | collective-permute-start | bytes 393224 | tf_op jit(solution)/shard_map/ppermute | solution.py:862
  25.8 0.9 %more.12 = (bf16[8,512,512]{2,1,0:T(8,128)(2,1)S(1)}, f32[8,128,512]{2,1,0:T(8,128)S(1)}) custom-call(bf16[512,4096]{1,0:T(8,128)(2,1)S(1)} %get-tuple-element.61.x_ref, bf16[8,4608]{1,0:T(8,128)(2,1)S(1)} %collective-permute-done.rim_ref, f32[4,4096]{1,0:T(4,128)S(1)} %copy-done, ...), custom_call_target="tpu_custom_call", output_to_operand_aliasing={{0}: (7, {}), {1}: (8, {})} | custom-call | flops 134217728 | bytes 1048576 | tf_op jit(solution)/shard_map/more/pallas_call | solution.py:909
  27.5 3.5 %collective-permute-start.8 = (bf16[128,512]{1,0:T(8,128)(2,1)S(1)}, bf16[128,512]{1,0:T(8,128)(2,1)S(1)}, u32[]{:S(2)}, u32[]{:S(2)}) collective-permute-start(bf16[128,512]{1,0:T(8,128)(2,1)S(1)} %join.14.token_ref), channel_id=1, source_target_pairs={{0,4},{1,5},{4,8},{5,9},{8,12},{9,13},{12,0},{13,1},{2,6},{3,7},{6... | collective-permute-start | bytes 393224 | tf_op jit(solution)/shard_map/ppermute | solution.py:862
  31.1 1.0 %more.13 = (bf16[8,512,512]{2,1,0:T(8,128)(2,1)S(1)}, f32[8,128,512]{2,1,0:T(8,128)S(1)}) custom-call(bf16[512,4096]{1,0:T(8,128)(2,1)S(1)} %get-tuple-element.61.x_ref, bf16[8,4608]{1,0:T(8,128)(2,1)S(1)} %collective-permute-done.rim_ref, f32[4,4096]{1,0:T(4,128)S(1)} %copy-done, ...), custom_call_target="tpu_custom_call", output_to_operand_aliasing={{0}: (7, {}), {1}: (8, {})} | custom-call | flops 134217728 | bytes 1048576 | tf_op jit(solution)/shard_map/more/pallas_call | solution.py:909
  32.1 1.6 %collective-permute-start.7 = (bf16[128,512]{1,0:T(8,128)(2,1)S(1)}, bf16[128,512]{1,0:T(8,128)(2,1)S(1)}, u32[]{:S(2)}, u32[]{:S(2)}) collective-permute-start(bf16[128,512]{1,0:T(8,128)(2,1)S(1)} %join.15.rest_2_), channel_id=1, source_target_pairs={{0,4},{1,5},{4,8},{5,9},{8,12},{9,13},{12,0},{13,1},{2,6},{3,7},{6... | collective-permute-start | bytes 393224 | tf_op jit(solution)/shard_map/ppermute | solution.py:862
  34.9 1.5 %collective-permute-start.10 = (bf16[128,512]{1,0:T(8,128)(2,1)S(1)}, bf16[128,512]{1,0:T(8,128)(2,1)S(1)}, u32[]{:S(2)}, u32[]{:S(2)}) collective-permute-start(bf16[128,512]{1,0:T(8,128)(2,1)S(1)} %join.16.token_ref), channel_id=1, source_target_pairs={{0,1},{1,0},{4,8},{5,9},{8,12},{9,13},{12,4},{13,5},{2,3},{3,2},{6... | collective-permute-start | bytes 393224 | tf_op jit(solution)/shard_map/ppermute | solution.py:862
  36.4 1.7 %collective-permute-done.7.recv_ref = bf16[128,512]{1,0:T(8,128)(2,1)S(1)} collective-permute-done((bf16[128,512]{1,0:T(8,128)(2,1)S(1)}, bf16[128,512]{1,0:T(8,128)(2,1)S(1)}, u32[]{:S(2)}, u32[]{:S(2)}) %collective-permute-start.7) | collective-permute-done | bytes 131104 | tf_op jit(solution)/shard_map/ppermute | solution.py:862
  38.2 1.1 %out.20 = (bf16[512,4096]{1,0:T(8,128)(2,1)}, bf16[512,512]{1,0:T(8,128)(2,1)S(1)}) custom-call(f32[8,2,512]{2,1,0:T(2,128)S(1)} %get-tuple-element.60.fade_ref, bf16[8,512,512]{2,1,0:T(8,128)(2,1)S(1)} %get-tuple-element.79.mx_ref, bf16[2,512,128]{2,1,0:T(8,128)(2,1)S(1)} %get-tuple-element.83.c_ref, ...), custom_call_target="tpu_custom_call", output_to_operand_aliasing={{0}: (8, {})} | custom-call | flops 268435456 | bytes 1572864 | tf_op jit(solution)/shard_map/out/pallas_call | solution.py:953
  39.3 1.1 %out.21 = (bf16[512,4096]{1,0:T(8,128)(2,1)}, bf16[512,512]{1,0:T(8,128)(2,1)S(1)}) custom-call(f32[8,2,512]{2,1,0:T(2,128)S(1)} %get-tuple-element.60.fade_ref, bf16[8,512,512]{2,1,0:T(8,128)(2,1)S(1)} %get-tuple-element.79.mx_ref, bf16[2,512,128]{2,1,0:T(8,128)(2,1)S(1)} %get-tuple-element.83.c_ref, ...), custom_call_target="tpu_custom_call", output_to_operand_aliasing={{0}: (8, {})} | custom-call | flops 268435456 | bytes 1572864 | tf_op jit(solution)/shard_map/out/pallas_call | solution.py:953
  40.4 1.1 %out.22 = (bf16[512,4096]{1,0:T(8,128)(2,1)}, bf16[512,512]{1,0:T(8,128)(2,1)S(1)}) custom-call(f32[8,2,512]{2,1,0:T(2,128)S(1)} %get-tuple-element.60.fade_ref, bf16[8,512,512]{2,1,0:T(8,128)(2,1)S(1)} %get-tuple-element.79.mx_ref, bf16[2,512,128]{2,1,0:T(8,128)(2,1)S(1)} %get-tuple-element.83.c_ref, ...), custom_call_target="tpu_custom_call", output_to_operand_aliasing={{0}: (8, {})} | custom-call | flops 268435456 | bytes 1572864 | tf_op jit(solution)/shard_map/out/pallas_call | solution.py:953
  41.5 2.1 %collective-permute-start.12 = (bf16[128,512]{1,0:T(8,128)(2,1)S(1)}, bf16[128,512]{1,0:T(8,128)(2,1)S(1)}, u32[]{:S(2)}, u32[]{:S(2)}) collective-permute-start(bf16[128,512]{1,0:T(8,128)(2,1)S(1)} %join.18.rest_2_), channel_id=1, source_target_pairs={{0,1},{1,0},{4,5},{5,4},{8,12},{9,13},{12,8},{13,9},{2,3},{3,2},{6... | collective-permute-start | bytes 393224 | tf_op jit(solution)/shard_map/ppermute | solution.py:862
  43.6 1.8 %out.23 = (bf16[512,4096]{1,0:T(8,128)(2,1)}, bf16[512,512]{1,0:T(8,128)(2,1)S(1)}) custom-call(f32[8,2,512]{2,1,0:T(2,128)S(1)} %get-tuple-element.60.fade_ref, bf16[8,512,512]{2,1,0:T(8,128)(2,1)S(1)} %get-tuple-element.79.mx_ref, bf16[2,512,128]{2,1,0:T(8,128)(2,1)S(1)} %get-tuple-element.83.c_ref, ...), custom_call_target="tpu_custom_call", output_to_operand_aliasing={{0}: (8, {})} | custom-call | flops 268435456 | bytes 1572864 | tf_op jit(solution)/shard_map/out/pallas_call | solution.py:953
  45.5 1.1 %out.24 = (bf16[512,4096]{1,0:T(8,128)(2,1)}, bf16[512,512]{1,0:T(8,128)(2,1)S(1)}) custom-call(f32[8,2,512]{2,1,0:T(2,128)S(1)} %get-tuple-element.60.fade_ref, bf16[8,512,512]{2,1,0:T(8,128)(2,1)S(1)} %get-tuple-element.79.mx_ref, bf16[2,512,128]{2,1,0:T(8,128)(2,1)S(1)} %get-tuple-element.83.c_ref, ...), custom_call_target="tpu_custom_call", output_to_operand_aliasing={{0}: (8, {})} | custom-call | flops 268435456 | bytes 1572864 | tf_op jit(solution)/shard_map/out/pallas_call | solution.py:953
  46.6 1.8 %out.25 = (bf16[512,4096]{1,0:T(8,128)(2,1)}, bf16[512,512]{1,0:T(8,128)(2,1)S(1)}) custom-call(f32[8,2,512]{2,1,0:T(2,128)S(1)} %get-tuple-element.60.fade_ref, bf16[8,512,512]{2,1,0:T(8,128)(2,1)S(1)} %get-tuple-element.79.mx_ref, bf16[2,512,128]{2,1,0:T(8,128)(2,1)S(1)} %get-tuple-element.83.c_ref, ...), custom_call_target="tpu_custom_call", output_to_operand_aliasing={{0}: (8, {})} | custom-call | flops 268435456 | bytes 1572864 | tf_op jit(solution)/shard_map/out/pallas_call | solution.py:953
  48.4 1.1 %out.26 = (bf16[512,4096]{1,0:T(8,128)(2,1)}, bf16[512,512]{1,0:T(8,128)(2,1)S(1)}) custom-call(f32[8,2,512]{2,1,0:T(2,128)S(1)} %get-tuple-element.60.fade_ref, bf16[8,512,512]{2,1,0:T(8,128)(2,1)S(1)} %get-tuple-element.79.mx_ref, bf16[2,512,128]{2,1,0:T(8,128)(2,1)S(1)} %get-tuple-element.83.c_ref, ...), custom_call_target="tpu_custom_call", output_to_operand_aliasing={{0}: (8, {})} | custom-call | flops 268435456 | bytes 1572864 | tf_op jit(solution)/shard_map/out/pallas_call | solution.py:953
  49.5 1.0 %collective-permute-done.11.recv_ref = bf16[128,512]{1,0:T(8,128)(2,1)S(1)} collective-permute-done((bf16[128,512]{1,0:T(8,128)(2,1)S(1)}, bf16[128,512]{1,0:T(8,128)(2,1)S(1)}, u32[]{:S(2)}, u32[]{:S(2)}) %collective-permute-start.11) | collective-permute-done | bytes 131104 | tf_op jit(solution)/shard_map/ppermute | solution.py:862
  50.5 2.5 %out.27 = (bf16[512,4096]{1,0:T(8,128)(2,1)}, bf16[512,512]{1,0:T(8,128)(2,1)}) custom-call(f32[8,2,512]{2,1,0:T(2,128)S(1)} %get-tuple-element.60.fade_ref, bf16[8,512,512]{2,1,0:T(8,128)(2,1)S(1)} %get-tuple-element.79.mx_ref, bf16[2,512,128]{2,1,0:T(8,128)(2,1)S(1)} %get-tuple-element.83.c_ref, ...), custom_call_target="tpu_custom_call", output_to_operand_aliasing={{0}: (8, {})} | custom-call | flops 268435456 | bytes 1572864 | tf_op jit(solution)/shard_map/out/pallas_call | solution.py:953
  (45 shorter events, 7.9 us)
Async XLA Ops:
  0.0 6.6 %copy-start = (f32[4,4096]{1,0:T(4,128)S(1)}, f32[4,4096]{1,0:T(4,128)}, u32[]{:S(2)}) copy-start(f32[4,4096]{1,0:T(4,128)} %wx_ref.15) | copy-start | bytes 196612
  0.0 6.6 %copy-start.1 = (f32[4096]{0:T(1024)S(1)}, f32[4096]{0:T(1024)}, u32[]{:S(2)}) copy-start(f32[4096]{0:T(1024)} %param.18) | copy-start | bytes 49156
  1.6 5.0 %collective-permute-start = (bf16[8,4608]{1,0:T(8,128)(2,1)S(1)}, bf16[8,4608]{1,0:T(8,128)(2,1)S(1)}, u32[]{:S(2)}, u32[]{:S(2)}) collective-permute-start(bf16[8,4608]{1,0:T(8,128)(2,1)S(1)} %pad_maximum_fusion), channel_id=1, source_target_pairs={{0,4},{4,8},{8,12},{12,0},{1,5},{5,9},{9,13},{13,1},{2,6},{6,10},{... | collective-permute-start | bytes 221192 | tf_op jit(solution)/shard_map/ppermute | solution.py:869
  8.6 2.5 %collective-permute-start.2 = (bf16[128,512]{1,0:T(8,128)(2,1)S(1)}, bf16[128,512]{1,0:T(8,128)(2,1)S(1)}, u32[]{:S(2)}, u32[]{:S(2)}) collective-permute-start(bf16[128,512]{1,0:T(8,128)(2,1)S(1)} %get-tuple-element.82.recv_ref), channel_id=1, source_target_pairs={{0,4},{1,5},{4,0},{5,1},{8,9},{9,8},{12,13},{13,12},{2,6},{3,7},{6... | collective-permute-start | bytes 393224 | tf_op jit(solution)/shard_map/ppermute | solution.py:862
  9.6 2.6 %collective-permute-start.1 = (bf16[128,512]{1,0:T(8,128)(2,1)S(1)}, bf16[128,512]{1,0:T(8,128)(2,1)S(1)}, u32[]{:S(2)}, u32[]{:S(2)}) collective-permute-start(bf16[128,512]{1,0:T(8,128)(2,1)S(1)} %get-tuple-element.81.recv_ref), channel_id=1, source_target_pairs={{0,4},{1,5},{4,0},{5,1},{8,9},{9,8},{12,13},{13,12},{2,6},{3,7},{6... | collective-permute-start | bytes 393224 | tf_op jit(solution)/shard_map/ppermute | solution.py:862
  11.2 4.4 %collective-permute-start.4 = (bf16[128,512]{1,0:T(8,128)(2,1)S(1)}, bf16[128,512]{1,0:T(8,128)(2,1)S(1)}, u32[]{:S(2)}, u32[]{:S(2)}) collective-permute-start(bf16[128,512]{1,0:T(8,128)(2,1)S(1)} %join.10.token_ref), channel_id=1, source_target_pairs={{0,4},{1,5},{4,8},{5,9},{8,0},{9,1},{12,13},{13,12},{2,6},{3,7},{6... | collective-permute-start | bytes 393224 | tf_op jit(solution)/shard_map/ppermute | solution.py:862
  12.3 12.9 %collective-permute-start.3 = (bf16[128,512]{1,0:T(8,128)(2,1)S(1)}, bf16[128,512]{1,0:T(8,128)(2,1)S(1)}, u32[]{:S(2)}, u32[]{:S(2)}) collective-permute-start(bf16[128,512]{1,0:T(8,128)(2,1)S(1)} %join.11.after_ref), channel_id=1, source_target_pairs={{0,4},{1,5},{4,8},{5,9},{8,0},{9,1},{12,13},{13,12},{2,6},{3,7},{6... | collective-permute-start | bytes 393224 | tf_op jit(solution)/shard_map/ppermute | solution.py:862
  15.6 11.8 %collective-permute-start.6 = (bf16[128,512]{1,0:T(8,128)(2,1)S(1)}, bf16[128,512]{1,0:T(8,128)(2,1)S(1)}, u32[]{:S(2)}, u32[]{:S(2)}) collective-permute-start(bf16[128,512]{1,0:T(8,128)(2,1)S(1)} %join.12.token_ref), channel_id=1, source_target_pairs={{0,4},{1,5},{4,8},{5,9},{8,12},{9,13},{12,0},{13,1},{2,6},{3,7},{6... | collective-permute-start | bytes 393224 | tf_op jit(solution)/shard_map/ppermute | solution.py:862
  25.2 6.8 %collective-permute-start.5 = (bf16[128,512]{1,0:T(8,128)(2,1)S(1)}, bf16[128,512]{1,0:T(8,128)(2,1)S(1)}, u32[]{:S(2)}, u32[]{:S(2)}) collective-permute-start(bf16[128,512]{1,0:T(8,128)(2,1)S(1)} %join.13), channel_id=1, source_target_pairs={{0,4},{1,5},{4,8},{5,9},{8,12},{9,13},{12,0},{13,1},{2,6},{3,7},{6... | collective-permute-start | bytes 393224 | tf_op jit(solution)/shard_map/ppermute | solution.py:862
  27.5 7.3 %collective-permute-start.8 = (bf16[128,512]{1,0:T(8,128)(2,1)S(1)}, bf16[128,512]{1,0:T(8,128)(2,1)S(1)}, u32[]{:S(2)}, u32[]{:S(2)}) collective-permute-start(bf16[128,512]{1,0:T(8,128)(2,1)S(1)} %join.14.token_ref), channel_id=1, source_target_pairs={{0,4},{1,5},{4,8},{5,9},{8,12},{9,13},{12,0},{13,1},{2,6},{3,7},{6... | collective-permute-start | bytes 393224 | tf_op jit(solution)/shard_map/ppermute | solution.py:862
  32.1 6.0 %collective-permute-start.7 = (bf16[128,512]{1,0:T(8,128)(2,1)S(1)}, bf16[128,512]{1,0:T(8,128)(2,1)S(1)}, u32[]{:S(2)}, u32[]{:S(2)}) collective-permute-start(bf16[128,512]{1,0:T(8,128)(2,1)S(1)} %join.15.rest_2_), channel_id=1, source_target_pairs={{0,4},{1,5},{4,8},{5,9},{8,12},{9,13},{12,0},{13,1},{2,6},{3,7},{6... | collective-permute-start | bytes 393224 | tf_op jit(solution)/shard_map/ppermute | solution.py:862
  34.9 6.6 %collective-permute-start.10 = (bf16[128,512]{1,0:T(8,128)(2,1)S(1)}, bf16[128,512]{1,0:T(8,128)(2,1)S(1)}, u32[]{:S(2)}, u32[]{:S(2)}) collective-permute-start(bf16[128,512]{1,0:T(8,128)(2,1)S(1)} %join.16.token_ref), channel_id=1, source_target_pairs={{0,1},{1,0},{4,8},{5,9},{8,12},{9,13},{12,4},{13,5},{2,3},{3,2},{6... | collective-permute-start | bytes 393224 | tf_op jit(solution)/shard_map/ppermute | solution.py:862
  38.1 7.3 %collective-permute-start.9 = (bf16[128,512]{1,0:T(8,128)(2,1)S(1)}, bf16[128,512]{1,0:T(8,128)(2,1)S(1)}, u32[]{:S(2)}, u32[]{:S(2)}) collective-permute-start(bf16[128,512]{1,0:T(8,128)(2,1)S(1)} %join.17.rest_2_), channel_id=1, source_target_pairs={{0,1},{1,0},{4,8},{5,9},{8,12},{9,13},{12,4},{13,5},{2,3},{3,2},{6... | collective-permute-start | bytes 393224 | tf_op jit(solution)/shard_map/ppermute | solution.py:862
  41.5 6.9 %collective-permute-start.12 = (bf16[128,512]{1,0:T(8,128)(2,1)S(1)}, bf16[128,512]{1,0:T(8,128)(2,1)S(1)}, u32[]{:S(2)}, u32[]{:S(2)}) collective-permute-start(bf16[128,512]{1,0:T(8,128)(2,1)S(1)} %join.18.rest_2_), channel_id=1, source_target_pairs={{0,1},{1,0},{4,5},{5,4},{8,12},{9,13},{12,8},{13,9},{2,3},{3,2},{6... | collective-permute-start | bytes 393224 | tf_op jit(solution)/shard_map/ppermute | solution.py:862
  45.4 5.0 %collective-permute-start.11 = (bf16[128,512]{1,0:T(8,128)(2,1)S(1)}, bf16[128,512]{1,0:T(8,128)(2,1)S(1)}, u32[]{:S(2)}, u32[]{:S(2)}) collective-permute-start(bf16[128,512]{1,0:T(8,128)(2,1)S(1)} %join.19.rest_2_), channel_id=1, source_target_pairs={{0,1},{1,0},{4,5},{5,4},{8,12},{9,13},{12,8},{13,9},{2,3},{3,2},{6... | collective-permute-start | bytes 393224 | tf_op jit(solution)/shard_map/ppermute | solution.py:862

commit v8 on v7

--- a/solution.py
+++ b/solution.py
@@ -31,6 +31,31 @@
 
 def silu_half(u):
     return u + u * jnp.tanh(u)
+
+
+def doc_at(pos, starts_ref):
+    count = jnp.int32(-1)
+    for j in range(starts_ref.shape[0]):
+        count = count + (pos >= starts_ref[j]).astype(jnp.int32)
+    return count
+
+
+def column_of(ref):
+    heads = ref.shape[0]
+    index = lax.broadcasted_iota(jnp.int32, (heads, 1), 0)
+    column = jnp.zeros((heads, 1), F32)
+    for h in range(heads):
+        column = jnp.where(index == h, ref[h], column)
+    return column
+
+
+def split(value, parts):
+    pieces = []
+    for _ in range(parts - 1):
+        piece = value.astype(BF16).astype(F32)
+        pieces.append(piece)
+        value = value - piece
+    return pieces + [value]
 
 
 def doc_at(pos, starts_ref):
@@ -992,9 +1017,6 @@
             elif s == 0:
                 ready = waiting + ready
                 waiting = []
-            if turn == slots - 1 and turn > per_stream and s == 0:
-                before, token, out = flush(ready, before, token, out)
-                ready = []
             ready.append((turn, s, got))
             if (turn > per_stream and turn != slots - 1) or turn == slots:
                 before, token, out = flush(ready, before, token, out)

time: 53.5 us -> 53.2 us (level)
  the two profiles are of different devices: /device:TPU:24 before, /device:TPU:28 now
where the time goes in v8:
time: 53.2 us; the launch traced here: 52.8 us
  Pallas kernels  26.5 us (50%)
  starting transfers between devices  19.1 us (36%)
  waiting for transfers between devices  3.88 us (7%)
  local copies, waits for them, and re-layouts  2.72 us (5%)
    ppermute x12, starting transfers between devices, hop(): return lax.ppermute(send, ('seq', 'sub'), pairs)  18.8 us
    pallas_call x14, Pallas kernels, output(): pl.pallas_call(functools.partial(out_kernel, turn=turn, stream=s, before=...  11.9 us
    pallas_call x7, Pallas kernels, more(): pl.pallas_call(functools.partial(more_kernel, heads=heads, per_group=per_...  6.63 us
    ppermute x12, waiting for transfers between devices, hop(): return lax.ppermute(send, ('seq', 'sub'), pairs)  3.88 us
    pallas_call x1, Pallas kernels, per_device(): pl.pallas_call(params_kernel, in_specs=[SMEM] * 4 + [VMEM, ANY], out_spec...  3.75 us
    pallas_call x1, Pallas kernels, per_device(): pl.pallas_call(functools.partial(first_kernel, heads=heads), in_specs=[VM...  1.97 us
    unnamed x7, local copies, waits for them, and re-layouts  1.87 us
    pallas_call x1, Pallas kernels, scores(): pl.pallas_call(score_kernel, in_specs=[VMEM] * 7 + [ANY], out_specs=[VMEM...  1.8 us
  transfers between devices with their start and end apart: 13, of which 4 were waited for; matrix products, arithmetic and copies ran while one was open for 2% of the time, Pallas kernels for 42%

profile of v8, /device:TPU:28, one launch (start us, length us, event | category | flops | bytes accessed | tf_op | source)
XLA Modules:
  0.0 52.8 jit_solution(17168553624677000069)
XLA Ops:
  1.9 1.1 %copy.40 = bf16[64,8,2,256]{3,1,2,0:T(8,128)(2,1)S(1)} copy(bf16[64,8,2,256]{3,2,1,0:T(2,128)(2,1)} %bitcast.16) | data formatting | bytes 1048576
  3.0 3.8 %params.1 = (bf16[512,128]{1,0:T(8,128)(2,1)S(1)}, f32[512,128]{1,0:T(8,128)S(1)}, f32[8,4,512]{2,1,0:T(4,128)S(1)}, f32[8,2,512]{2,1,0:T(2,128)S(1)}, bf16[4,38...) custom-call(s32[4]{0:T(128)} %starts_ref.1, f32[32]{0:T(128)} %bias_ref.1, ...), custom_call_target="tpu_custom_call" | custom-call | tf_op jit(solution)/shard_map/params/pallas_call | solution.py:897
  6.8 2.0 %first.1 = (bf16[8,512,512]{2,1,0:T(8,128)(2,1)S(1)}, f32[8,128,512]{2,1,0:T(8,128)S(1)}, bf16[128,512]{1,0:T(8,128)(2,1)S(1)}, bf16[2,128,512]{2,1,0:T(8,128)(2,1)S(1)}) custom-call(bf16[512,4096]{1,0:T(8,128)(2,1)S(1)} %get-tuple-element.61.x_ref, bf16[8,4608]{1,0:T(8,128)(2,1)S(1)} %collective-permute-done.rim_ref, f32[4,4096]{1,0:T(4,128)S(1)} %copy-done, ...), custom_call_target="tpu_custom_call" | custom-call | tf_op jit(solution)/shard_map/first/pallas_call | solution.py:920
  8.9 1.0 %more.7 = (bf16[8,512,512]{2,1,0:T(8,128)(2,1)S(1)}, f32[8,128,512]{2,1,0:T(8,128)S(1)}, bf16[128,512]{1,0:T(8,128)(2,1)S(1)}) custom-call(bf16[512,4096]{1,0:T(8,128)(2,1)S(1)} %get-tuple-element.61.x_ref, bf16[8,4608]{1,0:T(8,128)(2,1)S(1)} %collective-permute-done.rim_ref, f32[4,4096]{1,0:T(4,128)S(1)} %copy-done, ...), custom_call_target="tpu_custom_call", output_to_operand_aliasing={{0}: (7, {}), {1}: (8, {})} | custom-call | flops 134217728 | bytes 1048576 | tf_op jit(solution)/shard_map/more/pallas_call | solution.py:934
  10.4 0.9 %more.8 = (bf16[8,512,512]{2,1,0:T(8,128)(2,1)S(1)}, f32[8,128,512]{2,1,0:T(8,128)S(1)}) custom-call(bf16[512,4096]{1,0:T(8,128)(2,1)S(1)} %get-tuple-element.61.x_ref, bf16[8,4608]{1,0:T(8,128)(2,1)S(1)} %collective-permute-done.rim_ref, f32[4,4096]{1,0:T(4,128)S(1)} %copy-done, ...), custom_call_target="tpu_custom_call", output_to_operand_aliasing={{0}: (7, {}), {1}: (8, {})} | custom-call | flops 134217728 | bytes 1048576 | tf_op jit(solution)/shard_map/more/pallas_call | solution.py:934
  11.5 0.9 %more.9 = (bf16[8,512,512]{2,1,0:T(8,128)(2,1)S(1)}, f32[8,128,512]{2,1,0:T(8,128)S(1)}) custom-call(bf16[512,4096]{1,0:T(8,128)(2,1)S(1)} %get-tuple-element.61.x_ref, bf16[8,4608]{1,0:T(8,128)(2,1)S(1)} %collective-permute-done.rim_ref, f32[4,4096]{1,0:T(4,128)S(1)} %copy-done, ...), custom_call_target="tpu_custom_call", output_to_operand_aliasing={{0}: (7, {}), {1}: (8, {})} | custom-call | flops 134217728 | bytes 1048576 | tf_op jit(solution)/shard_map/more/pallas_call | solution.py:934
  13.0 1.8 %score.1 = (bf16[2,512,128]{2,1,0:T(8,128)(2,1)S(1)}, f32[2,512,512]{2,1,0:T(8,128)S(1)}) custom-call(bf16[8,4608]{1,0:T(8,128)(2,1)S(1)} %collective-permute-done.rim_ref, bf16[4,384,256]{2,1,0:T(8,128)(2,1)S(1)} %get-tuple-element.62.shift_ref, f32[512,512]{1,0:T(8,128)S(1)} %get-tuple-element.80.keep_ref, bf16[512,512]{1,0:T(8,128)(2,1)S(1)} %bitcast.7, ...), custom_call_target="tpu_custom_call" | custom-call | tf_op jit(solution)/shard_map/score/pallas_call | solution.py:956
  14.8 0.9 %more.10 = (bf16[8,512,512]{2,1,0:T(8,128)(2,1)S(1)}, f32[8,128,512]{2,1,0:T(8,128)S(1)}) custom-call(bf16[512,4096]{1,0:T(8,128)(2,1)S(1)} %get-tuple-element.61.x_ref, bf16[8,4608]{1,0:T(8,128)(2,1)S(1)} %collective-permute-done.rim_ref, f32[4,4096]{1,0:T(4,128)S(1)} %copy-done, ...), custom_call_target="tpu_custom_call", output_to_operand_aliasing={{0}: (7, {}), {1}: (8, {})} | custom-call | flops 134217728 | bytes 1048576 | tf_op jit(solution)/shard_map/more/pallas_call | solution.py:934
  15.9 8.4 %collective-permute-start.6 = (bf16[128,512]{1,0:T(8,128)(2,1)S(1)}, bf16[128,512]{1,0:T(8,128)(2,1)S(1)}, u32[]{:S(2)}, u32[]{:S(2)}) collective-permute-start(bf16[128,512]{1,0:T(8,128)(2,1)S(1)} %join.12.token_ref), channel_id=1, source_target_pairs={{0,4},{1,5},{4,8},{5,9},{8,12},{9,13},{12,0},{13,1},{2,6},{3,7},{6... | collective-permute-start | bytes 393224 | tf_op jit(solution)/shard_map/ppermute | solution.py:887
  24.2 0.9 %more.11 = (bf16[8,512,512]{2,1,0:T(8,128)(2,1)S(1)}, f32[8,128,512]{2,1,0:T(8,128)S(1)}) custom-call(bf16[512,4096]{1,0:T(8,128)(2,1)S(1)} %get-tuple-element.61.x_ref, bf16[8,4608]{1,0:T(8,128)(2,1)S(1)} %collective-permute-done.rim_ref, f32[4,4096]{1,0:T(4,128)S(1)} %copy-done, ...), custom_call_target="tpu_custom_call", output_to_operand_aliasing={{0}: (7, {}), {1}: (8, {})} | custom-call | flops 134217728 | bytes 1048576 | tf_op jit(solution)/shard_map/more/pallas_call | solution.py:934
  27.5 3.5 %collective-permute-start.8 = (bf16[128,512]{1,0:T(8,128)(2,1)S(1)}, bf16[128,512]{1,0:T(8,128)(2,1)S(1)}, u32[]{:S(2)}, u32[]{:S(2)}) collective-permute-start(bf16[128,512]{1,0:T(8,128)(2,1)S(1)} %join.14.token_ref), channel_id=1, source_target_pairs={{0,4},{1,5},{4,8},{5,9},{8,12},{9,13},{12,0},{13,1},{2,6},{3,7},{6... | collective-permute-start | bytes 393224 | tf_op jit(solution)/shard_map/ppermute | solution.py:887
  31.1 1.0 %more.13 = (bf16[8,512,512]{2,1,0:T(8,128)(2,1)S(1)}, f32[8,128,512]{2,1,0:T(8,128)S(1)}) custom-call(bf16[512,4096]{1,0:T(8,128)(2,1)S(1)} %get-tuple-element.61.x_ref, bf16[8,4608]{1,0:T(8,128)(2,1)S(1)} %collective-permute-done.rim_ref, f32[4,4096]{1,0:T(4,128)S(1)} %copy-done, ...), custom_call_target="tpu_custom_call", output_to_operand_aliasing={{0}: (7, {}), {1}: (8, {})} | custom-call | flops 134217728 | bytes 1048576 | tf_op jit(solution)/shard_map/more/pallas_call | solution.py:934
  32.1 1.6 %collective-permute-start.7 = (bf16[128,512]{1,0:T(8,128)(2,1)S(1)}, bf16[128,512]{1,0:T(8,128)(2,1)S(1)}, u32[]{:S(2)}, u32[]{:S(2)}) collective-permute-start(bf16[128,512]{1,0:T(8,128)(2,1)S(1)} %join.15.rest_2_), channel_id=1, source_target_pairs={{0,4},{1,5},{4,8},{5,9},{8,12},{9,13},{12,0},{13,1},{2,6},{3,7},{6... | collective-permute-start | bytes 393224 | tf_op jit(solution)/shard_map/ppermute | solution.py:887
  34.9 1.5 %collective-permute-start.10 = (bf16[128,512]{1,0:T(8,128)(2,1)S(1)}, bf16[128,512]{1,0:T(8,128)(2,1)S(1)}, u32[]{:S(2)}, u32[]{:S(2)}) collective-permute-start(bf16[128,512]{1,0:T(8,128)(2,1)S(1)} %join.16.token_ref), channel_id=1, source_target_pairs={{0,1},{1,0},{4,8},{5,9},{8,12},{9,13},{12,4},{13,5},{2,3},{3,2},{6... | collective-permute-start | bytes 393224 | tf_op jit(solution)/shard_map/ppermute | solution.py:887
  36.4 1.6 %collective-permute-done.7.recv_ref = bf16[128,512]{1,0:T(8,128)(2,1)S(1)} collective-permute-done((bf16[128,512]{1,0:T(8,128)(2,1)S(1)}, bf16[128,512]{1,0:T(8,128)(2,1)S(1)}, u32[]{:S(2)}, u32[]{:S(2)}) %collective-permute-start.7) | collective-permute-done | bytes 131104 | tf_op jit(solution)/shard_map/ppermute | solution.py:887
  38.2 1.1 %out.20 = (bf16[512,4096]{1,0:T(8,128)(2,1)}, bf16[512,512]{1,0:T(8,128)(2,1)S(1)}) custom-call(f32[8,2,512]{2,1,0:T(2,128)S(1)} %get-tuple-element.60.fade_ref, bf16[8,512,512]{2,1,0:T(8,128)(2,1)S(1)} %get-tuple-element.79.mx_ref, bf16[2,512,128]{2,1,0:T(8,128)(2,1)S(1)} %get-tuple-element.83.c_ref, ...), custom_call_target="tpu_custom_call", output_to_operand_aliasing={{0}: (8, {})} | custom-call | flops 268435456 | bytes 1572864 | tf_op jit(solution)/shard_map/out/pallas_call | solution.py:978
  39.3 1.1 %out.21 = (bf16[512,4096]{1,0:T(8,128)(2,1)}, bf16[512,512]{1,0:T(8,128)(2,1)S(1)}) custom-call(f32[8,2,512]{2,1,0:T(2,128)S(1)} %get-tuple-element.60.fade_ref, bf16[8,512,512]{2,1,0:T(8,128)(2,1)S(1)} %get-tuple-element.79.mx_ref, bf16[2,512,128]{2,1,0:T(8,128)(2,1)S(1)} %get-tuple-element.83.c_ref, ...), custom_call_target="tpu_custom_call", output_to_operand_aliasing={{0}: (8, {})} | custom-call | flops 268435456 | bytes 1572864 | tf_op jit(solution)/shard_map/out/pallas_call | solution.py:978
  40.4 1.1 %out.22 = (bf16[512,4096]{1,0:T(8,128)(2,1)}, bf16[512,512]{1,0:T(8,128)(2,1)S(1)}) custom-call(f32[8,2,512]{2,1,0:T(2,128)S(1)} %get-tuple-element.60.fade_ref, bf16[8,512,512]{2,1,0:T(8,128)(2,1)S(1)} %get-tuple-element.79.mx_ref, bf16[2,512,128]{2,1,0:T(8,128)(2,1)S(1)} %get-tuple-element.83.c_ref, ...), custom_call_target="tpu_custom_call", output_to_operand_aliasing={{0}: (8, {})} | custom-call | flops 268435456 | bytes 1572864 | tf_op jit(solution)/shard_map/out/pallas_call | solution.py:978
  41.5 2.1 %collective-permute-start.12 = (bf16[128,512]{1,0:T(8,128)(2,1)S(1)}, bf16[128,512]{1,0:T(8,128)(2,1)S(1)}, u32[]{:S(2)}, u32[]{:S(2)}) collective-permute-start(bf16[128,512]{1,0:T(8,128)(2,1)S(1)} %join.18.token_ref), channel_id=1, source_target_pairs={{0,1},{1,0},{4,5},{5,4},{8,12},{9,13},{12,8},{13,9},{2,3},{3,2},{6... | collective-permute-start | bytes 393224 | tf_op jit(solution)/shard_map/ppermute | solution.py:887
  44.3 1.8 %out.23 = (bf16[512,4096]{1,0:T(8,128)(2,1)}, bf16[512,512]{1,0:T(8,128)(2,1)S(1)}) custom-call(f32[8,2,512]{2,1,0:T(2,128)S(1)} %get-tuple-element.60.fade_ref, bf16[8,512,512]{2,1,0:T(8,128)(2,1)S(1)} %get-tuple-element.79.mx_ref, bf16[2,512,128]{2,1,0:T(8,128)(2,1)S(1)} %get-tuple-element.83.c_ref, ...), custom_call_target="tpu_custom_call", output_to_operand_aliasing={{0}: (8, {})} | custom-call | flops 268435456 | bytes 1572864 | tf_op jit(solution)/shard_map/out/pallas_call | solution.py:978
  46.1 1.1 %out.24 = (bf16[512,4096]{1,0:T(8,128)(2,1)}, bf16[512,512]{1,0:T(8,128)(2,1)S(1)}) custom-call(f32[8,2,512]{2,1,0:T(2,128)S(1)} %get-tuple-element.60.fade_ref, bf16[8,512,512]{2,1,0:T(8,128)(2,1)S(1)} %get-tuple-element.79.mx_ref, bf16[2,512,128]{2,1,0:T(8,128)(2,1)S(1)} %get-tuple-element.83.c_ref, ...), custom_call_target="tpu_custom_call", output_to_operand_aliasing={{0}: (8, {})} | custom-call | flops 268435456 | bytes 1572864 | tf_op jit(solution)/shard_map/out/pallas_call | solution.py:978
  47.2 1.8 %out.25 = (bf16[512,4096]{1,0:T(8,128)(2,1)}, bf16[512,512]{1,0:T(8,128)(2,1)S(1)}) custom-call(f32[8,2,512]{2,1,0:T(2,128)S(1)} %get-tuple-element.60.fade_ref, bf16[8,512,512]{2,1,0:T(8,128)(2,1)S(1)} %get-tuple-element.79.mx_ref, bf16[2,512,128]{2,1,0:T(8,128)(2,1)S(1)} %get-tuple-element.83.c_ref, ...), custom_call_target="tpu_custom_call", output_to_operand_aliasing={{0}: (8, {})} | custom-call | flops 268435456 | bytes 1572864 | tf_op jit(solution)/shard_map/out/pallas_call | solution.py:978
  49.0 1.1 %out.26 = (bf16[512,4096]{1,0:T(8,128)(2,1)}, bf16[512,512]{1,0:T(8,128)(2,1)S(1)}) custom-call(f32[8,2,512]{2,1,0:T(2,128)S(1)} %get-tuple-element.60.fade_ref, bf16[8,512,512]{2,1,0:T(8,128)(2,1)S(1)} %get-tuple-element.79.mx_ref, bf16[2,512,128]{2,1,0:T(8,128)(2,1)S(1)} %get-tuple-element.83.c_ref, ...), custom_call_target="tpu_custom_call", output_to_operand_aliasing={{0}: (8, {})} | custom-call | flops 268435456 | bytes 1572864 | tf_op jit(solution)/shard_map/out/pallas_call | solution.py:978
  50.1 2.5 %out.27 = (bf16[512,4096]{1,0:T(8,128)(2,1)}, bf16[512,512]{1,0:T(8,128)(2,1)}) custom-call(f32[8,2,512]{2,1,0:T(2,128)S(1)} %get-tuple-element.60.fade_ref, bf16[8,512,512]{2,1,0:T(8,128)(2,1)S(1)} %get-tuple-element.79.mx_ref, bf16[2,512,128]{2,1,0:T(8,128)(2,1)S(1)} %get-tuple-element.83.c_ref, ...), custom_call_target="tpu_custom_call", output_to_operand_aliasing={{0}: (8, {})} | custom-call | flops 268435456 | bytes 1572864 | tf_op jit(solution)/shard_map/out/pallas_call | solution.py:978
  (45 shorter events, 7.7 us)
Async XLA Ops:
  0.0 6.8 %copy-start = (f32[4,4096]{1,0:T(4,128)S(1)}, f32[4,4096]{1,0:T(4,128)}, u32[]{:S(2)}) copy-start(f32[4,4096]{1,0:T(4,128)} %wx_ref.15) | copy-start | bytes 196612
  0.0 6.8 %copy-start.1 = (f32[4096]{0:T(1024)S(1)}, f32[4096]{0:T(1024)}, u32[]{:S(2)}) copy-start(f32[4096]{0:T(1024)} %param.18) | copy-start | bytes 49156
  1.6 5.2 %collective-permute-start = (bf16[8,4608]{1,0:T(8,128)(2,1)S(1)}, bf16[8,4608]{1,0:T(8,128)(2,1)S(1)}, u32[]{:S(2)}, u32[]{:S(2)}) collective-permute-start(bf16[8,4608]{1,0:T(8,128)(2,1)S(1)} %pad_maximum_fusion), channel_id=1, source_target_pairs={{0,4},{4,8},{8,12},{12,0},{1,5},{5,9},{9,13},{13,1},{2,6},{6,10},{... | collective-permute-start | bytes 221192 | tf_op jit(solution)/shard_map/ppermute | solution.py:894
  8.8 2.6 %collective-permute-start.2 = (bf16[128,512]{1,0:T(8,128)(2,1)S(1)}, bf16[128,512]{1,0:T(8,128)(2,1)S(1)}, u32[]{:S(2)}, u32[]{:S(2)}) collective-permute-start(bf16[128,512]{1,0:T(8,128)(2,1)S(1)} %get-tuple-element.82.recv_ref), channel_id=1, source_target_pairs={{0,4},{1,5},{4,0},{5,1},{8,9},{9,8},{12,13},{13,12},{2,6},{3,7},{6... | collective-permute-start | bytes 393224 | tf_op jit(solution)/shard_map/ppermute | solution.py:887
  9.8 2.6 %collective-permute-start.1 = (bf16[128,512]{1,0:T(8,128)(2,1)S(1)}, bf16[128,512]{1,0:T(8,128)(2,1)S(1)}, u32[]{:S(2)}, u32[]{:S(2)}) collective-permute-start(bf16[128,512]{1,0:T(8,128)(2,1)S(1)} %get-tuple-element.81.recv_ref), channel_id=1, source_target_pairs={{0,4},{1,5},{4,0},{5,1},{8,9},{9,8},{12,13},{13,12},{2,6},{3,7},{6... | collective-permute-start | bytes 393224 | tf_op jit(solution)/shard_map/ppermute | solution.py:887
  11.4 4.4 %collective-permute-start.4 = (bf16[128,512]{1,0:T(8,128)(2,1)S(1)}, bf16[128,512]{1,0:T(8,128)(2,1)S(1)}, u32[]{:S(2)}, u32[]{:S(2)}) collective-permute-start(bf16[128,512]{1,0:T(8,128)(2,1)S(1)} %join.10.token_ref), channel_id=1, source_target_pairs={{0,4},{1,5},{4,8},{5,9},{8,0},{9,1},{12,13},{13,12},{2,6},{3,7},{6... | collective-permute-start | bytes 393224 | tf_op jit(solution)/shard_map/ppermute | solution.py:887
  12.5 12.7 %collective-permute-start.3 = (bf16[128,512]{1,0:T(8,128)(2,1)S(1)}, bf16[128,512]{1,0:T(8,128)(2,1)S(1)}, u32[]{:S(2)}, u32[]{:S(2)}) collective-permute-start(bf16[128,512]{1,0:T(8,128)(2,1)S(1)} %join.11.after_ref), channel_id=1, source_target_pairs={{0,4},{1,5},{4,8},{5,9},{8,0},{9,1},{12,13},{13,12},{2,6},{3,7},{6... | collective-permute-start | bytes 393224 | tf_op jit(solution)/shard_map/ppermute | solution.py:887
  15.9 11.6 %collective-permute-start.6 = (bf16[128,512]{1,0:T(8,128)(2,1)S(1)}, bf16[128,512]{1,0:T(8,128)(2,1)S(1)}, u32[]{:S(2)}, u32[]{:S(2)}) collective-permute-start(bf16[128,512]{1,0:T(8,128)(2,1)S(1)} %join.12.token_ref), channel_id=1, source_target_pairs={{0,4},{1,5},{4,8},{5,9},{8,12},{9,13},{12,0},{13,1},{2,6},{3,7},{6... | collective-permute-start | bytes 393224 | tf_op jit(solution)/shard_map/ppermute | solution.py:887
  25.2 6.8 %collective-permute-start.5 = (bf16[128,512]{1,0:T(8,128)(2,1)S(1)}, bf16[128,512]{1,0:T(8,128)(2,1)S(1)}, u32[]{:S(2)}, u32[]{:S(2)}) collective-permute-start(bf16[128,512]{1,0:T(8,128)(2,1)S(1)} %join.13), channel_id=1, source_target_pairs={{0,4},{1,5},{4,8},{5,9},{8,12},{9,13},{12,0},{13,1},{2,6},{3,7},{6... | collective-permute-start | bytes 393224 | tf_op jit(solution)/shard_map/ppermute | solution.py:887
  27.5 7.3 %collective-permute-start.8 = (bf16[128,512]{1,0:T(8,128)(2,1)S(1)}, bf16[128,512]{1,0:T(8,128)(2,1)S(1)}, u32[]{:S(2)}, u32[]{:S(2)}) collective-permute-start(bf16[128,512]{1,0:T(8,128)(2,1)S(1)} %join.14.token_ref), channel_id=1, source_target_pairs={{0,4},{1,5},{4,8},{5,9},{8,12},{9,13},{12,0},{13,1},{2,6},{3,7},{6... | collective-permute-start | bytes 393224 | tf_op jit(solution)/shard_map/ppermute | solution.py:887
  32.1 6.0 %collective-permute-start.7 = (bf16[128,512]{1,0:T(8,128)(2,1)S(1)}, bf16[128,512]{1,0:T(8,128)(2,1)S(1)}, u32[]{:S(2)}, u32[]{:S(2)}) collective-permute-start(bf16[128,512]{1,0:T(8,128)(2,1)S(1)} %join.15.rest_2_), channel_id=1, source_target_pairs={{0,4},{1,5},{4,8},{5,9},{8,12},{9,13},{12,0},{13,1},{2,6},{3,7},{6... | collective-permute-start | bytes 393224 | tf_op jit(solution)/shard_map/ppermute | solution.py:887
  34.9 6.5 %collective-permute-start.10 = (bf16[128,512]{1,0:T(8,128)(2,1)S(1)}, bf16[128,512]{1,0:T(8,128)(2,1)S(1)}, u32[]{:S(2)}, u32[]{:S(2)}) collective-permute-start(bf16[128,512]{1,0:T(8,128)(2,1)S(1)} %join.16.token_ref), channel_id=1, source_target_pairs={{0,1},{1,0},{4,8},{5,9},{8,12},{9,13},{12,4},{13,5},{2,3},{3,2},{6... | collective-permute-start | bytes 393224 | tf_op jit(solution)/shard_map/ppermute | solution.py:887
  38.1 6.1 %collective-permute-start.9 = (bf16[128,512]{1,0:T(8,128)(2,1)S(1)}, bf16[128,512]{1,0:T(8,128)(2,1)S(1)}, u32[]{:S(2)}, u32[]{:S(2)}) collective-permute-start(bf16[128,512]{1,0:T(8,128)(2,1)S(1)} %join.17.rest_2_), channel_id=1, source_target_pairs={{0,1},{1,0},{4,8},{5,9},{8,12},{9,13},{12,4},{13,5},{2,3},{3,2},{6... | collective-permute-start | bytes 393224 | tf_op jit(solution)/shard_map/ppermute | solution.py:887
  41.5 7.4 %collective-permute-start.12 = (bf16[128,512]{1,0:T(8,128)(2,1)S(1)}, bf16[128,512]{1,0:T(8,128)(2,1)S(1)}, u32[]{:S(2)}, u32[]{:S(2)}) collective-permute-start(bf16[128,512]{1,0:T(8,128)(2,1)S(1)} %join.18.token_ref), channel_id=1, source_target_pairs={{0,1},{1,0},{4,5},{5,4},{8,12},{9,13},{12,8},{13,9},{2,3},{3,2},{6... | collective-permute-start | bytes 393224 | tf_op jit(solution)/shard_map/ppermute | solution.py:887
  44.2 5.9 %collective-permute-start.11 = (bf16[128,512]{1,0:T(8,128)(2,1)S(1)}, bf16[128,512]{1,0:T(8,128)(2,1)S(1)}, u32[]{:S(2)}, u32[]{:S(2)}) collective-permute-start(bf16[128,512]{1,0:T(8,128)(2,1)S(1)} %join.19.rest_2_), channel_id=1, source_target_pairs={{0,1},{1,0},{4,5},{5,4},{8,12},{9,13},{12,8},{13,9},{2,3},{3,2},{6... | collective-permute-start | bytes 393224 | tf_op jit(solution)/shard_map/ppermute | solution.py:887
